TPU v7x, 32 devices: a whole 2x2x4 slice. The times are simulated.
32 devices in a mesh: dp: 2 (over y), tok: 8 (over z, core), col: 2 (over x).
Axes of the slice: x: 2, y: 2, z: 4, core: 2. Of those that a mesh axis runs over, the one named last changes fastest.
Arguments:
- tokens: bfloat16 [2, 4096, 1024], P('dp', 'tok'), may hold values from -6 to 6
- ln_gain: bfloat16 [1024], replicated, may hold values from 0.099609375 to 1.8984375
- qkv_weight: bfloat16 [3, 1024, 512], P(None, None, 'col'), may hold values from -0.375 to 0.375
- out_weight: bfloat16 [512, 1024], P('col'), may hold values from -0.25 to 0.25
- readout_weight: bfloat16 [1024, 64], replicated, may hold values from -0.1875 to 0.1875
- conv_weight: bfloat16 [2, 64, 576], replicated, may hold values from -0.25 to 0.25
- head_weight: bfloat16 [2, 64], replicated, may hold values from -0.75 to 0.75
- holo_cot: float32 [2, 2, 16, 256], P('dp', None, 'tok', 'col'), may hold values from -2.5 to 2.5
Outputs:
- hologram: float32 [2, 2, 16, 256], P('dp', None, 'tok', 'col')
- conv_grad: float32 [2, 64, 576], replicated
- out_grad: float32 [512, 1024], P('col')
All inputs are finite; a program needn't handle non-finite values.
Results may differ from a plain program's by a relative error of at most 0.017.
The roundings to bfloat16 on the way count: a program that leaves them out, or rounds other values in their place, can miss the bound.
Values may be sent and summed in bfloat16 or wider, within the bound.
No kernel may reach another device: no remote copies, remote signals or barrier semaphores. Data moves between devices by JAX's collectives and lax.ppermute only.
A program may use at most 128 MiB of HBM per device.

v0:
```python
import functools

import jax
import jax.numpy as jnp
from jax import lax
from jax.experimental import pallas as pl
from jax.experimental.pallas import tpu as pltpu
from jax.sharding import PartitionSpec as P


HEAD = 64
EPSILON = 1e-05
BF16 = jnp.bfloat16
F32 = jnp.float32
VMEM = pl.BlockSpec(memory_space=pltpu.VMEM)
SMEM = pl.BlockSpec(memory_space=pltpu.SMEM)
PARAMS = pltpu.CompilerParams(vmem_limit_bytes=16 * 2**20)
NT = (((1,), (1,)), ((), ()))
TN = (((0,), (0,)), ((), ()))


def dot(a, b):
    return jnp.dot(a, b, preferred_element_type=F32)


def split3(values):
    high = values.astype(BF16)
    rest = values - high.astype(F32)
    mid = rest.astype(BF16)
    low = (rest - mid.astype(F32)).astype(BF16)
    return high, mid, low


def normalize_kernel(tokens, gain, normed):
    values = tokens[...].astype(F32)
    center = values - jnp.mean(values, axis=-1, keepdims=True)
    spread = jnp.mean(center * center, axis=-1, keepdims=True)
    normed[...] = (center * lax.rsqrt(spread + EPSILON) * gain[...]).astype(BF16)


def normalize(tokens, gain):
    return pl.pallas_call(
        normalize_kernel,
        out_shape=jax.ShapeDtypeStruct(tokens.shape, BF16),
        in_specs=[VMEM, VMEM],
        out_specs=VMEM,
        compiler_params=PARAMS,
        name="normalize",
    )(tokens, gain)


def project_kernel(members, place, normed, weight, mine, theirs, turned):
    core = place[0]
    kept = mine.shape[0] * HEAD
    rows = normed[...]
    for at, member in enumerate(members):
        product = dot(rows, weight[member]).astype(BF16)
        if member == 0:
            product = product * jnp.asarray(1.0 / HEAD**0.5, BF16)
        turned[at] = product.T
        for which, out in ((1 - core, theirs), (core, mine)):
            for head in range(mine.shape[0]):
                start = pl.multiple_of(which * kept + head * HEAD, HEAD)
                out[head, at * HEAD : (at + 1) * HEAD, :] = turned[at, pl.ds(start, HEAD), :]


def project(members, place, normed, weight):
    count, length = weight.shape[2] // HEAD // 2, normed.shape[0]
    shape = jax.ShapeDtypeStruct((count, len(members) * HEAD, length), BF16)
    return pl.pallas_call(
        functools.partial(project_kernel, members),
        out_shape=(shape, shape),
        in_specs=[SMEM, VMEM, VMEM],
        out_specs=(VMEM,) * 2,
        scratch_shapes=[pltpu.VMEM((len(members), weight.shape[2], length), BF16)],
        compiler_params=PARAMS,
        name="project",
    )(place, normed, weight)


def attend(queries, block, running, best):
    length = block.shape[1]
    keys = block[:HEAD].T
    values = jnp.concatenate([block[HEAD:], jnp.ones((16, length), BF16)], axis=0)
    depth = min(512, length)
    for below in range(0, length, depth):
        scores = dot(keys[below : below + depth], queries)
        raised_top = jnp.max(scores, axis=0, keepdims=True)
        if best is not None:
            raised_top = jnp.maximum(best, raised_top)
        weights = jnp.exp(scores - raised_top).astype(BF16)
        added = dot(values[:, below : below + depth], weights)
        running = added if best is None else running * jnp.exp(best - raised_top) + added
        best = raised_top
    return running, best


def absorb_kernel(first, own, got, block, *refs):
    carried, carried_top = (None, None) if first else refs[:2]
    out, top = refs[-2:]
    length = own.shape[2]
    for head in range(own.shape[0]):
        for side, queries in enumerate((own, got)):
            where = slice(side * length, (side + 1) * length)
            running = None if first else carried[head, :, where]
            best = None if first else carried_top[head, 0:1, where]
            running, best = attend(queries[head], block[head], running, best)
            out[head, :, where] = running
            top[head, :, where] = jnp.broadcast_to(best, (8, length))


def absorb(queries, block, state):
    heads, _, length = queries[0].shape
    shapes = tuple(jax.ShapeDtypeStruct((heads, rows, 2 * length), F32) for rows in (HEAD + 16, 8))
    first = state is None
    return pl.pallas_call(
        functools.partial(absorb_kernel, first),
        out_shape=shapes,
        in_specs=[VMEM] * (3 if first else 5),
        out_specs=(VMEM, VMEM),
        input_output_aliases={} if first else {3: 0, 4: 1},
        compiler_params=PARAMS,
        name="absorb",
    )(*queries, block, *(() if first else state))


def closing_kernel(side, queries, block, carried, carried_top, folded, context, share):
    length = context.shape[1]
    where = slice(side * length, (side + 1) * length)
    for head in range(queries.shape[0]):
        running, _ = attend(queries[head], block[head], carried[head, :, where], carried_top[head, 0:1, where])
        context[head * HEAD : (head + 1) * HEAD, :] = (running[:HEAD] / running[HEAD : HEAD + 1]).astype(BF16)
    whole = context[...]
    share[...] = sum(dot(part, whole) for part in split3(folded[...]))


def closing(side, queries, block, state, folded):
    heads, _, length = queries[side].shape
    return pl.pallas_call(
        functools.partial(closing_kernel, side),
        out_shape=(
            jax.ShapeDtypeStruct((heads * HEAD, length), BF16),
            jax.ShapeDtypeStruct((folded.shape[0], length), F32),
        ),
        in_specs=[VMEM] * 5,
        out_specs=(VMEM, VMEM),
        compiler_params=PARAMS,
        name="closing",
    )(queries[side], block, *state, folded)


def arrange_kernel(weight, forward, backward):
    channels = weight.shape[1]
    for layer in range(weight.shape[0]):
        taps = weight[layer]
        turned_taps = taps.astype(F32).T
        for row in range(3):
            forward[layer, row] = taps[:, row * 3 * channels : (row + 1) * 3 * channels]
            at = [((2 - row) * 3 + 2 - column) * channels for column in range(3)]
            backward[layer, row] = jnp.concatenate(
                [turned_taps[start : start + channels, :] for start in at], axis=1
            ).astype(BF16)


def arrange(weight):
    layers, channels, wide = weight.shape
    shape = jax.ShapeDtypeStruct((layers, 3, channels, wide // 3), BF16)
    return pl.pallas_call(
        arrange_kernel,
        out_shape=(shape, shape),
        in_specs=[VMEM],
        out_specs=(VMEM, VMEM),
        compiler_params=PARAMS,
        name="arrange",
    )(weight)


def turned(values, step):
    return pltpu.roll(values, step % values.shape[1], 1)


def three_columns(values, cols):
    cells = values.shape[1]
    column = lax.rem(lax.broadcasted_iota(jnp.int32, (1, cells), 1), cols)
    wide = values.astype(F32)
    left = jnp.where(column == 0, 0.0, turned(wide, 1)).astype(BF16)
    right = jnp.where(column == cols - 1, 0.0, turned(wide, -1)).astype(BF16)
    return jnp.concatenate([left, values.astype(BF16), right], axis=0)


def three_rows(weights, columns, cols):
    cells = columns.shape[1] - 2 * cols
    return sum(dot(weights[a], columns[:, a * cols : a * cols + cells]) for a in range(3))


def network_kernel(
    cols, frame_rows, place, chip_map, near, far, forward, backward, head, own_context, their_context, holo, sums,
    gradient, hidden, pre_one, pre_two, grads,
):
    core, half, row_at = place[0], place[1], place[2]
    own = chip_map.shape[1]
    cells = hidden.shape[1]
    rim = (cells - own) // 2
    row_count = cells // cols
    above = rim // cols
    first_row = row_at - above
    piece = own // 2
    down = (core == place[3]).astype(jnp.int32)
    for source, base, lead in ((chip_map, own, core), (near, 2 * own * down, core), (far, 2 * own * (1 - down), 1 - core)):
        for side in range(2):
            start = pl.multiple_of(base + lax.rem(lead + side, 2) * piece, 128)
            hidden[:, pl.ds(start, piece)] = source[:, side * piece : (side + 1) * piece]

    def inside(start_row, rows):
        lane = lax.broadcasted_iota(jnp.int32, (1, rows * cols), 1)
        frame_lane = lane + (first_row + start_row) * cols
        return jnp.logical_and(frame_lane >= 0, frame_lane < frame_rows * cols)

    channels, outputs = forward.shape[2], head.shape[0]
    columns_zero = three_columns(jnp.where(inside(0, row_count), hidden[:channels, :].astype(F32), 0.0), cols)
    first = three_rows(forward[0], columns_zero, cols)
    rows_one = row_count - 2
    one = jnp.where(inside(1, rows_one), first * jax.nn.sigmoid(first), 0.0)
    columns_one = three_columns(one, cols)
    second = three_rows(forward[1], columns_one, cols)
    rows_two = row_count - 4
    sigmoid_two = jax.nn.sigmoid(second)
    two = (second * sigmoid_two).astype(BF16)
    holo[...] = dot(head[...], two[:, rim - 2 * cols : rim - 2 * cols + own])
    pieces = hidden[channels:, 2 * cols : cells - 2 * cols].astype(F32)
    cotangent = pieces[:outputs] + pieces[outputs : 2 * outputs] + pieces[2 * outputs : 3 * outputs]
    grad_two = lax.dot_general(
        head[...].astype(F32), cotangent, TN, precision=lax.Precision.HIGHEST, preferred_element_type=F32
    ).astype(BF16)
    slope = grad_two.astype(F32) * sigmoid_two * (1.0 + second * (1.0 - sigmoid_two))
    pre_grad_two = jnp.where(inside(2, rows_two), slope, 0.0)
    grad_one = three_rows(backward[1], three_columns(pre_grad_two, cols), cols).astype(BF16)
    rows_grad = row_count - 6
    middle = first[:, 2 * cols : 2 * cols + rows_grad * cols]
    sigmoid_one = jax.nn.sigmoid(middle)
    slope = grad_one.astype(F32) * sigmoid_one * (1.0 + middle * (1.0 - sigmoid_one))
    pre_grad_one = jnp.where(inside(3, rows_grad), slope, 0.0)
    grad_zero = three_rows(backward[0], three_columns(pre_grad_one, cols), cols).astype(BF16)
    pre_one[...] = pre_grad_one[:, rim - 3 * cols : rim - 3 * cols + own].astype(BF16)
    pre_two[...] = pre_grad_two[:, rim - 2 * cols : rim - 2 * cols + own].astype(BF16)

    share = sums.shape[0]
    taps = 9 * channels
    for layer, (pre, columns, offset) in enumerate(((pre_one, columns_zero, rim), (pre_two, columns_one, rim - cols))):

        @pl.when(core == layer)
        def _(pre=pre, columns=columns, offset=offset):
            stacked = jnp.concatenate(
                [columns[:, offset + (a - 1) * cols : offset + (a - 1) * cols + own] for a in range(3)], axis=0
            )
            rows = pre[pl.ds(pl.multiple_of(half * share, 16), share), :]
            sums[:, :taps] = lax.dot_general(rows, stacked, NT, preferred_element_type=F32)

    grads[...] = grad_zero
    gradient[...] = sum(
        lax.dot_general(
            grads[:, pl.ds(pl.multiple_of(at * piece, 128), piece)], seen[...], NT, preferred_element_type=F32
        )
        for at, seen in ((core, own_context), (1 - core, their_context))
    )


def network(place, maps, forward, backward, head, own_context, their_context, cols, frame_rows, col_count):
    own = maps[0].shape[1]
    channels = forward.shape[2]
    return pl.pallas_call(
        functools.partial(network_kernel, cols, frame_rows),
        out_shape=(
            jax.ShapeDtypeStruct((head.shape[0], own), F32),
            jax.ShapeDtypeStruct((channels // col_count, 9 * channels), F32),
            jax.ShapeDtypeStruct((channels, own_context.shape[0]), F32),
        ),
        in_specs=[SMEM] + [VMEM] * 8,
        out_specs=(VMEM,) * 3,
        scratch_shapes=[pltpu.VMEM((maps[0].shape[0], 3 * own), BF16)] + [pltpu.VMEM((channels, own), BF16)] * 3,
        compiler_params=PARAMS,
        name="network",
    )(place, *maps, forward, backward, head, own_context, their_context)


def swapped(values, axis):
    size = lax.axis_size(axis)
    return lax.ppermute(values, axis, [(i, i ^ 1) for i in range(size)])


def passed(values, axis, step, wrap):
    size = lax.axis_size(axis)
    pairs = [(i, (i + step) % size) for i in range(size) if wrap or 0 <= i + step < size]
    return lax.ppermute(values, axis, pairs)


def beside(values):
    size, cols = lax.axis_size("tok"), lax.axis_size("col")
    pairs = []
    for at in range(size // 2):
        for core, other in ((0, at ^ 1), (1, ((at + 1) ^ 1) - 1)):
            inside = 0 <= other < size // 2
            for col in range(cols):
                target = (other if inside else at, col if inside or cols == 1 else col ^ 1)
                pairs.append(((2 * at + core) * cols + col, (2 * target[0] + core) * cols + target[1]))
    return lax.ppermute(values, ("tok", "col"), pairs)


def round_ring(values):
    size = lax.axis_size("tok")
    chips = size // 2
    order = [at for at in range(chips) if at == 0 or at % 2 == 1] + [
        at for at in reversed(range(chips)) if at and at % 2 == 0
    ]
    following = {order[at]: order[(at + 1) % chips] for at in range(chips)}
    return lax.ppermute(values, "tok", [(i, 2 * following[i // 2] + i % 2) for i in range(size)])


def everyone(values, axis, stride, count):
    sent = values.astype(BF16)
    terms = [(passed(sent, axis, stride * step, True) if step else sent).astype(F32) for step in range(count)]
    while len(terms) > 1:
        apart = len(terms) // 2
        terms = [terms[at] + terms[at + apart] for at in range(apart)]
    return terms[0]


def in_order(core, mine, theirs, axis):
    return jnp.where(
        core == 0, jnp.concatenate([mine, theirs], axis=axis), jnp.concatenate([theirs, mine], axis=axis)
    )


def step(
    tokens, ln_gain, qkv_weight, out_weight, readout_weight, conv_weight, head_weight, holo_cot
):
    frame_rows = tokens[0]
    cotangent = holo_cot[0]
    rows_dev, cols_dev = cotangent.shape[1:]
    tok_count, col_count, dp_count = (lax.axis_size(axis) for axis in ("tok", "col", "dp"))
    chips = tok_count // 2
    tok_at, half = lax.axis_index("tok"), lax.axis_index("col")
    core = lax.rem(tok_at, 2)
    chip_row = (tok_at - core) * rows_dev
    place = jnp.stack([core, half, chip_row, lax.rem(tok_at // 2, 2)]).astype(jnp.int32)
    cols = cols_dev * col_count

    gain, qkv_weight, out_weight = lax.optimization_barrier(
        (ln_gain.astype(F32).reshape(1, -1), qkv_weight, out_weight)
    )
    normed = normalize(frame_rows, gain)
    own_keyed, their_keyed = project((1, 2), place, normed, qkv_weight)
    own_keyed, their_keyed, normed = lax.optimization_barrier((own_keyed, their_keyed, normed))
    got_keyed = swapped(their_keyed, "tok")
    own_queries, their_queries = project((0,), place, normed, qkv_weight)
    queries = (own_queries, swapped(their_queries, "tok"))
    kept = own_keyed.shape[0] * HEAD

    def prepare(conv_weight, out_weight, readout_weight, frame_rows, cotangent):
        forward, backward = arrange(conv_weight)
        own_out = lax.dynamic_slice_in_dim(out_weight, core * kept, kept, 0)
        folded = lax.dot_general(readout_weight, own_out, (((0,), (1,)), ((), ())), preferred_element_type=F32)
        direct = lax.dot_general(readout_weight, frame_rows, (((0,), (1,)), ((), ())), preferred_element_type=F32)
        wide_cot = in_order(half, cotangent, swapped(cotangent, "col"), 2)
        exact_cot = jnp.concatenate(split3(wide_cot.reshape(wide_cot.shape[0], -1)), axis=0)
        exact_cot = jnp.pad(exact_cot, ((0, -exact_cot.shape[0] % 16), (0, 0)))
        return (forward, backward, folded, direct, exact_cot)

    state, blocks = None, [own_keyed, got_keyed]
    for turn in range(chips):
        arriving = []
        if turn < chips - 1:
            for block in blocks:
                arriving.append(round_ring(block))
        for at, block in enumerate(blocks):
            if turn == chips - 1 and at == 1:
                break
            state = absorb(queries, block, state)
            if at == 1 and turn == min(1, chips - 2):
                state, given = lax.optimization_barrier(
                    (state, (conv_weight, out_weight, readout_weight, frame_rows, cotangent))
                )
                prepared = prepare(*given)
            if at == 0 and turn == chips - 1:
                state, prepared = lax.optimization_barrier((state, prepared))
            if turn < chips - 2:
                arriving[at], state = lax.optimization_barrier((arriving[at], state))
        blocks = arriving if turn < chips - 1 else blocks
    forward, backward, folded, direct, exact_cot = prepared

    their_context, their_share = closing(1, queries, blocks[1], state, folded)
    own_context, own_share = closing(0, queries, blocks[1], state, folded)
    partial = own_share + swapped(their_share, "tok")
    partial = (partial + jnp.where(half == 0, direct, 0.0)).astype(BF16)
    own_map = (partial.astype(F32) + swapped(partial, "col").astype(F32)).astype(BF16)
    own_map = jnp.concatenate([own_map, exact_cot], axis=0)
    chip_map = jnp.concatenate([own_map, swapped(own_map, "tok")], axis=1)
    near = beside(chip_map)
    rows_chip = 2 * rows_dev
    maps = (chip_map, near, swapped(near, "tok"))
    holo, sums, gradient = network(
        place, maps, forward, backward, head_weight, own_context, their_context, cols, tok_count * rows_dev, col_count
    )
    holo = holo.reshape(-1, rows_chip, cols)
    hologram = lax.dynamic_slice(
        holo, (0, core * rows_dev, half * cols_dev), (holo.shape[0], rows_dev, cols_dev)
    )

    taps_wide = sums.shape[1]
    lanes = 128 * ((taps_wide + 127) // 128)
    rows = sums.shape[0]
    pieces = gradient.shape[0] // rows
    folded_gradient = [gradient[at * rows : (at + 1) * rows] for at in range(pieces)]
    sent = jnp.concatenate([jnp.pad(sums, ((0, 0), (0, lanes - taps_wide))), *folded_gradient], axis=1)
    summed = everyone(sent, "dp", 1, dp_count)
    total = everyone(summed, "tok", 2, chips)
    own_grad = total[:, :taps_wide]
    col_grad = swapped(own_grad, "col")
    wide = gradient.shape[1]
    own_small = jnp.concatenate(
        [total[:, lanes + at * wide : lanes + (at + 1) * wide] for at in range(pieces)], axis=0
    )
    small = in_order(core, own_small, swapped(own_small, "tok"), 1)
    out_grad = lax.dot_general(
        small, readout_weight.astype(F32), (((0,), (1,)), ((), ())), precision=lax.Precision.HIGHEST
    )
    core_grad = swapped(own_grad, "tok")
    col_grad, out_grad, core_grad = lax.optimization_barrier((col_grad, out_grad, core_grad))
    far_grad = swapped(col_grad, "tok")
    layer_grad = in_order(half, own_grad, col_grad, 0)
    other_grad = in_order(half, core_grad, far_grad, 0)
    conv_grad = in_order(core, layer_grad[None], other_grad[None], 0)
    return (hologram[None], conv_grad, out_grad)


def solution(mesh):
    in_specs = (
        P("dp", "tok", None),
        P(),
        P(None, None, "col"),
        P("col", None),
        P(),
        P(),
        P(),
        P("dp", None, "tok", "col"),
    )
    out_specs = (P("dp", None, "tok", "col"), P(), P("col", None))
    return jax.shard_map(step, mesh=mesh, in_specs=in_specs, out_specs=out_specs, check_vma=False)
```

profile of v0, /device:TPU:0, one launch (start us, length us, event | category | flops | bytes accessed | tf_op | source)
XLA Modules:
  0.0 86.9 jit_solution(15423779145423106359)
XLA Ops:
  3.5 1.4 %project.2 = (bf16[2,128,512]{2,1,0:T(8,128)(2,1)S(1)}, bf16[2,128,512]{2,1,0:T(8,128)(2,1)S(1)}) custom-call(s32[4]{0:T(128)S(1)} %pad_add_fusion.place, bf16[512,1024]{1,0:T(8,128)(2,1)S(1)} %normalize.1.normed, bf16[3,1024,256]{2,1,0:T(8,128)(2,1)S(1)} %copy-done.1), custom_call_target="tpu_custom_call" | custom-call | tf_op jit(solution)/shard_map/project/pallas_call | solution.py:70
  5.4 2.6 %collective-permute-start.3 = (bf16[2,128,512]{2,1,0:T(8,128)(2,1)S(1)}, bf16[2,128,512]{2,1,0:T(8,128)(2,1)S(1)}, u32[]{:S(2)}, u32[]{:S(2)}) collective-permute-start(bf16[2,128,512]{2,1,0:T(8,128)(2,1)S(1)} %get-tuple-element.73.block), channel_id=1, source_target_pairs={{0,4},{2,6},{4,12},{6,14},{8,0},{10,2},{12,8},{14,10},{1,5},{3,7},... | collective-permute-start | bytes 786440 | tf_op jit(solution)/shard_map/ppermute | solution.py:316
  9.3 2.6 %collective-permute-start.1 = (bf16[2,128,512]{2,1,0:T(8,128)(2,1)S(1)}, bf16[2,128,512]{2,1,0:T(8,128)(2,1)S(1)}, u32[]{:S(2)}, u32[]{:S(2)}) collective-permute-start(bf16[2,128,512]{2,1,0:T(8,128)(2,1)S(1)} %collective-permute-done.block), channel_id=1, source_target_pairs={{0,4},{2,6},{4,12},{6,14},{8,0},{10,2},{12,8},{14,10},{1,5},{3,7},... | collective-permute-start | bytes 786440 | tf_op jit(solution)/shard_map/ppermute | solution.py:316
  11.9 2.0 %absorb.7 = (f32[2,80,1024]{2,1,0:T(8,128)S(1)}, f32[2,8,1024]{2,1,0:T(8,128)S(1)}) custom-call(bf16[2,64,512]{2,1,0:T(8,128)(2,1)S(1)} %get-tuple-element.70.own.queries, bf16[2,64,512]{2,1,0:T(8,128)(2,1)S(1)} %collective-permute-done.2.got.queries, bf16[2,128,512]{2,1,0:T(8,128)(2,1)S(1)} %get-tuple-element.73.block), custom_call_target="tpu_custom_call" | custom-call | tf_op jit(solution)/shard_map/absorb/pallas_call | solution.py:116
  13.9 2.3 %collective-permute-done.3.block = bf16[2,128,512]{2,1,0:T(8,128)(2,1)S(1)} collective-permute-done((bf16[2,128,512]{2,1,0:T(8,128)(2,1)S(1)}, bf16[2,128,512]{2,1,0:T(8,128)(2,1)S(1)}, u32[]{:S(2)}, u32[]{:S(2)}) %collective-permute-start.3) | collective-permute-done | bytes 262176 | tf_op jit(solution)/shard_map/ppermute | solution.py:316
  17.3 2.0 %absorb.8 = (f32[2,80,1024]{2,1,0:T(8,128)S(1)}, f32[2,8,1024]{2,1,0:T(8,128)S(1)}) custom-call(bf16[2,64,512]{2,1,0:T(8,128)(2,1)S(1)} %get-tuple-element.70.own.queries, bf16[2,64,512]{2,1,0:T(8,128)(2,1)S(1)} %collective-permute-done.2.got.queries, ...), custom_call_target="tpu_custom_call", output_to_operand_aliasing={{0}: (3, {}), {1}: (4, {})} | custom-call | tf_op jit(solution)/shard_map/absorb/pallas_call | solution.py:116
  19.4 2.4 %collective-permute-done.1.block = bf16[2,128,512]{2,1,0:T(8,128)(2,1)S(1)} collective-permute-done((bf16[2,128,512]{2,1,0:T(8,128)(2,1)S(1)}, bf16[2,128,512]{2,1,0:T(8,128)(2,1)S(1)}, u32[]{:S(2)}, u32[]{:S(2)}) %collective-permute-start.1) | collective-permute-done | bytes 262176 | tf_op jit(solution)/shard_map/ppermute | solution.py:316
  21.8 2.0 %absorb.9 = (f32[2,80,1024]{2,1,0:T(8,128)S(1)}, f32[2,8,1024]{2,1,0:T(8,128)S(1)}) custom-call(bf16[2,64,512]{2,1,0:T(8,128)(2,1)S(1)} %get-tuple-element.70.own.queries, bf16[2,64,512]{2,1,0:T(8,128)(2,1)S(1)} %collective-permute-done.2.got.queries, ...), custom_call_target="tpu_custom_call", output_to_operand_aliasing={{0}: (3, {}), {1}: (4, {})} | custom-call | tf_op jit(solution)/shard_map/absorb/pallas_call | solution.py:116
  23.9 3.3 %collective-permute-done.5.block = bf16[2,128,512]{2,1,0:T(8,128)(2,1)S(1)} collective-permute-done((bf16[2,128,512]{2,1,0:T(8,128)(2,1)S(1)}, bf16[2,128,512]{2,1,0:T(8,128)(2,1)S(1)}, u32[]{:S(2)}, u32[]{:S(2)}) %collective-permute-start.5) | collective-permute-done | bytes 262176 | tf_op jit(solution)/shard_map/ppermute | solution.py:316
  28.1 2.0 %absorb.10 = (f32[2,80,1024]{2,1,0:T(8,128)S(1)}, f32[2,8,1024]{2,1,0:T(8,128)S(1)}) custom-call(bf16[2,64,512]{2,1,0:T(8,128)(2,1)S(1)} %get-tuple-element.70.own.queries, bf16[2,64,512]{2,1,0:T(8,128)(2,1)S(1)} %collective-permute-done.2.got.queries, ...), custom_call_target="tpu_custom_call", output_to_operand_aliasing={{0}: (3, {}), {1}: (4, {})} | custom-call | tf_op jit(solution)/shard_map/absorb/pallas_call | solution.py:116
  30.1 1.6 %collective-permute-start.8 = (f32[2,2,128]{2,1,0:T(2,128)S(1)}, f32[2,2,128]{2,1,0:T(2,128)S(1)}, u32[]{:S(2)}, u32[]{:S(2)}) collective-permute-start(f32[2,2,128]{2,1,0:T(2,128)S(1)} %bitcast.29), channel_id=1, source_target_pairs={{0,1},{1,0},{2,3},{3,2},{4,5},{5,4},{6,7},{7,6},{8,9},{9,8},{10,11... | collective-permute-start | bytes 6152 | tf_op jit(solution)/shard_map/ppermute | solution.py:288
  31.7 3.4 %collective-permute-start.7 = (bf16[2,128,512]{2,1,0:T(8,128)(2,1)S(1)}, bf16[2,128,512]{2,1,0:T(8,128)(2,1)S(1)}, u32[]{:S(2)}, u32[]{:S(2)}) collective-permute-start(bf16[2,128,512]{2,1,0:T(8,128)(2,1)S(1)} %collective-permute-done.5.block), channel_id=1, source_target_pairs={{0,4},{2,6},{4,12},{6,14},{8,0},{10,2},{12,8},{14,10},{1,5},{3,7},... | collective-permute-start | bytes 786440 | tf_op jit(solution)/shard_map/ppermute | solution.py:316
  38.2 2.1 %absorb.11 = (f32[2,80,1024]{2,1,0:T(8,128)S(1)}, f32[2,8,1024]{2,1,0:T(8,128)S(1)}) custom-call(bf16[2,64,512]{2,1,0:T(8,128)(2,1)S(1)} %get-tuple-element.70.own.queries, bf16[2,64,512]{2,1,0:T(8,128)(2,1)S(1)} %collective-permute-done.2.got.queries, ...), custom_call_target="tpu_custom_call", output_to_operand_aliasing={{0}: (3, {}), {1}: (4, {})} | custom-call | tf_op jit(solution)/shard_map/absorb/pallas_call | solution.py:116
  40.2 2.1 %absorb.12 = (f32[2,80,1024]{2,1,0:T(8,128)S(1)}, f32[2,8,1024]{2,1,0:T(8,128)S(1)}) custom-call(bf16[2,64,512]{2,1,0:T(8,128)(2,1)S(1)} %get-tuple-element.70.own.queries, bf16[2,64,512]{2,1,0:T(8,128)(2,1)S(1)} %collective-permute-done.2.got.queries, ...), custom_call_target="tpu_custom_call", output_to_operand_aliasing={{0}: (3, {}), {1}: (4, {})} | custom-call | tf_op jit(solution)/shard_map/absorb/pallas_call | solution.py:116
  42.9 2.0 %absorb.13 = (f32[2,80,1024]{2,1,0:T(8,128)S(1)}, f32[2,8,1024]{2,1,0:T(8,128)S(1)}) custom-call(bf16[2,64,512]{2,1,0:T(8,128)(2,1)S(1)} %get-tuple-element.70.own.queries, bf16[2,64,512]{2,1,0:T(8,128)(2,1)S(1)} %collective-permute-done.2.got.queries, ...), custom_call_target="tpu_custom_call", output_to_operand_aliasing={{0}: (3, {}), {1}: (4, {})} | custom-call | tf_op jit(solution)/shard_map/absorb/pallas_call | solution.py:116
  45.0 2.4 %collective-permute-done.6.block = bf16[2,128,512]{2,1,0:T(8,128)(2,1)S(1)} collective-permute-done((bf16[2,128,512]{2,1,0:T(8,128)(2,1)S(1)}, bf16[2,128,512]{2,1,0:T(8,128)(2,1)S(1)}, u32[]{:S(2)}, u32[]{:S(2)}) %collective-permute-start.6) | collective-permute-done | bytes 262176 | tf_op jit(solution)/shard_map/ppermute | solution.py:316
  47.4 1.3 %closing.3 = (bf16[128,512]{1,0:T(8,128)(2,1)S(1)}, f32[64,512]{1,0:T(8,128)S(1)}) custom-call(bf16[2,64,512]{2,1,0:T(8,128)(2,1)S(1)} %collective-permute-done.2.got.queries, bf16[2,128,512]{2,1,0:T(8,128)(2,1)S(1)} %collective-permute-done.6.block, f32[2,80,1024]{2,1,0:T(8,128)S(1)} %get-tuple-element.110.carried, ...), custom_call_target="tpu_custom_call" | custom-call | tf_op jit(solution)/shard_map/closing/pallas_call | solution.py:139
  48.8 1.3 %closing.2 = (bf16[128,512]{1,0:T(8,128)(2,1)S(1)}, f32[64,512]{1,0:T(8,128)S(1)}) custom-call(bf16[2,64,512]{2,1,0:T(8,128)(2,1)S(1)} %get-tuple-element.70.own.queries, bf16[2,128,512]{2,1,0:T(8,128)(2,1)S(1)} %collective-permute-done.6.block, f32[2,80,1024]{2,1,0:T(8,128)S(1)} %get-tuple-element.110.carried, ...), custom_call_target="tpu_custom_call" | custom-call | tf_op jit(solution)/shard_map/closing/pallas_call | solution.py:139
  50.2 1.3 %collective-permute-start.10 = (bf16[64,512]{1,0:T(8,128)(2,1)S(1)}, bf16[64,512]{1,0:T(8,128)(2,1)S(1)}, u32[]{:S(2)}, u32[]{:S(2)}) collective-permute-start(bf16[64,512]{1,0:T(8,128)(2,1)S(1)} %add_convert_fusion.1), channel_id=1, source_target_pairs={{0,1},{1,0},{2,3},{3,2},{4,5},{5,4},{6,7},{7,6},{8,9},{9,8},{10,11... | collective-permute-start | bytes 196616 | tf_op jit(solution)/shard_map/ppermute | solution.py:288
  51.5 3.2 %collective-permute-done.10 = bf16[64,512]{1,0:T(8,128)(2,1)S(1)} collective-permute-done((bf16[64,512]{1,0:T(8,128)(2,1)S(1)}, bf16[64,512]{1,0:T(8,128)(2,1)S(1)}, u32[]{:S(2)}, u32[]{:S(2)}) %collective-permute-start.10) | collective-permute-done | bytes 65568 | tf_op jit(solution)/shard_map/ppermute | solution.py:288
  56.7 4.8 %collective-permute-done.12.near = bf16[80,1024]{1,0:T(8,128)(2,1)S(1)} collective-permute-done((bf16[80,1024]{1,0:T(8,128)(2,1)S(1)}, bf16[80,1024]{1,0:T(8,128)(2,1)S(1)}, u32[]{:S(2)}, u32[]{:S(2)}) %collective-permute-start.12) | collective-permute-done | bytes 163872 | tf_op jit(solution)/shard_map/ppermute | solution.py:306
  61.5 1.4 %collective-permute-done.13.far = bf16[80,1024]{1,0:T(8,128)(2,1)S(1)} collective-permute-done((bf16[80,1024]{1,0:T(8,128)(2,1)S(1)}, bf16[80,1024]{1,0:T(8,128)(2,1)S(1)}, u32[]{:S(2)}, u32[]{:S(2)}) %collective-permute-start.13) | collective-permute-done | bytes 163872 | tf_op jit(solution)/shard_map/ppermute | solution.py:288
  62.9 3.8 %network.1 = (f32[2,1024]{1,0:T(2,128)S(1)}, f32[32,576]{1,0:T(8,128)S(1)}, f32[64,128]{1,0:T(8,128)S(1)}) custom-call(s32[4]{0:T(128)S(1)} %pad_add_fusion.place, bf16[80,1024]{1,0:T(8,128)(2,1)S(1)} %pad_maximum_fusion.chip_map, bf16[80,1024]{1,0:T(8,128)(2,1)S(1)} %collective-permute-done.12.near, bf16[80,1024]{1,0:T(8,128)(2,1)S(1)} %collective-permute-done.13.far, ...), custom_call_target="tpu_custom_call" | custom-call | tf_op jit(solution)/shard_map/network/pallas_call | solution.py:271
  66.8 1.4 %collective-permute-start.14 = (bf16[32,896]{1,0:T(8,128)(2,1)S(1)}, bf16[32,896]{1,0:T(8,128)(2,1)S(1)}, u32[]{:S(2)}, u32[]{:S(2)}) collective-permute-start(bf16[32,896]{1,0:T(8,128)(2,1)S(1)} %fusion.14), channel_id=1, source_target_pairs={{0,16},{16,0},{1,17},{17,1},{2,18},{18,2},{3,19},{19,3},{4,20},{20... | collective-permute-start | bytes 172040 | tf_op jit(solution)/shard_map/ppermute | solution.py:294
  68.2 2.9 %collective-permute-done.14 = bf16[32,896]{1,0:T(8,128)(2,1)S(1)} collective-permute-done((bf16[32,896]{1,0:T(8,128)(2,1)S(1)}, bf16[32,896]{1,0:T(8,128)(2,1)S(1)}, u32[]{:S(2)}, u32[]{:S(2)}) %collective-permute-start.14) | collective-permute-done | bytes 57376 | tf_op jit(solution)/shard_map/ppermute | solution.py:294
  71.1 2.0 %collective-permute-start.15 = (bf16[32,896]{1,0:T(8,128)(2,1)S(1)}, bf16[32,896]{1,0:T(8,128)(2,1)S(1)}, u32[]{:S(2)}, u32[]{:S(2)}) collective-permute-start(bf16[32,896]{1,0:T(8,128)(2,1)S(1)} %add_convert_fusion.2), channel_id=1, source_target_pairs={{0,8},{2,10},{4,12},{6,14},{8,0},{10,2},{12,4},{14,6},{1,9},{3,11}... | collective-permute-start | bytes 172040 | tf_op jit(solution)/shard_map/ppermute | solution.py:294
  73.1 2.0 %collective-permute-start.16 = (bf16[32,896]{1,0:T(8,128)(2,1)S(1)}, bf16[32,896]{1,0:T(8,128)(2,1)S(1)}, u32[]{:S(2)}, u32[]{:S(2)}) collective-permute-start(bf16[32,896]{1,0:T(8,128)(2,1)S(1)} %add_convert_fusion.2), channel_id=1, source_target_pairs={{0,4},{2,6},{4,8},{6,10},{8,12},{10,14},{12,0},{14,2},{1,5},{3,7},... | collective-permute-start | bytes 172040 | tf_op jit(solution)/shard_map/ppermute | solution.py:294
  75.1 1.8 %collective-permute-start.17 = (bf16[32,896]{1,0:T(8,128)(2,1)S(1)}, bf16[32,896]{1,0:T(8,128)(2,1)S(1)}, u32[]{:S(2)}, u32[]{:S(2)}) collective-permute-start(bf16[32,896]{1,0:T(8,128)(2,1)S(1)} %add_convert_fusion.2), channel_id=1, source_target_pairs={{0,12},{2,14},{4,0},{6,2},{8,4},{10,6},{12,8},{14,10},{1,13},{3,15... | collective-permute-start | bytes 172040 | tf_op jit(solution)/shard_map/ppermute | solution.py:294
  77.8 1.4 %collective-permute-done.16 = bf16[32,896]{1,0:T(8,128)(2,1)S(1)} collective-permute-done((bf16[32,896]{1,0:T(8,128)(2,1)S(1)}, bf16[32,896]{1,0:T(8,128)(2,1)S(1)}, u32[]{:S(2)}, u32[]{:S(2)}) %collective-permute-start.16) | collective-permute-done | bytes 57376 | tf_op jit(solution)/shard_map/ppermute | solution.py:294
  79.9 1.6 %collective-permute-start.18 = (f32[32,576]{1,0:T(8,128)S(1)}, f32[32,576]{1,0:T(8,128)S(1)}, u32[]{:S(2)}, u32[]{:S(2)}) collective-permute-start(f32[32,576]{1,0:T(8,128)S(1)} %get-tuple-element.128), channel_id=1, source_target_pairs={{0,1},{1,0},{2,3},{3,2},{4,5},{5,4},{6,7},{7,6},{8,9},{9,8},{10,11... | collective-permute-start | bytes 221192 | tf_op jit(solution)/shard_map/ppermute | solution.py:288
  81.7 1.6 %fusion.3 = f32[256,1024]{1,0:T(8,128)} fusion(bf16[1024,64]{0,1:T(8,128)(2,1)S(1)} %copy-done.6, f32[64,128]{1,0:T(8,128)S(1)} %collective-permute-done.19, f32[32,128]{1,0:T(8,128)S(1)} %get-tuple-element.130, f32[32,128]{1,0:T(8,128)S(1)} %get-tuple-element.129, pred[]{:T(512)S(6)} %eq.5), kind=kOutput, calls=%fused_computation.14 | convolution fusion | flops 201408512 | bytes 1245185 | tf_op jit(solution)/shard_map/dot_general | solution.py:424
  83.3 1.5 %collective-permute-done.18 = f32[32,576]{1,0:T(8,128)S(1)} collective-permute-done((f32[32,576]{1,0:T(8,128)S(1)}, f32[32,576]{1,0:T(8,128)S(1)}, u32[]{:S(2)}, u32[]{:S(2)}) %collective-permute-start.18) | collective-permute-done | bytes 73760 | tf_op jit(solution)/shard_map/ppermute | solution.py:288
  (70 shorter events, 16.4 us)
Async XLA Ops:
  0.6 34.9 %copy-start = (bf16[256,1024]{1,0:T(8,128)(2,1)S(1)}, bf16[256,1024]{1,0:T(8,128)(2,1)}, u32[]{:S(2)}) copy-start(bf16[256,1024]{1,0:T(8,128)(2,1)} %param.11) | copy-start | bytes 1572868
  0.6 2.8 %copy-start.1 = (bf16[3,1024,256]{2,1,0:T(8,128)(2,1)S(1)}, bf16[3,1024,256]{2,1,0:T(8,128)(2,1)}, u32[]{:S(2)}) copy-start(bf16[3,1024,256]{2,1,0:T(8,128)(2,1)} %weight.1) | copy-start | bytes 4718596
  1.5 1.2 %copy-start.2 = (bf16[1,512,1024]{2,1,0:T(8,128)(2,1)S(1)}, bf16[1,512,1024]{2,1,0:T(8,128)(2,1)}, u32[]{:S(2)}) copy-start(bf16[1,512,1024]{2,1,0:T(8,128)(2,1)} %param.8) | copy-start | bytes 3145732
  4.9 4.5 %collective-permute-start = (bf16[2,128,512]{2,1,0:T(8,128)(2,1)S(1)}, bf16[2,128,512]{2,1,0:T(8,128)(2,1)S(1)}, u32[]{:S(2)}, u32[]{:S(2)}) collective-permute-start(bf16[2,128,512]{2,1,0:T(8,128)(2,1)S(1)} %get-tuple-element.71), channel_id=1, source_target_pairs={{0,2},{2,0},{4,6},{6,4},{8,10},{10,8},{12,14},{14,12},{1,3},{3,1},... | collective-permute-start | bytes 786440 | tf_op jit(solution)/shard_map/ppermute | solution.py:288
  5.4 10.8 %collective-permute-start.3 = (bf16[2,128,512]{2,1,0:T(8,128)(2,1)S(1)}, bf16[2,128,512]{2,1,0:T(8,128)(2,1)S(1)}, u32[]{:S(2)}, u32[]{:S(2)}) collective-permute-start(bf16[2,128,512]{2,1,0:T(8,128)(2,1)S(1)} %get-tuple-element.73.block), channel_id=1, source_target_pairs={{0,4},{2,6},{4,12},{6,14},{8,0},{10,2},{12,8},{14,10},{1,5},{3,7},... | collective-permute-start | bytes 786440 | tf_op jit(solution)/shard_map/ppermute | solution.py:316
  9.1 2.8 %collective-permute-start.2 = (bf16[2,64,512]{2,1,0:T(8,128)(2,1)S(1)}, bf16[2,64,512]{2,1,0:T(8,128)(2,1)S(1)}, u32[]{:S(2)}, u32[]{:S(2)}) collective-permute-start(bf16[2,64,512]{2,1,0:T(8,128)(2,1)S(1)} %get-tuple-element.72), channel_id=1, source_target_pairs={{0,2},{2,0},{4,6},{6,4},{8,10},{10,8},{12,14},{14,12},{1,3},{3,1},... | collective-permute-start | bytes 393224 | tf_op jit(solution)/shard_map/ppermute | solution.py:288
  9.3 12.5 %collective-permute-start.1 = (bf16[2,128,512]{2,1,0:T(8,128)(2,1)S(1)}, bf16[2,128,512]{2,1,0:T(8,128)(2,1)S(1)}, u32[]{:S(2)}, u32[]{:S(2)}) collective-permute-start(bf16[2,128,512]{2,1,0:T(8,128)(2,1)S(1)} %collective-permute-done.block), channel_id=1, source_target_pairs={{0,4},{2,6},{4,12},{6,14},{8,0},{10,2},{12,8},{14,10},{1,5},{3,7},... | collective-permute-start | bytes 786440 | tf_op jit(solution)/shard_map/ppermute | solution.py:316
  16.2 11.0 %collective-permute-start.5 = (bf16[2,128,512]{2,1,0:T(8,128)(2,1)S(1)}, bf16[2,128,512]{2,1,0:T(8,128)(2,1)S(1)}, u32[]{:S(2)}, u32[]{:S(2)}) collective-permute-start(bf16[2,128,512]{2,1,0:T(8,128)(2,1)S(1)} %collective-permute-done.3.block), channel_id=1, source_target_pairs={{0,4},{2,6},{4,12},{6,14},{8,0},{10,2},{12,8},{14,10},{1,5},{3,7},... | collective-permute-start | bytes 786440 | tf_op jit(solution)/shard_map/ppermute | solution.py:316
  17.3 12.8 %copy-start.7 = (f32[1,2,2,128]{3,2,1,0:T(2,128)S(1)}, f32[1,2,2,128]{3,2,1,0:T(2,128)}, u32[]{:S(2)}) copy-start(f32[1,2,2,128]{3,2,1,0:T(2,128)} %param.15) | copy-start | bytes 6148
  17.3 17.7 %copy-start.3 = (bf16[1,512,1024]{2,1,0:T(8,128)(2,1)S(1)}, bf16[1,512,1024]{2,1,0:T(8,128)(2,1)}, u32[]{:S(2)}) copy-start(bf16[1,512,1024]{2,1,0:T(8,128)(2,1)} %param.8) | copy-start | bytes 3145732
  17.3 17.7 %copy-start.6 = (bf16[1024,64]{0,1:T(8,128)(2,1)S(1)}, bf16[1024,64]{0,1:T(8,128)(2,1)}, u32[]{:S(2)}) copy-start(bf16[1024,64]{0,1:T(8,128)(2,1)} %param.12) | copy-start | bytes 393220
  23.9 11.8 %copy-start.4 = (bf16[2,64,576]{2,1,0:T(8,128)(2,1)S(1)}, bf16[2,64,576]{2,1,0:T(8,128)(2,1)}, u32[]{:S(2)}) copy-start(bf16[2,64,576]{2,1,0:T(8,128)(2,1)} %weight.2) | copy-start | bytes 442372
  27.2 10.1 %collective-permute-start.4 = (bf16[2,128,512]{2,1,0:T(8,128)(2,1)S(1)}, bf16[2,128,512]{2,1,0:T(8,128)(2,1)S(1)}, u32[]{:S(2)}, u32[]{:S(2)}) collective-permute-start(bf16[2,128,512]{2,1,0:T(8,128)(2,1)S(1)} %collective-permute-done.1.block), channel_id=1, source_target_pairs={{0,4},{2,6},{4,12},{6,14},{8,0},{10,2},{12,8},{14,10},{1,5},{3,7},... | collective-permute-start | bytes 786440 | tf_op jit(solution)/shard_map/ppermute | solution.py:316
  30.1 5.9 %collective-permute-start.8 = (f32[2,2,128]{2,1,0:T(2,128)S(1)}, f32[2,2,128]{2,1,0:T(2,128)S(1)}, u32[]{:S(2)}, u32[]{:S(2)}) collective-permute-start(f32[2,2,128]{2,1,0:T(2,128)S(1)} %bitcast.29), channel_id=1, source_target_pairs={{0,1},{1,0},{2,3},{3,2},{4,5},{5,4},{6,7},{7,6},{8,9},{9,8},{10,11... | collective-permute-start | bytes 6152 | tf_op jit(solution)/shard_map/ppermute | solution.py:288
  31.7 11.2 %collective-permute-start.7 = (bf16[2,128,512]{2,1,0:T(8,128)(2,1)S(1)}, bf16[2,128,512]{2,1,0:T(8,128)(2,1)S(1)}, u32[]{:S(2)}, u32[]{:S(2)}) collective-permute-start(bf16[2,128,512]{2,1,0:T(8,128)(2,1)S(1)} %collective-permute-done.5.block), channel_id=1, source_target_pairs={{0,4},{2,6},{4,12},{6,14},{8,0},{10,2},{12,8},{14,10},{1,5},{3,7},... | collective-permute-start | bytes 786440 | tf_op jit(solution)/shard_map/ppermute | solution.py:316
  37.3 10.1 %collective-permute-start.6 = (bf16[2,128,512]{2,1,0:T(8,128)(2,1)S(1)}, bf16[2,128,512]{2,1,0:T(8,128)(2,1)S(1)}, u32[]{:S(2)}, u32[]{:S(2)}) collective-permute-start(bf16[2,128,512]{2,1,0:T(8,128)(2,1)S(1)} %collective-permute-done.4.block), channel_id=1, source_target_pairs={{0,4},{2,6},{4,12},{6,14},{8,0},{10,2},{12,8},{14,10},{1,5},{3,7},... | collective-permute-start | bytes 786440 | tf_op jit(solution)/shard_map/ppermute | solution.py:316
  45.0 17.9 %copy-start.5 = (bf16[2,64]{1,0:T(2,128)(2,1)S(1)}, bf16[2,64]{1,0:T(2,128)(2,1)}, u32[]{:S(2)}) copy-start(bf16[2,64]{1,0:T(2,128)(2,1)} %head.1) | copy-start | bytes 772
  48.7 1.4 %collective-permute-start.9 = (f32[64,512]{1,0:T(8,128)S(1)}, f32[64,512]{1,0:T(8,128)S(1)}, u32[]{:S(2)}, u32[]{:S(2)}) collective-permute-start(f32[64,512]{1,0:T(8,128)S(1)} %get-tuple-element.114), channel_id=1, source_target_pairs={{0,2},{2,0},{4,6},{6,4},{8,10},{10,8},{12,14},{14,12},{1,3},{3,1},... | collective-permute-start | bytes 393224 | tf_op jit(solution)/shard_map/ppermute | solution.py:288
  50.2 4.5 %collective-permute-start.10 = (bf16[64,512]{1,0:T(8,128)(2,1)S(1)}, bf16[64,512]{1,0:T(8,128)(2,1)S(1)}, u32[]{:S(2)}, u32[]{:S(2)}) collective-permute-start(bf16[64,512]{1,0:T(8,128)(2,1)S(1)} %add_convert_fusion.1), channel_id=1, source_target_pairs={{0,1},{1,0},{2,3},{3,2},{4,5},{5,4},{6,7},{7,6},{8,9},{9,8},{10,11... | collective-permute-start | bytes 196616 | tf_op jit(solution)/shard_map/ppermute | solution.py:288
  54.7 1.3 %collective-permute-start.11 = (bf16[80,512]{1,0:T(8,128)(2,1)S(1)}, bf16[80,512]{1,0:T(8,128)(2,1)S(1)}, u32[]{:S(2)}, u32[]{:S(2)}) collective-permute-start(bf16[80,512]{1,0:T(8,128)(2,1)S(1)} %pad_maximum_fusion.1), channel_id=1, source_target_pairs={{0,2},{2,0},{4,6},{6,4},{8,10},{10,8},{12,14},{14,12},{1,3},{3,1},... | collective-permute-start | bytes 245768 | tf_op jit(solution)/shard_map/ppermute | solution.py:288
  56.1 5.4 %collective-permute-start.12 = (bf16[80,1024]{1,0:T(8,128)(2,1)S(1)}, bf16[80,1024]{1,0:T(8,128)(2,1)S(1)}, u32[]{:S(2)}, u32[]{:S(2)}) collective-permute-start(bf16[80,1024]{1,0:T(8,128)(2,1)S(1)} %pad_maximum_fusion.chip_map), channel_id=1, source_target_pairs={{0,4},{1,5},{2,3},{3,2},{4,0},{5,1},{6,10},{7,11},{8,12},{9,13},{1... | collective-permute-start | bytes 491528 | tf_op jit(solution)/shard_map/ppermute | solution.py:306
  61.5 1.4 %collective-permute-start.13 = (bf16[80,1024]{1,0:T(8,128)(2,1)S(1)}, bf16[80,1024]{1,0:T(8,128)(2,1)S(1)}, u32[]{:S(2)}, u32[]{:S(2)}) collective-permute-start(bf16[80,1024]{1,0:T(8,128)(2,1)S(1)} %collective-permute-done.12.near), channel_id=1, source_target_pairs={{0,2},{2,0},{4,6},{6,4},{8,10},{10,8},{12,14},{14,12},{1,3},{3,1},... | collective-permute-start | bytes 491528 | tf_op jit(solution)/shard_map/ppermute | solution.py:288
  66.8 4.2 %collective-permute-start.14 = (bf16[32,896]{1,0:T(8,128)(2,1)S(1)}, bf16[32,896]{1,0:T(8,128)(2,1)S(1)}, u32[]{:S(2)}, u32[]{:S(2)}) collective-permute-start(bf16[32,896]{1,0:T(8,128)(2,1)S(1)} %fusion.14), channel_id=1, source_target_pairs={{0,16},{16,0},{1,17},{17,1},{2,18},{18,2},{3,19},{19,3},{4,20},{20... | collective-permute-start | bytes 172040 | tf_op jit(solution)/shard_map/ppermute | solution.py:294
  71.1 6.7 %collective-permute-start.15 = (bf16[32,896]{1,0:T(8,128)(2,1)S(1)}, bf16[32,896]{1,0:T(8,128)(2,1)S(1)}, u32[]{:S(2)}, u32[]{:S(2)}) collective-permute-start(bf16[32,896]{1,0:T(8,128)(2,1)S(1)} %add_convert_fusion.2), channel_id=1, source_target_pairs={{0,8},{2,10},{4,12},{6,14},{8,0},{10,2},{12,4},{14,6},{1,9},{3,11}... | collective-permute-start | bytes 172040 | tf_op jit(solution)/shard_map/ppermute | solution.py:294
  73.1 6.1 %collective-permute-start.16 = (bf16[32,896]{1,0:T(8,128)(2,1)S(1)}, bf16[32,896]{1,0:T(8,128)(2,1)S(1)}, u32[]{:S(2)}, u32[]{:S(2)}) collective-permute-start(bf16[32,896]{1,0:T(8,128)(2,1)S(1)} %add_convert_fusion.2), channel_id=1, source_target_pairs={{0,4},{2,6},{4,8},{6,10},{8,12},{10,14},{12,0},{14,2},{1,5},{3,7},... | collective-permute-start | bytes 172040 | tf_op jit(solution)/shard_map/ppermute | solution.py:294
  75.1 4.7 %collective-permute-start.17 = (bf16[32,896]{1,0:T(8,128)(2,1)S(1)}, bf16[32,896]{1,0:T(8,128)(2,1)S(1)}, u32[]{:S(2)}, u32[]{:S(2)}) collective-permute-start(bf16[32,896]{1,0:T(8,128)(2,1)S(1)} %add_convert_fusion.2), channel_id=1, source_target_pairs={{0,12},{2,14},{4,0},{6,2},{8,4},{10,6},{12,8},{14,10},{1,13},{3,15... | collective-permute-start | bytes 172040 | tf_op jit(solution)/shard_map/ppermute | solution.py:294
  79.8 1.9 %collective-permute-start.19 = (f32[64,128]{1,0:T(8,128)S(1)}, f32[64,128]{1,0:T(8,128)S(1)}, u32[]{:S(2)}, u32[]{:S(2)}) collective-permute-start(f32[64,128]{1,0:T(8,128)S(1)} %pad_maximum_fusion.2), channel_id=1, source_target_pairs={{0,2},{2,0},{4,6},{6,4},{8,10},{10,8},{12,14},{14,12},{1,3},{3,1},... | collective-permute-start | bytes 98312 | tf_op jit(solution)/shard_map/ppermute | solution.py:288
  79.9 4.9 %collective-permute-start.18 = (f32[32,576]{1,0:T(8,128)S(1)}, f32[32,576]{1,0:T(8,128)S(1)}, u32[]{:S(2)}, u32[]{:S(2)}) collective-permute-start(f32[32,576]{1,0:T(8,128)S(1)} %get-tuple-element.128), channel_id=1, source_target_pairs={{0,1},{1,0},{2,3},{3,2},{4,5},{5,4},{6,7},{7,6},{8,9},{9,8},{10,11... | collective-permute-start | bytes 221192 | tf_op jit(solution)/shard_map/ppermute | solution.py:288
  81.5 3.3 %collective-permute-start.20 = (f32[32,576]{1,0:T(8,128)S(1)}, f32[32,576]{1,0:T(8,128)S(1)}, u32[]{:S(2)}, u32[]{:S(2)}) collective-permute-start(f32[32,576]{1,0:T(8,128)S(1)} %get-tuple-element.128), channel_id=1, source_target_pairs={{0,2},{2,0},{4,6},{6,4},{8,10},{10,8},{12,14},{14,12},{1,3},{3,1},... | collective-permute-start | bytes 221192 | tf_op jit(solution)/shard_map/ppermute | solution.py:288
  84.8 1.3 %collective-permute-start.21 = (f32[32,576]{1,0:T(8,128)S(1)}, f32[32,576]{1,0:T(8,128)S(1)}, u32[]{:S(2)}, u32[]{:S(2)}) collective-permute-start(f32[32,576]{1,0:T(8,128)S(1)} %collective-permute-done.18), channel_id=1, source_target_pairs={{0,2},{2,0},{4,6},{6,4},{8,10},{10,8},{12,14},{14,12},{1,3},{3,1},... | collective-permute-start | bytes 221192 | tf_op jit(solution)/shard_map/ppermute | solution.py:288
where the time goes:
time: 87 us; the launch traced here: 86.9 us
  waiting for transfers between devices  30.9 us (36%)
  starting transfers between devices  24.9 us (29%)
  Pallas kernels  24 us (28%)
  matrix products  2.25 us (3%)
  local copies, waits for them, and re-layouts  1.96 us (2%)
  other arithmetic  1.87 us (2%)
  between operations  0.99 us (1%)
    pallas_call x7, Pallas kernels, absorb(): pl.pallas_call(functools.partial(absorb_kernel, first), out_shape=shapes,...  14.3 us
    ppermute x6, waiting for transfers between devices, round_ring(): lax.ppermute(values, 'tok', [(i, 2 * following[i // 2] + i % 2) for i in...  12.4 us
    ppermute x6, starting transfers between devices, round_ring(): lax.ppermute(values, 'tok', [(i, 2 * following[i // 2] + i % 2) for i in...  11.4 us
    ppermute x11, waiting for transfers between devices, swapped(): return lax.ppermute(values, axis, [(i, i ^ 1) for i in range(size)])  8.69 us
    ppermute x4, starting transfers between devices, passed(): return lax.ppermute(values, axis, pairs)  7.18 us
    ppermute x11, starting transfers between devices, swapped(): return lax.ppermute(values, axis, [(i, i ^ 1) for i in range(size)])  5.67 us
    ppermute x4, waiting for transfers between devices, passed(): return lax.ppermute(values, axis, pairs)  5.07 us
    ppermute x1, waiting for transfers between devices, beside(): return lax.ppermute(values, ('tok', 'col'), pairs)  4.75 us
  transfers between devices with their start and end apart: 22, of which 16 were waited for; matrix products, arithmetic and copies ran while one was open for 3% of the time, Pallas kernels for 19%

commit v1 on v0

--- a/solution.py
+++ b/solution.py
@@ -16,7 +16,6 @@
 SMEM = pl.BlockSpec(memory_space=pltpu.SMEM)
 PARAMS = pltpu.CompilerParams(vmem_limit_bytes=16 * 2**20)
 NT = (((1,), (1,)), ((), ()))
-TN = (((0,), (0,)), ((), ()))
 
 
 def dot(a, b):
@@ -220,7 +219,8 @@
     columns_zero = three_columns(jnp.where(inside(0, row_count), hidden[:channels, :].astype(F32), 0.0), cols)
     first = three_rows(forward[0], columns_zero, cols)
     rows_one = row_count - 2
-    one = jnp.where(inside(1, rows_one), first * jax.nn.sigmoid(first), 0.0)
+    sigmoid_first = jax.nn.sigmoid(first)
+    one = jnp.where(inside(1, rows_one), first * sigmoid_first, 0.0)
     columns_one = three_columns(one, cols)
     second = three_rows(forward[1], columns_one, cols)
     rows_two = row_count - 4
@@ -229,15 +229,14 @@
     holo[...] = dot(head[...], two[:, rim - 2 * cols : rim - 2 * cols + own])
     pieces = hidden[channels:, 2 * cols : cells - 2 * cols].astype(F32)
     cotangent = pieces[:outputs] + pieces[outputs : 2 * outputs] + pieces[2 * outputs : 3 * outputs]
-    grad_two = lax.dot_general(
-        head[...].astype(F32), cotangent, TN, precision=lax.Precision.HIGHEST, preferred_element_type=F32
-    ).astype(BF16)
+    wide_head = head[...].astype(F32).T
+    grad_two = sum(wide_head[:, at : at + 1] * cotangent[at : at + 1, :] for at in range(outputs)).astype(BF16)
     slope = grad_two.astype(F32) * sigmoid_two * (1.0 + second * (1.0 - sigmoid_two))
     pre_grad_two = jnp.where(inside(2, rows_two), slope, 0.0)
     grad_one = three_rows(backward[1], three_columns(pre_grad_two, cols), cols).astype(BF16)
     rows_grad = row_count - 6
     middle = first[:, 2 * cols : 2 * cols + rows_grad * cols]
-    sigmoid_one = jax.nn.sigmoid(middle)
+    sigmoid_one = sigmoid_first[:, 2 * cols : 2 * cols + rows_grad * cols]
     slope = grad_one.astype(F32) * sigmoid_one * (1.0 + middle * (1.0 - sigmoid_one))
     pre_grad_one = jnp.where(inside(3, rows_grad), slope, 0.0)
     grad_zero = three_rows(backward[0], three_columns(pre_grad_one, cols), cols).astype(BF16)
@@ -356,15 +355,17 @@
     queries = (own_queries, swapped(their_queries, "tok"))
     kept = own_keyed.shape[0] * HEAD
 
-    def prepare(conv_weight, out_weight, readout_weight, frame_rows, cotangent):
+    def prepare(conv_weight, out_weight, readout_weight, frame_rows):
         forward, backward = arrange(conv_weight)
         own_out = lax.dynamic_slice_in_dim(out_weight, core * kept, kept, 0)
         folded = lax.dot_general(readout_weight, own_out, (((0,), (1,)), ((), ())), preferred_element_type=F32)
         direct = lax.dot_general(readout_weight, frame_rows, (((0,), (1,)), ((), ())), preferred_element_type=F32)
-        wide_cot = in_order(half, cotangent, swapped(cotangent, "col"), 2)
+        return (forward, backward, folded, direct)
+
+    def exact_rows(other_cot):
+        wide_cot = in_order(half, cotangent, other_cot, 2)
         exact_cot = jnp.concatenate(split3(wide_cot.reshape(wide_cot.shape[0], -1)), axis=0)
-        exact_cot = jnp.pad(exact_cot, ((0, -exact_cot.shape[0] % 16), (0, 0)))
-        return (forward, backward, folded, direct, exact_cot)
+        return jnp.pad(exact_cot, ((0, -exact_cot.shape[0] % 16), (0, 0)))
 
     state, blocks = None, [own_keyed, got_keyed]
     for turn in range(chips):
@@ -376,17 +377,20 @@
             if turn == chips - 1 and at == 1:
                 break
             state = absorb(queries, block, state)
-            if at == 1 and turn == min(1, chips - 2):
-                state, given = lax.optimization_barrier(
-                    (state, (conv_weight, out_weight, readout_weight, frame_rows, cotangent))
+            if at == 0 and turn == chips - 2:
+                state, given, own_cot = lax.optimization_barrier(
+                    (state, (conv_weight, out_weight, readout_weight, frame_rows), cotangent)
                 )
-                prepared = prepare(*given)
+                prepared, other_cot = prepare(*given), swapped(own_cot, "col")
+            if at == 1 and turn == chips - 2:
+                state, other_cot = lax.optimization_barrier((state, other_cot))
+                exact_cot = exact_rows(other_cot)
             if at == 0 and turn == chips - 1:
-                state, prepared = lax.optimization_barrier((state, prepared))
+                state, prepared, exact_cot = lax.optimization_barrier((state, prepared, exact_cot))
             if turn < chips - 2:
                 arriving[at], state = lax.optimization_barrier((arriving[at], state))
         blocks = arriving if turn < chips - 1 else blocks
-    forward, backward, folded, direct, exact_cot = prepared
+    forward, backward, folded, direct = prepared
 
     their_context, their_share = closing(1, queries, blocks[1], state, folded)
     own_context, own_share = closing(0, queries, blocks[1], state, folded)

time: 87 us -> 84.5 us (0.971)
  starting transfers between devices: 24.9 us -> 23 us
    ppermute x11, waiting for transfers between devices: 8.69 us -> 11.3 us  [swapped(): return lax.ppermute(values, axis, [(i, i ^ 1) for i in range(size)])]
    ppermute x6, starting transfers between devices: 11.4 us -> 9.34 us  [round_ring(): lax.ppermute(values, 'tok', [(i, 2 * following[i // 2] + i % 2) for i in...]
    ppermute x6, waiting for transfers between devices: 12.4 us -> 10.4 us  [round_ring(): lax.ppermute(values, 'tok', [(i, 2 * following[i // 2] + i % 2) for i in...]
    ppermute x11, starting transfers between devices: 5.67 us -> 4.52 us  [swapped(): return lax.ppermute(values, axis, [(i, i ^ 1) for i in range(size)])]
  transfers between devices with their start and end apart: 22 -> 22, of which waited for: 16 -> 16; matrix products, arithmetic and copies ran while one was open for 3% -> 4% of each run, Pallas kernels for 19% -> 20%
where the time goes in v1:
time: 84.5 us; the launch traced here: 84.3 us
  waiting for transfers between devices  30.5 us (36%)
  Pallas kernels  23.8 us (28%)
  starting transfers between devices  23 us (27%)
  matrix products  2.25 us (3%)
  local copies, waits for them, and re-layouts  1.96 us (2%)
  other arithmetic  1.87 us (2%)
  between operations  1.01 us (1%)
    pallas_call x7, Pallas kernels, absorb(): pl.pallas_call(functools.partial(absorb_kernel, first), out_shape=shapes,...  14.3 us
    ppermute x11, waiting for transfers between devices, swapped(): return lax.ppermute(values, axis, [(i, i ^ 1) for i in range(size)])  11.3 us
    ppermute x6, waiting for transfers between devices, round_ring(): lax.ppermute(values, 'tok', [(i, 2 * following[i // 2] + i % 2) for i in...  10.4 us
    ppermute x6, starting transfers between devices, round_ring(): lax.ppermute(values, 'tok', [(i, 2 * following[i // 2] + i % 2) for i in...  9.34 us
    ppermute x4, starting transfers between devices, passed(): return lax.ppermute(values, axis, pairs)  7.63 us
    ppermute x4, waiting for transfers between devices, passed(): return lax.ppermute(values, axis, pairs)  4.85 us
    ppermute x11, starting transfers between devices, swapped(): return lax.ppermute(values, axis, [(i, i ^ 1) for i in range(size)])  4.52 us
    ppermute x1, waiting for transfers between devices, beside(): return lax.ppermute(values, ('tok', 'col'), pairs)  3.89 us
  transfers between devices with their start and end apart: 22, of which 16 were waited for; matrix products, arithmetic and copies ran while one was open for 4% of the time, Pallas kernels for 20%

profile of v1, /device:TPU:0, one launch (start us, length us, event | category | flops | bytes accessed | tf_op | source)
XLA Modules:
  0.0 84.3 jit_solution(6648164551768782816)
XLA Ops:
  3.5 1.4 %project.2 = (bf16[2,128,512]{2,1,0:T(8,128)(2,1)S(1)}, bf16[2,128,512]{2,1,0:T(8,128)(2,1)S(1)}) custom-call(s32[4]{0:T(128)S(1)} %pad_add_fusion.place, bf16[512,1024]{1,0:T(8,128)(2,1)S(1)} %normalize.1.normed, bf16[3,1024,256]{2,1,0:T(8,128)(2,1)S(1)} %copy-done.1), custom_call_target="tpu_custom_call" | custom-call | tf_op jit(solution)/shard_map/project/pallas_call | solution.py:69
  5.4 2.6 %collective-permute-start.3 = (bf16[2,128,512]{2,1,0:T(8,128)(2,1)S(1)}, bf16[2,128,512]{2,1,0:T(8,128)(2,1)S(1)}, u32[]{:S(2)}, u32[]{:S(2)}) collective-permute-start(bf16[2,128,512]{2,1,0:T(8,128)(2,1)S(1)} %get-tuple-element.76.block), channel_id=1, source_target_pairs={{0,4},{2,6},{4,12},{6,14},{8,0},{10,2},{12,8},{14,10},{1,5},{3,7},... | collective-permute-start | bytes 786440 | tf_op jit(solution)/shard_map/ppermute | solution.py:315
  8.1 2.6 %collective-permute-start.1 = (bf16[2,128,512]{2,1,0:T(8,128)(2,1)S(1)}, bf16[2,128,512]{2,1,0:T(8,128)(2,1)S(1)}, u32[]{:S(2)}, u32[]{:S(2)}) collective-permute-start(bf16[2,128,512]{2,1,0:T(8,128)(2,1)S(1)} %collective-permute-done.block), channel_id=1, source_target_pairs={{0,4},{2,6},{4,12},{6,14},{8,0},{10,2},{12,8},{14,10},{1,5},{3,7},... | collective-permute-start | bytes 786440 | tf_op jit(solution)/shard_map/ppermute | solution.py:315
  11.8 1.3 %collective-permute-done.2.got.queries = bf16[2,64,512]{2,1,0:T(8,128)(2,1)S(1)} collective-permute-done((bf16[2,64,512]{2,1,0:T(8,128)(2,1)S(1)}, bf16[2,64,512]{2,1,0:T(8,128)(2,1)S(1)}, u32[]{:S(2)}, u32[]{:S(2)}) %collective-permute-start.2) | collective-permute-done | bytes 131104 | tf_op jit(solution)/shard_map/ppermute | solution.py:287
  13.1 2.0 %absorb.7 = (f32[2,80,1024]{2,1,0:T(8,128)S(1)}, f32[2,8,1024]{2,1,0:T(8,128)S(1)}) custom-call(bf16[2,64,512]{2,1,0:T(8,128)(2,1)S(1)} %get-tuple-element.73.own.queries, bf16[2,64,512]{2,1,0:T(8,128)(2,1)S(1)} %collective-permute-done.2.got.queries, bf16[2,128,512]{2,1,0:T(8,128)(2,1)S(1)} %get-tuple-element.76.block), custom_call_target="tpu_custom_call" | custom-call | tf_op jit(solution)/shard_map/absorb/pallas_call | solution.py:115
  17.3 2.1 %absorb.8 = (f32[2,80,1024]{2,1,0:T(8,128)S(1)}, f32[2,8,1024]{2,1,0:T(8,128)S(1)}) custom-call(bf16[2,64,512]{2,1,0:T(8,128)(2,1)S(1)} %get-tuple-element.73.own.queries, bf16[2,64,512]{2,1,0:T(8,128)(2,1)S(1)} %collective-permute-done.2.got.queries, ...), custom_call_target="tpu_custom_call", output_to_operand_aliasing={{0}: (3, {}), {1}: (4, {})} | custom-call | tf_op jit(solution)/shard_map/absorb/pallas_call | solution.py:115
  19.4 2.4 %collective-permute-done.1.block = bf16[2,128,512]{2,1,0:T(8,128)(2,1)S(1)} collective-permute-done((bf16[2,128,512]{2,1,0:T(8,128)(2,1)S(1)}, bf16[2,128,512]{2,1,0:T(8,128)(2,1)S(1)}, u32[]{:S(2)}, u32[]{:S(2)}) %collective-permute-start.1) | collective-permute-done | bytes 262176 | tf_op jit(solution)/shard_map/ppermute | solution.py:315
  23.0 2.0 %absorb.9 = (f32[2,80,1024]{2,1,0:T(8,128)S(1)}, f32[2,8,1024]{2,1,0:T(8,128)S(1)}) custom-call(bf16[2,64,512]{2,1,0:T(8,128)(2,1)S(1)} %get-tuple-element.73.own.queries, bf16[2,64,512]{2,1,0:T(8,128)(2,1)S(1)} %collective-permute-done.2.got.queries, ...), custom_call_target="tpu_custom_call", output_to_operand_aliasing={{0}: (3, {}), {1}: (4, {})} | custom-call | tf_op jit(solution)/shard_map/absorb/pallas_call | solution.py:115
  25.0 2.4 %collective-permute-done.5.block = bf16[2,128,512]{2,1,0:T(8,128)(2,1)S(1)} collective-permute-done((bf16[2,128,512]{2,1,0:T(8,128)(2,1)S(1)}, bf16[2,128,512]{2,1,0:T(8,128)(2,1)S(1)}, u32[]{:S(2)}, u32[]{:S(2)}) %collective-permute-start.5) | collective-permute-done | bytes 262176 | tf_op jit(solution)/shard_map/ppermute | solution.py:315
  28.6 2.1 %absorb.10 = (f32[2,80,1024]{2,1,0:T(8,128)S(1)}, f32[2,8,1024]{2,1,0:T(8,128)S(1)}) custom-call(bf16[2,64,512]{2,1,0:T(8,128)(2,1)S(1)} %get-tuple-element.73.own.queries, bf16[2,64,512]{2,1,0:T(8,128)(2,1)S(1)} %collective-permute-done.2.got.queries, ...), custom_call_target="tpu_custom_call", output_to_operand_aliasing={{0}: (3, {}), {1}: (4, {})} | custom-call | tf_op jit(solution)/shard_map/absorb/pallas_call | solution.py:115
  30.6 2.4 %collective-permute-done.4.block = bf16[2,128,512]{2,1,0:T(8,128)(2,1)S(1)} collective-permute-done((bf16[2,128,512]{2,1,0:T(8,128)(2,1)S(1)}, bf16[2,128,512]{2,1,0:T(8,128)(2,1)S(1)}, u32[]{:S(2)}, u32[]{:S(2)}) %collective-permute-start.4) | collective-permute-done | bytes 262176 | tf_op jit(solution)/shard_map/ppermute | solution.py:315
  33.1 2.1 %absorb.11 = (f32[2,80,1024]{2,1,0:T(8,128)S(1)}, f32[2,8,1024]{2,1,0:T(8,128)S(1)}) custom-call(bf16[2,64,512]{2,1,0:T(8,128)(2,1)S(1)} %get-tuple-element.73.own.queries, bf16[2,64,512]{2,1,0:T(8,128)(2,1)S(1)} %collective-permute-done.2.got.queries, ...), custom_call_target="tpu_custom_call", output_to_operand_aliasing={{0}: (3, {}), {1}: (4, {})} | custom-call | tf_op jit(solution)/shard_map/absorb/pallas_call | solution.py:115
  35.1 1.9 %collective-permute-start.8 = (f32[2,2,128]{2,1,0:T(2,128)S(1)}, f32[2,2,128]{2,1,0:T(2,128)S(1)}, u32[]{:S(2)}, u32[]{:S(2)}) collective-permute-start(f32[2,2,128]{2,1,0:T(2,128)S(1)} %bitcast.29), channel_id=1, source_target_pairs={{0,1},{1,0},{2,3},{3,2},{4,5},{5,4},{6,7},{7,6},{8,9},{9,8},{10,11... | collective-permute-start | bytes 6152 | tf_op jit(solution)/shard_map/ppermute | solution.py:287
  38.7 2.0 %absorb.12 = (f32[2,80,1024]{2,1,0:T(8,128)S(1)}, f32[2,8,1024]{2,1,0:T(8,128)S(1)}) custom-call(bf16[2,64,512]{2,1,0:T(8,128)(2,1)S(1)} %get-tuple-element.73.own.queries, bf16[2,64,512]{2,1,0:T(8,128)(2,1)S(1)} %collective-permute-done.2.got.queries, ...), custom_call_target="tpu_custom_call", output_to_operand_aliasing={{0}: (3, {}), {1}: (4, {})} | custom-call | tf_op jit(solution)/shard_map/absorb/pallas_call | solution.py:115
  40.9 2.0 %absorb.13 = (f32[2,80,1024]{2,1,0:T(8,128)S(1)}, f32[2,8,1024]{2,1,0:T(8,128)S(1)}) custom-call(bf16[2,64,512]{2,1,0:T(8,128)(2,1)S(1)} %get-tuple-element.73.own.queries, bf16[2,64,512]{2,1,0:T(8,128)(2,1)S(1)} %collective-permute-done.2.got.queries, ...), custom_call_target="tpu_custom_call", output_to_operand_aliasing={{0}: (3, {}), {1}: (4, {})} | custom-call | tf_op jit(solution)/shard_map/absorb/pallas_call | solution.py:115
  43.0 2.0 %collective-permute-done.6.block = bf16[2,128,512]{2,1,0:T(8,128)(2,1)S(1)} collective-permute-done((bf16[2,128,512]{2,1,0:T(8,128)(2,1)S(1)}, bf16[2,128,512]{2,1,0:T(8,128)(2,1)S(1)}, u32[]{:S(2)}, u32[]{:S(2)}) %collective-permute-start.6) | collective-permute-done | bytes 262176 | tf_op jit(solution)/shard_map/ppermute | solution.py:315
  44.9 1.3 %closing.3 = (bf16[128,512]{1,0:T(8,128)(2,1)S(1)}, f32[64,512]{1,0:T(8,128)S(1)}) custom-call(bf16[2,64,512]{2,1,0:T(8,128)(2,1)S(1)} %collective-permute-done.2.got.queries, bf16[2,128,512]{2,1,0:T(8,128)(2,1)S(1)} %collective-permute-done.6.block, f32[2,80,1024]{2,1,0:T(8,128)S(1)} %get-tuple-element.116.carried, ...), custom_call_target="tpu_custom_call" | custom-call | tf_op jit(solution)/shard_map/closing/pallas_call | solution.py:138
  46.3 1.3 %closing.2 = (bf16[128,512]{1,0:T(8,128)(2,1)S(1)}, f32[64,512]{1,0:T(8,128)S(1)}) custom-call(bf16[2,64,512]{2,1,0:T(8,128)(2,1)S(1)} %get-tuple-element.73.own.queries, bf16[2,128,512]{2,1,0:T(8,128)(2,1)S(1)} %collective-permute-done.6.block, f32[2,80,1024]{2,1,0:T(8,128)S(1)} %get-tuple-element.116.carried, ...), custom_call_target="tpu_custom_call" | custom-call | tf_op jit(solution)/shard_map/closing/pallas_call | solution.py:138
  48.5 3.7 %collective-permute-done.10 = bf16[64,512]{1,0:T(8,128)(2,1)S(1)} collective-permute-done((bf16[64,512]{1,0:T(8,128)(2,1)S(1)}, bf16[64,512]{1,0:T(8,128)(2,1)S(1)}, u32[]{:S(2)}, u32[]{:S(2)}) %collective-permute-start.10) | collective-permute-done | bytes 65568 | tf_op jit(solution)/shard_map/ppermute | solution.py:287
  52.3 1.3 %collective-permute-done.11 = bf16[80,512]{1,0:T(8,128)(2,1)S(1)} collective-permute-done((bf16[80,512]{1,0:T(8,128)(2,1)S(1)}, bf16[80,512]{1,0:T(8,128)(2,1)S(1)}, u32[]{:S(2)}, u32[]{:S(2)}) %collective-permute-start.11) | collective-permute-done | bytes 81952 | tf_op jit(solution)/shard_map/ppermute | solution.py:287
  53.6 1.5 %collective-permute-start.12 = (bf16[80,1024]{1,0:T(8,128)(2,1)S(1)}, bf16[80,1024]{1,0:T(8,128)(2,1)S(1)}, u32[]{:S(2)}, u32[]{:S(2)}) collective-permute-start(bf16[80,1024]{1,0:T(8,128)(2,1)S(1)} %pad_maximum_fusion.chip_map), channel_id=1, source_target_pairs={{0,4},{1,5},{2,3},{3,2},{4,0},{5,1},{6,10},{7,11},{8,12},{9,13},{1... | collective-permute-start | bytes 491528 | tf_op jit(solution)/shard_map/ppermute | solution.py:305
  55.1 3.9 %collective-permute-done.12.near = bf16[80,1024]{1,0:T(8,128)(2,1)S(1)} collective-permute-done((bf16[80,1024]{1,0:T(8,128)(2,1)S(1)}, bf16[80,1024]{1,0:T(8,128)(2,1)S(1)}, u32[]{:S(2)}, u32[]{:S(2)}) %collective-permute-start.12) | collective-permute-done | bytes 163872 | tf_op jit(solution)/shard_map/ppermute | solution.py:305
  59.0 1.4 %collective-permute-done.13.far = bf16[80,1024]{1,0:T(8,128)(2,1)S(1)} collective-permute-done((bf16[80,1024]{1,0:T(8,128)(2,1)S(1)}, bf16[80,1024]{1,0:T(8,128)(2,1)S(1)}, u32[]{:S(2)}, u32[]{:S(2)}) %collective-permute-start.13) | collective-permute-done | bytes 163872 | tf_op jit(solution)/shard_map/ppermute | solution.py:287
  60.4 3.5 %network.1 = (f32[2,1024]{1,0:T(2,128)S(1)}, f32[32,576]{1,0:T(8,128)S(1)}, f32[64,128]{1,0:T(8,128)S(1)}) custom-call(s32[4]{0:T(128)S(1)} %pad_add_fusion.place, bf16[80,1024]{1,0:T(8,128)(2,1)S(1)} %pad_maximum_fusion.chip_map, bf16[80,1024]{1,0:T(8,128)(2,1)S(1)} %collective-permute-done.12.near, bf16[80,1024]{1,0:T(8,128)(2,1)S(1)} %collective-permute-done.13.far, ...), custom_call_target="tpu_custom_call" | custom-call | tf_op jit(solution)/shard_map/network/pallas_call | solution.py:270
  64.0 1.6 %collective-permute-start.14 = (bf16[32,896]{1,0:T(8,128)(2,1)S(1)}, bf16[32,896]{1,0:T(8,128)(2,1)S(1)}, u32[]{:S(2)}, u32[]{:S(2)}) collective-permute-start(bf16[32,896]{1,0:T(8,128)(2,1)S(1)} %fusion.14), channel_id=1, source_target_pairs={{0,16},{16,0},{1,17},{17,1},{2,18},{18,2},{3,19},{19,3},{4,20},{20... | collective-permute-start | bytes 172040 | tf_op jit(solution)/shard_map/ppermute | solution.py:293
  65.6 2.6 %collective-permute-done.14 = bf16[32,896]{1,0:T(8,128)(2,1)S(1)} collective-permute-done((bf16[32,896]{1,0:T(8,128)(2,1)S(1)}, bf16[32,896]{1,0:T(8,128)(2,1)S(1)}, u32[]{:S(2)}, u32[]{:S(2)}) %collective-permute-start.14) | collective-permute-done | bytes 57376 | tf_op jit(solution)/shard_map/ppermute | solution.py:293
  68.3 2.2 %collective-permute-start.15 = (bf16[32,896]{1,0:T(8,128)(2,1)S(1)}, bf16[32,896]{1,0:T(8,128)(2,1)S(1)}, u32[]{:S(2)}, u32[]{:S(2)}) collective-permute-start(bf16[32,896]{1,0:T(8,128)(2,1)S(1)} %add_convert_fusion.2), channel_id=1, source_target_pairs={{0,8},{2,10},{4,12},{6,14},{8,0},{10,2},{12,4},{14,6},{1,9},{3,11}... | collective-permute-start | bytes 172040 | tf_op jit(solution)/shard_map/ppermute | solution.py:293
  70.5 2.0 %collective-permute-start.16 = (bf16[32,896]{1,0:T(8,128)(2,1)S(1)}, bf16[32,896]{1,0:T(8,128)(2,1)S(1)}, u32[]{:S(2)}, u32[]{:S(2)}) collective-permute-start(bf16[32,896]{1,0:T(8,128)(2,1)S(1)} %add_convert_fusion.2), channel_id=1, source_target_pairs={{0,4},{2,6},{4,8},{6,10},{8,12},{10,14},{12,0},{14,2},{1,5},{3,7},... | collective-permute-start | bytes 172040 | tf_op jit(solution)/shard_map/ppermute | solution.py:293
  72.5 1.8 %collective-permute-start.17 = (bf16[32,896]{1,0:T(8,128)(2,1)S(1)}, bf16[32,896]{1,0:T(8,128)(2,1)S(1)}, u32[]{:S(2)}, u32[]{:S(2)}) collective-permute-start(bf16[32,896]{1,0:T(8,128)(2,1)S(1)} %add_convert_fusion.2), channel_id=1, source_target_pairs={{0,12},{2,14},{4,0},{6,2},{8,4},{10,6},{12,8},{14,10},{1,13},{3,15... | collective-permute-start | bytes 172040 | tf_op jit(solution)/shard_map/ppermute | solution.py:293
  75.0 1.6 %collective-permute-done.16 = bf16[32,896]{1,0:T(8,128)(2,1)S(1)} collective-permute-done((bf16[32,896]{1,0:T(8,128)(2,1)S(1)}, bf16[32,896]{1,0:T(8,128)(2,1)S(1)}, u32[]{:S(2)}, u32[]{:S(2)}) %collective-permute-start.16) | collective-permute-done | bytes 57376 | tf_op jit(solution)/shard_map/ppermute | solution.py:293
  78.5 1.6 %fusion.3 = f32[256,1024]{1,0:T(8,128)} fusion(bf16[1024,64]{0,1:T(8,128)(2,1)S(1)} %copy-done.6, f32[64,128]{1,0:T(8,128)S(1)} %collective-permute-done.19, f32[32,128]{1,0:T(8,128)S(1)} %get-tuple-element.136, f32[32,128]{1,0:T(8,128)S(1)} %get-tuple-element.135, pred[]{:T(512)S(6)} %eq.5), kind=kOutput, calls=%fused_computation.14 | convolution fusion | flops 201408512 | bytes 1245185 | tf_op jit(solution)/shard_map/dot_general | solution.py:428
  80.1 2.1 %collective-permute-done.18 = f32[32,576]{1,0:T(8,128)S(1)} collective-permute-done((f32[32,576]{1,0:T(8,128)S(1)}, f32[32,576]{1,0:T(8,128)S(1)}, u32[]{:S(2)}, u32[]{:S(2)}) %collective-permute-start.18) | collective-permute-done | bytes 73760 | tf_op jit(solution)/shard_map/ppermute | solution.py:287
  (70 shorter events, 16.4 us)
Async XLA Ops:
  0.6 37.6 %copy-start = (bf16[256,1024]{1,0:T(8,128)(2,1)S(1)}, bf16[256,1024]{1,0:T(8,128)(2,1)}, u32[]{:S(2)}) copy-start(bf16[256,1024]{1,0:T(8,128)(2,1)} %param.11) | copy-start | bytes 1572868
  0.6 2.8 %copy-start.1 = (bf16[3,1024,256]{2,1,0:T(8,128)(2,1)S(1)}, bf16[3,1024,256]{2,1,0:T(8,128)(2,1)}, u32[]{:S(2)}) copy-start(bf16[3,1024,256]{2,1,0:T(8,128)(2,1)} %weight.1) | copy-start | bytes 4718596
  1.5 1.2 %copy-start.2 = (bf16[1,512,1024]{2,1,0:T(8,128)(2,1)S(1)}, bf16[1,512,1024]{2,1,0:T(8,128)(2,1)}, u32[]{:S(2)}) copy-start(bf16[1,512,1024]{2,1,0:T(8,128)(2,1)} %param.8) | copy-start | bytes 3145732
  4.9 3.2 %collective-permute-start = (bf16[2,128,512]{2,1,0:T(8,128)(2,1)S(1)}, bf16[2,128,512]{2,1,0:T(8,128)(2,1)S(1)}, u32[]{:S(2)}, u32[]{:S(2)}) collective-permute-start(bf16[2,128,512]{2,1,0:T(8,128)(2,1)S(1)} %get-tuple-element.74), channel_id=1, source_target_pairs={{0,2},{2,0},{4,6},{6,4},{8,10},{10,8},{12,14},{14,12},{1,3},{3,1},... | collective-permute-start | bytes 786440 | tf_op jit(solution)/shard_map/ppermute | solution.py:287
  5.4 10.8 %collective-permute-start.3 = (bf16[2,128,512]{2,1,0:T(8,128)(2,1)S(1)}, bf16[2,128,512]{2,1,0:T(8,128)(2,1)S(1)}, u32[]{:S(2)}, u32[]{:S(2)}) collective-permute-start(bf16[2,128,512]{2,1,0:T(8,128)(2,1)S(1)} %get-tuple-element.76.block), channel_id=1, source_target_pairs={{0,4},{2,6},{4,12},{6,14},{8,0},{10,2},{12,8},{14,10},{1,5},{3,7},... | collective-permute-start | bytes 786440 | tf_op jit(solution)/shard_map/ppermute | solution.py:315
  8.1 13.8 %collective-permute-start.1 = (bf16[2,128,512]{2,1,0:T(8,128)(2,1)S(1)}, bf16[2,128,512]{2,1,0:T(8,128)(2,1)S(1)}, u32[]{:S(2)}, u32[]{:S(2)}) collective-permute-start(bf16[2,128,512]{2,1,0:T(8,128)(2,1)S(1)} %collective-permute-done.block), channel_id=1, source_target_pairs={{0,4},{2,6},{4,12},{6,14},{8,0},{10,2},{12,8},{14,10},{1,5},{3,7},... | collective-permute-start | bytes 786440 | tf_op jit(solution)/shard_map/ppermute | solution.py:315
  11.7 1.4 %collective-permute-start.2 = (bf16[2,64,512]{2,1,0:T(8,128)(2,1)S(1)}, bf16[2,64,512]{2,1,0:T(8,128)(2,1)S(1)}, u32[]{:S(2)}, u32[]{:S(2)}) collective-permute-start(bf16[2,64,512]{2,1,0:T(8,128)(2,1)S(1)} %get-tuple-element.75), channel_id=1, source_target_pairs={{0,2},{2,0},{4,6},{6,4},{8,10},{10,8},{12,14},{14,12},{1,3},{3,1},... | collective-permute-start | bytes 393224 | tf_op jit(solution)/shard_map/ppermute | solution.py:287
  16.2 11.2 %collective-permute-start.5 = (bf16[2,128,512]{2,1,0:T(8,128)(2,1)S(1)}, bf16[2,128,512]{2,1,0:T(8,128)(2,1)S(1)}, u32[]{:S(2)}, u32[]{:S(2)}) collective-permute-start(bf16[2,128,512]{2,1,0:T(8,128)(2,1)S(1)} %collective-permute-done.3.block), channel_id=1, source_target_pairs={{0,4},{2,6},{4,12},{6,14},{8,0},{10,2},{12,8},{14,10},{1,5},{3,7},... | collective-permute-start | bytes 786440 | tf_op jit(solution)/shard_map/ppermute | solution.py:315
  21.8 11.2 %collective-permute-start.4 = (bf16[2,128,512]{2,1,0:T(8,128)(2,1)S(1)}, bf16[2,128,512]{2,1,0:T(8,128)(2,1)S(1)}, u32[]{:S(2)}, u32[]{:S(2)}) collective-permute-start(bf16[2,128,512]{2,1,0:T(8,128)(2,1)S(1)} %collective-permute-done.1.block), channel_id=1, source_target_pairs={{0,4},{2,6},{4,12},{6,14},{8,0},{10,2},{12,8},{14,10},{1,5},{3,7},... | collective-permute-start | bytes 786440 | tf_op jit(solution)/shard_map/ppermute | solution.py:315
  23.0 12.2 %copy-start.7 = (f32[1,2,2,128]{3,2,1,0:T(2,128)S(1)}, f32[1,2,2,128]{3,2,1,0:T(2,128)}, u32[]{:S(2)}) copy-start(f32[1,2,2,128]{3,2,1,0:T(2,128)} %param.15) | copy-start | bytes 6148
  23.0 14.9 %copy-start.3 = (bf16[1,512,1024]{2,1,0:T(8,128)(2,1)S(1)}, bf16[1,512,1024]{2,1,0:T(8,128)(2,1)}, u32[]{:S(2)}) copy-start(bf16[1,512,1024]{2,1,0:T(8,128)(2,1)} %param.8) | copy-start | bytes 3145732
  23.0 14.9 %copy-start.6 = (bf16[1024,64]{0,1:T(8,128)(2,1)S(1)}, bf16[1024,64]{0,1:T(8,128)(2,1)}, u32[]{:S(2)}) copy-start(bf16[1024,64]{0,1:T(8,128)(2,1)} %param.12) | copy-start | bytes 393220
  27.5 13.4 %collective-permute-start.7 = (bf16[2,128,512]{2,1,0:T(8,128)(2,1)S(1)}, bf16[2,128,512]{2,1,0:T(8,128)(2,1)S(1)}, u32[]{:S(2)}, u32[]{:S(2)}) collective-permute-start(bf16[2,128,512]{2,1,0:T(8,128)(2,1)S(1)} %collective-permute-done.5.block), channel_id=1, source_target_pairs={{0,4},{2,6},{4,12},{6,14},{8,0},{10,2},{12,8},{14,10},{1,5},{3,7},... | collective-permute-start | bytes 786440 | tf_op jit(solution)/shard_map/ppermute | solution.py:315
  30.6 7.9 %copy-start.4 = (bf16[2,64,576]{2,1,0:T(8,128)(2,1)S(1)}, bf16[2,64,576]{2,1,0:T(8,128)(2,1)}, u32[]{:S(2)}) copy-start(bf16[2,64,576]{2,1,0:T(8,128)(2,1)} %weight.2) | copy-start | bytes 442372
  35.1 5.7 %collective-permute-start.8 = (f32[2,2,128]{2,1,0:T(2,128)S(1)}, f32[2,2,128]{2,1,0:T(2,128)S(1)}, u32[]{:S(2)}, u32[]{:S(2)}) collective-permute-start(f32[2,2,128]{2,1,0:T(2,128)S(1)} %bitcast.29), channel_id=1, source_target_pairs={{0,1},{1,0},{2,3},{3,2},{4,5},{5,4},{6,7},{7,6},{8,9},{9,8},{10,11... | collective-permute-start | bytes 6152 | tf_op jit(solution)/shard_map/ppermute | solution.py:287
  37.0 7.9 %collective-permute-start.6 = (bf16[2,128,512]{2,1,0:T(8,128)(2,1)S(1)}, bf16[2,128,512]{2,1,0:T(8,128)(2,1)S(1)}, u32[]{:S(2)}, u32[]{:S(2)}) collective-permute-start(bf16[2,128,512]{2,1,0:T(8,128)(2,1)S(1)} %collective-permute-done.4.block), channel_id=1, source_target_pairs={{0,4},{2,6},{4,12},{6,14},{8,0},{10,2},{12,8},{14,10},{1,5},{3,7},... | collective-permute-start | bytes 786440 | tf_op jit(solution)/shard_map/ppermute | solution.py:315
  43.0 17.4 %copy-start.5 = (bf16[2,64]{1,0:T(2,128)(2,1)S(1)}, bf16[2,64]{1,0:T(2,128)(2,1)}, u32[]{:S(2)}) copy-start(bf16[2,64]{1,0:T(2,128)(2,1)} %head.1) | copy-start | bytes 772
  46.2 1.4 %collective-permute-start.9 = (f32[64,512]{1,0:T(8,128)S(1)}, f32[64,512]{1,0:T(8,128)S(1)}, u32[]{:S(2)}, u32[]{:S(2)}) collective-permute-start(f32[64,512]{1,0:T(8,128)S(1)} %get-tuple-element.120), channel_id=1, source_target_pairs={{0,2},{2,0},{4,6},{6,4},{8,10},{10,8},{12,14},{14,12},{1,3},{3,1},... | collective-permute-start | bytes 393224 | tf_op jit(solution)/shard_map/ppermute | solution.py:287
  47.7 4.5 %collective-permute-start.10 = (bf16[64,512]{1,0:T(8,128)(2,1)S(1)}, bf16[64,512]{1,0:T(8,128)(2,1)S(1)}, u32[]{:S(2)}, u32[]{:S(2)}) collective-permute-start(bf16[64,512]{1,0:T(8,128)(2,1)S(1)} %add_convert_fusion.1), channel_id=1, source_target_pairs={{0,1},{1,0},{2,3},{3,2},{4,5},{5,4},{6,7},{7,6},{8,9},{9,8},{10,11... | collective-permute-start | bytes 196616 | tf_op jit(solution)/shard_map/ppermute | solution.py:287
  52.2 1.3 %collective-permute-start.11 = (bf16[80,512]{1,0:T(8,128)(2,1)S(1)}, bf16[80,512]{1,0:T(8,128)(2,1)S(1)}, u32[]{:S(2)}, u32[]{:S(2)}) collective-permute-start(bf16[80,512]{1,0:T(8,128)(2,1)S(1)} %pad_maximum_fusion.1), channel_id=1, source_target_pairs={{0,2},{2,0},{4,6},{6,4},{8,10},{10,8},{12,14},{14,12},{1,3},{3,1},... | collective-permute-start | bytes 245768 | tf_op jit(solution)/shard_map/ppermute | solution.py:287
  53.6 5.4 %collective-permute-start.12 = (bf16[80,1024]{1,0:T(8,128)(2,1)S(1)}, bf16[80,1024]{1,0:T(8,128)(2,1)S(1)}, u32[]{:S(2)}, u32[]{:S(2)}) collective-permute-start(bf16[80,1024]{1,0:T(8,128)(2,1)S(1)} %pad_maximum_fusion.chip_map), channel_id=1, source_target_pairs={{0,4},{1,5},{2,3},{3,2},{4,0},{5,1},{6,10},{7,11},{8,12},{9,13},{1... | collective-permute-start | bytes 491528 | tf_op jit(solution)/shard_map/ppermute | solution.py:305
  59.0 1.4 %collective-permute-start.13 = (bf16[80,1024]{1,0:T(8,128)(2,1)S(1)}, bf16[80,1024]{1,0:T(8,128)(2,1)S(1)}, u32[]{:S(2)}, u32[]{:S(2)}) collective-permute-start(bf16[80,1024]{1,0:T(8,128)(2,1)S(1)} %collective-permute-done.12.near), channel_id=1, source_target_pairs={{0,2},{2,0},{4,6},{6,4},{8,10},{10,8},{12,14},{14,12},{1,3},{3,1},... | collective-permute-start | bytes 491528 | tf_op jit(solution)/shard_map/ppermute | solution.py:287
  64.0 4.2 %collective-permute-start.14 = (bf16[32,896]{1,0:T(8,128)(2,1)S(1)}, bf16[32,896]{1,0:T(8,128)(2,1)S(1)}, u32[]{:S(2)}, u32[]{:S(2)}) collective-permute-start(bf16[32,896]{1,0:T(8,128)(2,1)S(1)} %fusion.14), channel_id=1, source_target_pairs={{0,16},{16,0},{1,17},{17,1},{2,18},{18,2},{3,19},{19,3},{4,20},{20... | collective-permute-start | bytes 172040 | tf_op jit(solution)/shard_map/ppermute | solution.py:293
  68.3 6.7 %collective-permute-start.15 = (bf16[32,896]{1,0:T(8,128)(2,1)S(1)}, bf16[32,896]{1,0:T(8,128)(2,1)S(1)}, u32[]{:S(2)}, u32[]{:S(2)}) collective-permute-start(bf16[32,896]{1,0:T(8,128)(2,1)S(1)} %add_convert_fusion.2), channel_id=1, source_target_pairs={{0,8},{2,10},{4,12},{6,14},{8,0},{10,2},{12,4},{14,6},{1,9},{3,11}... | collective-permute-start | bytes 172040 | tf_op jit(solution)/shard_map/ppermute | solution.py:293
  70.5 6.1 %collective-permute-start.16 = (bf16[32,896]{1,0:T(8,128)(2,1)S(1)}, bf16[32,896]{1,0:T(8,128)(2,1)S(1)}, u32[]{:S(2)}, u32[]{:S(2)}) collective-permute-start(bf16[32,896]{1,0:T(8,128)(2,1)S(1)} %add_convert_fusion.2), channel_id=1, source_target_pairs={{0,4},{2,6},{4,8},{6,10},{8,12},{10,14},{12,0},{14,2},{1,5},{3,7},... | collective-permute-start | bytes 172040 | tf_op jit(solution)/shard_map/ppermute | solution.py:293
  72.5 4.7 %collective-permute-start.17 = (bf16[32,896]{1,0:T(8,128)(2,1)S(1)}, bf16[32,896]{1,0:T(8,128)(2,1)S(1)}, u32[]{:S(2)}, u32[]{:S(2)}) collective-permute-start(bf16[32,896]{1,0:T(8,128)(2,1)S(1)} %add_convert_fusion.2), channel_id=1, source_target_pairs={{0,12},{2,14},{4,0},{6,2},{8,4},{10,6},{12,8},{14,10},{1,13},{3,15... | collective-permute-start | bytes 172040 | tf_op jit(solution)/shard_map/ppermute | solution.py:293
  77.2 1.3 %collective-permute-start.19 = (f32[64,128]{1,0:T(8,128)S(1)}, f32[64,128]{1,0:T(8,128)S(1)}, u32[]{:S(2)}, u32[]{:S(2)}) collective-permute-start(f32[64,128]{1,0:T(8,128)S(1)} %pad_maximum_fusion.2), channel_id=1, source_target_pairs={{0,2},{2,0},{4,6},{6,4},{8,10},{10,8},{12,14},{14,12},{1,3},{3,1},... | collective-permute-start | bytes 98312 | tf_op jit(solution)/shard_map/ppermute | solution.py:287
  77.3 4.9 %collective-permute-start.18 = (f32[32,576]{1,0:T(8,128)S(1)}, f32[32,576]{1,0:T(8,128)S(1)}, u32[]{:S(2)}, u32[]{:S(2)}) collective-permute-start(f32[32,576]{1,0:T(8,128)S(1)} %get-tuple-element.134), channel_id=1, source_target_pairs={{0,1},{1,0},{2,3},{3,2},{4,5},{5,4},{6,7},{7,6},{8,9},{9,8},{10,11... | collective-permute-start | bytes 221192 | tf_op jit(solution)/shard_map/ppermute | solution.py:287
  78.1 4.2 %collective-permute-start.20 = (f32[32,576]{1,0:T(8,128)S(1)}, f32[32,576]{1,0:T(8,128)S(1)}, u32[]{:S(2)}, u32[]{:S(2)}) collective-permute-start(f32[32,576]{1,0:T(8,128)S(1)} %get-tuple-element.134), channel_id=1, source_target_pairs={{0,2},{2,0},{4,6},{6,4},{8,10},{10,8},{12,14},{14,12},{1,3},{3,1},... | collective-permute-start | bytes 221192 | tf_op jit(solution)/shard_map/ppermute | solution.py:287
  82.2 1.3 %collective-permute-start.21 = (f32[32,576]{1,0:T(8,128)S(1)}, f32[32,576]{1,0:T(8,128)S(1)}, u32[]{:S(2)}, u32[]{:S(2)}) collective-permute-start(f32[32,576]{1,0:T(8,128)S(1)} %collective-permute-done.18), channel_id=1, source_target_pairs={{0,2},{2,0},{4,6},{6,4},{8,10},{10,8},{12,14},{14,12},{1,3},{3,1},... | collective-permute-start | bytes 221192 | tf_op jit(solution)/shard_map/ppermute | solution.py:287

commit v2 on v1

--- a/solution.py
+++ b/solution.py
@@ -30,30 +30,41 @@
     return high, mid, low
 
 
-def normalize_kernel(tokens, gain, normed):
-    values = tokens[...].astype(F32)
-    center = values - jnp.mean(values, axis=-1, keepdims=True)
-    spread = jnp.mean(center * center, axis=-1, keepdims=True)
-    normed[...] = (center * lax.rsqrt(spread + EPSILON) * gain[...]).astype(BF16)
-
-
-def normalize(tokens, gain):
-    return pl.pallas_call(
-        normalize_kernel,
-        out_shape=jax.ShapeDtypeStruct(tokens.shape, BF16),
-        in_specs=[VMEM, VMEM],
-        out_specs=VMEM,
-        compiler_params=PARAMS,
-        name="normalize",
-    )(tokens, gain)
-
-
-def project_kernel(members, place, normed, weight, mine, theirs, turned):
+def project_kernel(members, raw, place, rows, *refs):
+    if raw:
+        gain, weight, normed, mine, theirs, parts, turned, sems, taken, wide_gain, row_sems = refs
+        pieces = row_sems.shape[0] - 1
+        size = taken.shape[0] // pieces
+        row_copies = [pltpu.make_async_copy(gain, wide_gain, row_sems.at[pieces])] + [
+            pltpu.make_async_copy(
+                rows.at[pl.ds(at * size, size)], taken.at[pl.ds(at * size, size)], row_sems.at[at]
+            )
+            for at in range(pieces)
+        ]
+        for copy in row_copies:
+            copy.start()
+    else:
+        weight, mine, theirs, parts, turned, sems = refs
+    copies = [
+        pltpu.make_async_copy(weight.at[member], parts.at[at], sems.at[at]) for at, member in enumerate(members)
+    ]
+    for copy in copies:
+        copy.start()
+    if raw:
+        row_copies[0].wait()
+        for at in range(pieces):
+            row_copies[at + 1].wait()
+            values = taken[at * size : (at + 1) * size, :].astype(F32)
+            center = values - jnp.mean(values, axis=-1, keepdims=True)
+            spread = jnp.mean(center * center, axis=-1, keepdims=True)
+            scaled = center * lax.rsqrt(spread + EPSILON) * wide_gain[...].astype(F32)[None, :]
+            normed[at * size : (at + 1) * size, :] = scaled.astype(BF16)
+        rows = normed
     core = place[0]
     kept = mine.shape[0] * HEAD
-    rows = normed[...]
     for at, member in enumerate(members):
-        product = dot(rows, weight[member]).astype(BF16)
+        copies[at].wait()
+        product = dot(rows[...], parts[at]).astype(BF16)
         if member == 0:
             product = product * jnp.asarray(1.0 / HEAD**0.5, BF16)
         turned[at] = product.T
@@ -63,18 +74,30 @@
                 out[head, at * HEAD : (at + 1) * HEAD, :] = turned[at, pl.ds(start, HEAD), :]
 
 
-def project(members, place, normed, weight):
-    count, length = weight.shape[2] // HEAD // 2, normed.shape[0]
-    shape = jax.ShapeDtypeStruct((count, len(members) * HEAD, length), BF16)
+def project(members, place, rows, weight, gain=None):
+    length, width = rows.shape[0], weight.shape[2]
+    shape = jax.ShapeDtypeStruct((width // HEAD // 2, len(members) * HEAD, length), BF16)
+    raw = gain is not None
+    far = pl.BlockSpec(memory_space=pltpu.HBM)
+    pieces = 4 if length % 64 == 0 else 1
     return pl.pallas_call(
-        functools.partial(project_kernel, members),
-        out_shape=(shape, shape),
-        in_specs=[SMEM, VMEM, VMEM],
-        out_specs=(VMEM,) * 2,
-        scratch_shapes=[pltpu.VMEM((len(members), weight.shape[2], length), BF16)],
+        functools.partial(project_kernel, members, raw),
+        out_shape=((jax.ShapeDtypeStruct(rows.shape, BF16),) if raw else ()) + (shape, shape),
+        in_specs=[SMEM] + ([far, far] if raw else [VMEM]) + [far],
+        out_specs=(VMEM,) * (2 + raw),
+        scratch_shapes=[
+            pltpu.VMEM((len(members),) + weight.shape[1:], BF16),
+            pltpu.VMEM((len(members), width, length), BF16),
+            pltpu.SemaphoreType.DMA((len(members),)),
+        ]
+        + (
+            [pltpu.VMEM(rows.shape, BF16), pltpu.VMEM(gain.shape, BF16), pltpu.SemaphoreType.DMA((pieces + 1,))]
+            if raw
+            else []
+        ),
         compiler_params=PARAMS,
         name="project",
-    )(place, normed, weight)
+    )(place, rows, *((gain,) if raw else ()), weight)
 
 
 def attend(queries, block, running, best):
@@ -344,12 +367,10 @@
     place = jnp.stack([core, half, chip_row, lax.rem(tok_at // 2, 2)]).astype(jnp.int32)
     cols = cols_dev * col_count
 
-    gain, qkv_weight, out_weight = lax.optimization_barrier(
-        (ln_gain.astype(F32).reshape(1, -1), qkv_weight, out_weight)
-    )
-    normed = normalize(frame_rows, gain)
-    own_keyed, their_keyed = project((1, 2), place, normed, qkv_weight)
-    own_keyed, their_keyed, normed = lax.optimization_barrier((own_keyed, their_keyed, normed))
+    qkv_weight, far_rows, far_gain = (
+        pltpu.with_memory_space_constraint(array, pltpu.HBM) for array in (qkv_weight, frame_rows, ln_gain)
+    )
+    normed, own_keyed, their_keyed = project((1, 2), place, far_rows, qkv_weight, far_gain)
     got_keyed = swapped(their_keyed, "tok")
     own_queries, their_queries = project((0,), place, normed, qkv_weight)
     queries = (own_queries, swapped(their_queries, "tok"))

time: 84.5 us -> 84.4 us (level)
  Pallas kernels: 23.8 us -> 26.8 us
  waiting for transfers between devices: 30.5 us -> 29.1 us
  local copies, waits for them, and re-layouts: 1.96 us -> 0.73 us
    pallas_call x3 -> x2, Pallas kernels: 3.09 us -> 6.17 us  [project(): pl.pallas_call(functools.partial(project_kernel, members, raw), out_shape...]
    ppermute x6, waiting for transfers between devices: 10.4 us -> 8.97 us  [round_ring(): lax.ppermute(values, 'tok', [(i, 2 * following[i // 2] + i % 2) for i in...]
    unnamed x17 -> x13, local copies, waits for them, and re-layouts: 1.27 us -> 0.04 us
  transfers between devices with their start and end apart: 22 -> 22, of which waited for: 16 -> 16; matrix products, arithmetic and copies ran while one was open for 4% -> 4% of each run, Pallas kernels for 20% -> 21%
where the time goes in v2:
time: 84.4 us; the launch traced here: 84.2 us
  waiting for transfers between devices  29.1 us (34%)
  Pallas kernels  26.8 us (32%)
  starting transfers between devices  23.3 us (28%)
  matrix products  2.26 us (3%)
  other arithmetic  1.04 us (1%)
  between operations  1 us (1%)
    pallas_call x7, Pallas kernels, absorb(): pl.pallas_call(functools.partial(absorb_kernel, first), out_shape=shapes,...  14.3 us
    ppermute x11, waiting for transfers between devices, swapped(): return lax.ppermute(values, axis, [(i, i ^ 1) for i in range(size)])  11.4 us
    ppermute x6, starting transfers between devices, round_ring(): lax.ppermute(values, 'tok', [(i, 2 * following[i // 2] + i % 2) for i in...  9.7 us
    ppermute x6, waiting for transfers between devices, round_ring(): lax.ppermute(values, 'tok', [(i, 2 * following[i // 2] + i % 2) for i in...  8.97 us
    ppermute x4, starting transfers between devices, passed(): return lax.ppermute(values, axis, pairs)  7.6 us
    pallas_call x2, Pallas kernels, project(): pl.pallas_call(functools.partial(project_kernel, members, raw), out_shape...  6.17 us
    ppermute x4, waiting for transfers between devices, passed(): return lax.ppermute(values, axis, pairs)  4.86 us
    ppermute x11, starting transfers between devices, swapped(): return lax.ppermute(values, axis, [(i, i ^ 1) for i in range(size)])  4.51 us
  transfers between devices with their start and end apart: 22, of which 16 were waited for; matrix products, arithmetic and copies ran while one was open for 4% of the time, Pallas kernels for 21%

profile of v2, /device:TPU:0, one launch (start us, length us, event | category | flops | bytes accessed | tf_op | source)
XLA Modules:
  0.0 84.2 jit_solution(14875302731972186774)
XLA Ops:
  0.7 4.1 %project.2 = (bf16[512,1024]{1,0:T(8,128)(2,1)S(1)}, bf16[2,128,512]{2,1,0:T(8,128)(2,1)S(1)}, bf16[2,128,512]{2,1,0:T(8,128)(2,1)S(1)}) custom-call(s32[4]{0:T(128)S(1)} %pad_add_fusion.place, bf16[512,1024]{1,0:T(8,128)(2,1)} %bitcast.20, bf16[1024]{0:T(1024)(128)(2,1)} %refs_0_.2, bf16[3,1024,256]{2,1,0:T(8,128)(2,1)} %refs_0_.3), custom_call_target="tpu_custom_call" | custom-call | tf_op jit(solution)/shard_map/project/pallas_call | solution.py:83
  5.4 2.6 %collective-permute-start.3 = (bf16[2,128,512]{2,1,0:T(8,128)(2,1)S(1)}, bf16[2,128,512]{2,1,0:T(8,128)(2,1)S(1)}, u32[]{:S(2)}, u32[]{:S(2)}) collective-permute-start(bf16[2,128,512]{2,1,0:T(8,128)(2,1)S(1)} %get-tuple-element.67.block), channel_id=1, source_target_pairs={{0,4},{2,6},{4,12},{6,14},{8,0},{10,2},{12,8},{14,10},{1,5},{3,7},... | collective-permute-start | bytes 786440 | tf_op jit(solution)/shard_map/ppermute | solution.py:338
  8.0 2.6 %collective-permute-start.1 = (bf16[2,128,512]{2,1,0:T(8,128)(2,1)S(1)}, bf16[2,128,512]{2,1,0:T(8,128)(2,1)S(1)}, u32[]{:S(2)}, u32[]{:S(2)}) collective-permute-start(bf16[2,128,512]{2,1,0:T(8,128)(2,1)S(1)} %collective-permute-done.block), channel_id=1, source_target_pairs={{0,4},{2,6},{4,12},{6,14},{8,0},{10,2},{12,8},{14,10},{1,5},{3,7},... | collective-permute-start | bytes 786440 | tf_op jit(solution)/shard_map/ppermute | solution.py:338
  10.6 2.1 %project.3 = (bf16[2,64,512]{2,1,0:T(8,128)(2,1)S(1)}, bf16[2,64,512]{2,1,0:T(8,128)(2,1)S(1)}) custom-call(s32[4]{0:T(128)S(1)} %pad_add_fusion.place, bf16[512,1024]{1,0:T(8,128)(2,1)S(1)} %get-tuple-element.63.rows, bf16[3,1024,256]{2,1,0:T(8,128)(2,1)} %refs_0_.3), custom_call_target="tpu_custom_call" | custom-call | tf_op jit(solution)/shard_map/project/pallas_call | solution.py:83
  12.8 1.3 %collective-permute-done.2.got.queries = bf16[2,64,512]{2,1,0:T(8,128)(2,1)S(1)} collective-permute-done((bf16[2,64,512]{2,1,0:T(8,128)(2,1)S(1)}, bf16[2,64,512]{2,1,0:T(8,128)(2,1)S(1)}, u32[]{:S(2)}, u32[]{:S(2)}) %collective-permute-start.2) | collective-permute-done | bytes 131104 | tf_op jit(solution)/shard_map/ppermute | solution.py:310
  14.1 2.0 %absorb.7 = (f32[2,80,1024]{2,1,0:T(8,128)S(1)}, f32[2,8,1024]{2,1,0:T(8,128)S(1)}) custom-call(bf16[2,64,512]{2,1,0:T(8,128)(2,1)S(1)} %get-tuple-element.64.own.queries, bf16[2,64,512]{2,1,0:T(8,128)(2,1)S(1)} %collective-permute-done.2.got.queries, bf16[2,128,512]{2,1,0:T(8,128)(2,1)S(1)} %get-tuple-element.67.block), custom_call_target="tpu_custom_call" | custom-call | tf_op jit(solution)/shard_map/absorb/pallas_call | solution.py:138
  16.2 1.5 %collective-permute-start.5 = (bf16[2,128,512]{2,1,0:T(8,128)(2,1)S(1)}, bf16[2,128,512]{2,1,0:T(8,128)(2,1)S(1)}, u32[]{:S(2)}, u32[]{:S(2)}) collective-permute-start(bf16[2,128,512]{2,1,0:T(8,128)(2,1)S(1)} %collective-permute-done.3.block), channel_id=1, source_target_pairs={{0,4},{2,6},{4,12},{6,14},{8,0},{10,2},{12,8},{14,10},{1,5},{3,7},... | collective-permute-start | bytes 786440 | tf_op jit(solution)/shard_map/ppermute | solution.py:338
  17.7 2.1 %absorb.8 = (f32[2,80,1024]{2,1,0:T(8,128)S(1)}, f32[2,8,1024]{2,1,0:T(8,128)S(1)}) custom-call(bf16[2,64,512]{2,1,0:T(8,128)(2,1)S(1)} %get-tuple-element.64.own.queries, bf16[2,64,512]{2,1,0:T(8,128)(2,1)S(1)} %collective-permute-done.2.got.queries, ...), custom_call_target="tpu_custom_call", output_to_operand_aliasing={{0}: (3, {}), {1}: (4, {})} | custom-call | tf_op jit(solution)/shard_map/absorb/pallas_call | solution.py:138
  19.7 2.1 %collective-permute-done.1.block = bf16[2,128,512]{2,1,0:T(8,128)(2,1)S(1)} collective-permute-done((bf16[2,128,512]{2,1,0:T(8,128)(2,1)S(1)}, bf16[2,128,512]{2,1,0:T(8,128)(2,1)S(1)}, u32[]{:S(2)}, u32[]{:S(2)}) %collective-permute-start.1) | collective-permute-done | bytes 262176 | tf_op jit(solution)/shard_map/ppermute | solution.py:338
  22.9 2.0 %absorb.9 = (f32[2,80,1024]{2,1,0:T(8,128)S(1)}, f32[2,8,1024]{2,1,0:T(8,128)S(1)}) custom-call(bf16[2,64,512]{2,1,0:T(8,128)(2,1)S(1)} %get-tuple-element.64.own.queries, bf16[2,64,512]{2,1,0:T(8,128)(2,1)S(1)} %collective-permute-done.2.got.queries, ...), custom_call_target="tpu_custom_call", output_to_operand_aliasing={{0}: (3, {}), {1}: (4, {})} | custom-call | tf_op jit(solution)/shard_map/absorb/pallas_call | solution.py:138
  25.0 2.4 %collective-permute-done.5.block = bf16[2,128,512]{2,1,0:T(8,128)(2,1)S(1)} collective-permute-done((bf16[2,128,512]{2,1,0:T(8,128)(2,1)S(1)}, bf16[2,128,512]{2,1,0:T(8,128)(2,1)S(1)}, u32[]{:S(2)}, u32[]{:S(2)}) %collective-permute-start.5) | collective-permute-done | bytes 262176 | tf_op jit(solution)/shard_map/ppermute | solution.py:338
  28.5 2.0 %absorb.10 = (f32[2,80,1024]{2,1,0:T(8,128)S(1)}, f32[2,8,1024]{2,1,0:T(8,128)S(1)}) custom-call(bf16[2,64,512]{2,1,0:T(8,128)(2,1)S(1)} %get-tuple-element.64.own.queries, bf16[2,64,512]{2,1,0:T(8,128)(2,1)S(1)} %collective-permute-done.2.got.queries, ...), custom_call_target="tpu_custom_call", output_to_operand_aliasing={{0}: (3, {}), {1}: (4, {})} | custom-call | tf_op jit(solution)/shard_map/absorb/pallas_call | solution.py:138
  30.6 2.4 %collective-permute-done.4.block = bf16[2,128,512]{2,1,0:T(8,128)(2,1)S(1)} collective-permute-done((bf16[2,128,512]{2,1,0:T(8,128)(2,1)S(1)}, bf16[2,128,512]{2,1,0:T(8,128)(2,1)S(1)}, u32[]{:S(2)}, u32[]{:S(2)}) %collective-permute-start.4) | collective-permute-done | bytes 262176 | tf_op jit(solution)/shard_map/ppermute | solution.py:338
  33.0 2.0 %absorb.11 = (f32[2,80,1024]{2,1,0:T(8,128)S(1)}, f32[2,8,1024]{2,1,0:T(8,128)S(1)}) custom-call(bf16[2,64,512]{2,1,0:T(8,128)(2,1)S(1)} %get-tuple-element.64.own.queries, bf16[2,64,512]{2,1,0:T(8,128)(2,1)S(1)} %collective-permute-done.2.got.queries, ...), custom_call_target="tpu_custom_call", output_to_operand_aliasing={{0}: (3, {}), {1}: (4, {})} | custom-call | tf_op jit(solution)/shard_map/absorb/pallas_call | solution.py:138
  35.1 1.9 %collective-permute-start.8 = (f32[2,2,128]{2,1,0:T(2,128)S(1)}, f32[2,2,128]{2,1,0:T(2,128)S(1)}, u32[]{:S(2)}, u32[]{:S(2)}) collective-permute-start(f32[2,2,128]{2,1,0:T(2,128)S(1)} %bitcast.27), channel_id=1, source_target_pairs={{0,1},{1,0},{2,3},{3,2},{4,5},{5,4},{6,7},{7,6},{8,9},{9,8},{10,11... | collective-permute-start | bytes 6152 | tf_op jit(solution)/shard_map/ppermute | solution.py:310
  38.7 2.1 %absorb.12 = (f32[2,80,1024]{2,1,0:T(8,128)S(1)}, f32[2,8,1024]{2,1,0:T(8,128)S(1)}) custom-call(bf16[2,64,512]{2,1,0:T(8,128)(2,1)S(1)} %get-tuple-element.64.own.queries, bf16[2,64,512]{2,1,0:T(8,128)(2,1)S(1)} %collective-permute-done.2.got.queries, ...), custom_call_target="tpu_custom_call", output_to_operand_aliasing={{0}: (3, {}), {1}: (4, {})} | custom-call | tf_op jit(solution)/shard_map/absorb/pallas_call | solution.py:138
  40.8 2.1 %absorb.13 = (f32[2,80,1024]{2,1,0:T(8,128)S(1)}, f32[2,8,1024]{2,1,0:T(8,128)S(1)}) custom-call(bf16[2,64,512]{2,1,0:T(8,128)(2,1)S(1)} %get-tuple-element.64.own.queries, bf16[2,64,512]{2,1,0:T(8,128)(2,1)S(1)} %collective-permute-done.2.got.queries, ...), custom_call_target="tpu_custom_call", output_to_operand_aliasing={{0}: (3, {}), {1}: (4, {})} | custom-call | tf_op jit(solution)/shard_map/absorb/pallas_call | solution.py:138
  42.9 1.9 %collective-permute-done.6.block = bf16[2,128,512]{2,1,0:T(8,128)(2,1)S(1)} collective-permute-done((bf16[2,128,512]{2,1,0:T(8,128)(2,1)S(1)}, bf16[2,128,512]{2,1,0:T(8,128)(2,1)S(1)}, u32[]{:S(2)}, u32[]{:S(2)}) %collective-permute-start.6) | collective-permute-done | bytes 262176 | tf_op jit(solution)/shard_map/ppermute | solution.py:338
  46.3 1.3 %closing.2 = (bf16[128,512]{1,0:T(8,128)(2,1)S(1)}, f32[64,512]{1,0:T(8,128)S(1)}) custom-call(bf16[2,64,512]{2,1,0:T(8,128)(2,1)S(1)} %get-tuple-element.64.own.queries, bf16[2,128,512]{2,1,0:T(8,128)(2,1)S(1)} %collective-permute-done.6.block, f32[2,80,1024]{2,1,0:T(8,128)S(1)} %get-tuple-element.106.carried, ...), custom_call_target="tpu_custom_call" | custom-call | tf_op jit(solution)/shard_map/closing/pallas_call | solution.py:161
  48.5 3.7 %collective-permute-done.10 = bf16[64,512]{1,0:T(8,128)(2,1)S(1)} collective-permute-done((bf16[64,512]{1,0:T(8,128)(2,1)S(1)}, bf16[64,512]{1,0:T(8,128)(2,1)S(1)}, u32[]{:S(2)}, u32[]{:S(2)}) %collective-permute-start.10) | collective-permute-done | bytes 65568 | tf_op jit(solution)/shard_map/ppermute | solution.py:310
  53.6 1.5 %collective-permute-start.12 = (bf16[80,1024]{1,0:T(8,128)(2,1)S(1)}, bf16[80,1024]{1,0:T(8,128)(2,1)S(1)}, u32[]{:S(2)}, u32[]{:S(2)}) collective-permute-start(bf16[80,1024]{1,0:T(8,128)(2,1)S(1)} %pad_maximum_fusion.chip_map), channel_id=1, source_target_pairs={{0,4},{1,5},{2,3},{3,2},{4,0},{5,1},{6,10},{7,11},{8,12},{9,13},{1... | collective-permute-start | bytes 491528 | tf_op jit(solution)/shard_map/ppermute | solution.py:328
  55.1 3.9 %collective-permute-done.12.near = bf16[80,1024]{1,0:T(8,128)(2,1)S(1)} collective-permute-done((bf16[80,1024]{1,0:T(8,128)(2,1)S(1)}, bf16[80,1024]{1,0:T(8,128)(2,1)S(1)}, u32[]{:S(2)}, u32[]{:S(2)}) %collective-permute-start.12) | collective-permute-done | bytes 163872 | tf_op jit(solution)/shard_map/ppermute | solution.py:328
  59.0 1.4 %collective-permute-done.13.far = bf16[80,1024]{1,0:T(8,128)(2,1)S(1)} collective-permute-done((bf16[80,1024]{1,0:T(8,128)(2,1)S(1)}, bf16[80,1024]{1,0:T(8,128)(2,1)S(1)}, u32[]{:S(2)}, u32[]{:S(2)}) %collective-permute-start.13) | collective-permute-done | bytes 163872 | tf_op jit(solution)/shard_map/ppermute | solution.py:310
  60.4 3.5 %network.1 = (f32[2,1024]{1,0:T(2,128)S(1)}, f32[32,576]{1,0:T(8,128)S(1)}, f32[64,128]{1,0:T(8,128)S(1)}) custom-call(s32[4]{0:T(128)S(1)} %pad_add_fusion.place, bf16[80,1024]{1,0:T(8,128)(2,1)S(1)} %pad_maximum_fusion.chip_map, bf16[80,1024]{1,0:T(8,128)(2,1)S(1)} %collective-permute-done.12.near, bf16[80,1024]{1,0:T(8,128)(2,1)S(1)} %collective-permute-done.13.far, ...), custom_call_target="tpu_custom_call" | custom-call | tf_op jit(solution)/shard_map/network/pallas_call | solution.py:293
  64.0 1.6 %collective-permute-start.14 = (bf16[32,896]{1,0:T(8,128)(2,1)S(1)}, bf16[32,896]{1,0:T(8,128)(2,1)S(1)}, u32[]{:S(2)}, u32[]{:S(2)}) collective-permute-start(bf16[32,896]{1,0:T(8,128)(2,1)S(1)} %fusion.14), channel_id=1, source_target_pairs={{0,16},{16,0},{1,17},{17,1},{2,18},{18,2},{3,19},{19,3},{4,20},{20... | collective-permute-start | bytes 172040 | tf_op jit(solution)/shard_map/ppermute | solution.py:316
  65.6 2.6 %collective-permute-done.14 = bf16[32,896]{1,0:T(8,128)(2,1)S(1)} collective-permute-done((bf16[32,896]{1,0:T(8,128)(2,1)S(1)}, bf16[32,896]{1,0:T(8,128)(2,1)S(1)}, u32[]{:S(2)}, u32[]{:S(2)}) %collective-permute-start.14) | collective-permute-done | bytes 57376 | tf_op jit(solution)/shard_map/ppermute | solution.py:316
  68.2 2.2 %collective-permute-start.15 = (bf16[32,896]{1,0:T(8,128)(2,1)S(1)}, bf16[32,896]{1,0:T(8,128)(2,1)S(1)}, u32[]{:S(2)}, u32[]{:S(2)}) collective-permute-start(bf16[32,896]{1,0:T(8,128)(2,1)S(1)} %add_convert_fusion.2), channel_id=1, source_target_pairs={{0,8},{2,10},{4,12},{6,14},{8,0},{10,2},{12,4},{14,6},{1,9},{3,11}... | collective-permute-start | bytes 172040 | tf_op jit(solution)/shard_map/ppermute | solution.py:316
  70.4 2.0 %collective-permute-start.16 = (bf16[32,896]{1,0:T(8,128)(2,1)S(1)}, bf16[32,896]{1,0:T(8,128)(2,1)S(1)}, u32[]{:S(2)}, u32[]{:S(2)}) collective-permute-start(bf16[32,896]{1,0:T(8,128)(2,1)S(1)} %add_convert_fusion.2), channel_id=1, source_target_pairs={{0,4},{2,6},{4,8},{6,10},{8,12},{10,14},{12,0},{14,2},{1,5},{3,7},... | collective-permute-start | bytes 172040 | tf_op jit(solution)/shard_map/ppermute | solution.py:316
  72.5 1.8 %collective-permute-start.17 = (bf16[32,896]{1,0:T(8,128)(2,1)S(1)}, bf16[32,896]{1,0:T(8,128)(2,1)S(1)}, u32[]{:S(2)}, u32[]{:S(2)}) collective-permute-start(bf16[32,896]{1,0:T(8,128)(2,1)S(1)} %add_convert_fusion.2), channel_id=1, source_target_pairs={{0,12},{2,14},{4,0},{6,2},{8,4},{10,6},{12,8},{14,10},{1,13},{3,15... | collective-permute-start | bytes 172040 | tf_op jit(solution)/shard_map/ppermute | solution.py:316
  74.9 1.6 %collective-permute-done.16 = bf16[32,896]{1,0:T(8,128)(2,1)S(1)} collective-permute-done((bf16[32,896]{1,0:T(8,128)(2,1)S(1)}, bf16[32,896]{1,0:T(8,128)(2,1)S(1)}, u32[]{:S(2)}, u32[]{:S(2)}) %collective-permute-start.16) | collective-permute-done | bytes 57376 | tf_op jit(solution)/shard_map/ppermute | solution.py:316
  78.5 1.6 %fusion.3 = f32[256,1024]{1,0:T(8,128)} fusion(bf16[1024,64]{0,1:T(8,128)(2,1)S(1)} %copy-done.4, f32[64,128]{1,0:T(8,128)S(1)} %collective-permute-done.19, f32[32,128]{1,0:T(8,128)S(1)} %get-tuple-element.126, f32[32,128]{1,0:T(8,128)S(1)} %get-tuple-element.125, pred[]{:T(512)S(6)} %eq.5), kind=kOutput, calls=%fused_computation.14 | convolution fusion | flops 201408512 | bytes 1245185 | tf_op jit(solution)/shard_map/dot_general | solution.py:449
  80.1 2.1 %collective-permute-done.18 = f32[32,576]{1,0:T(8,128)S(1)} collective-permute-done((f32[32,576]{1,0:T(8,128)S(1)}, f32[32,576]{1,0:T(8,128)S(1)}, u32[]{:S(2)}, u32[]{:S(2)}) %collective-permute-start.18) | collective-permute-done | bytes 73760 | tf_op jit(solution)/shard_map/ppermute | solution.py:310
  (64 shorter events, 13.0 us)
Async XLA Ops:
  0.6 37.6 %copy-start = (bf16[256,1024]{1,0:T(8,128)(2,1)S(1)}, bf16[256,1024]{1,0:T(8,128)(2,1)}, u32[]{:S(2)}) copy-start(bf16[256,1024]{1,0:T(8,128)(2,1)} %param.11) | copy-start | bytes 1572868
  4.8 3.2 %collective-permute-start = (bf16[2,128,512]{2,1,0:T(8,128)(2,1)S(1)}, bf16[2,128,512]{2,1,0:T(8,128)(2,1)S(1)}, u32[]{:S(2)}, u32[]{:S(2)}) collective-permute-start(bf16[2,128,512]{2,1,0:T(8,128)(2,1)S(1)} %get-tuple-element.65), channel_id=1, source_target_pairs={{0,2},{2,0},{4,6},{6,4},{8,10},{10,8},{12,14},{14,12},{1,3},{3,1},... | collective-permute-start | bytes 786440 | tf_op jit(solution)/shard_map/ppermute | solution.py:310
  5.4 10.8 %collective-permute-start.3 = (bf16[2,128,512]{2,1,0:T(8,128)(2,1)S(1)}, bf16[2,128,512]{2,1,0:T(8,128)(2,1)S(1)}, u32[]{:S(2)}, u32[]{:S(2)}) collective-permute-start(bf16[2,128,512]{2,1,0:T(8,128)(2,1)S(1)} %get-tuple-element.67.block), channel_id=1, source_target_pairs={{0,4},{2,6},{4,12},{6,14},{8,0},{10,2},{12,8},{14,10},{1,5},{3,7},... | collective-permute-start | bytes 786440 | tf_op jit(solution)/shard_map/ppermute | solution.py:338
  8.0 13.8 %collective-permute-start.1 = (bf16[2,128,512]{2,1,0:T(8,128)(2,1)S(1)}, bf16[2,128,512]{2,1,0:T(8,128)(2,1)S(1)}, u32[]{:S(2)}, u32[]{:S(2)}) collective-permute-start(bf16[2,128,512]{2,1,0:T(8,128)(2,1)S(1)} %collective-permute-done.block), channel_id=1, source_target_pairs={{0,4},{2,6},{4,12},{6,14},{8,0},{10,2},{12,8},{14,10},{1,5},{3,7},... | collective-permute-start | bytes 786440 | tf_op jit(solution)/shard_map/ppermute | solution.py:338
  12.7 1.4 %collective-permute-start.2 = (bf16[2,64,512]{2,1,0:T(8,128)(2,1)S(1)}, bf16[2,64,512]{2,1,0:T(8,128)(2,1)S(1)}, u32[]{:S(2)}, u32[]{:S(2)}) collective-permute-start(bf16[2,64,512]{2,1,0:T(8,128)(2,1)S(1)} %get-tuple-element.66), channel_id=1, source_target_pairs={{0,2},{2,0},{4,6},{6,4},{8,10},{10,8},{12,14},{14,12},{1,3},{3,1},... | collective-permute-start | bytes 393224 | tf_op jit(solution)/shard_map/ppermute | solution.py:310
  16.2 11.2 %collective-permute-start.5 = (bf16[2,128,512]{2,1,0:T(8,128)(2,1)S(1)}, bf16[2,128,512]{2,1,0:T(8,128)(2,1)S(1)}, u32[]{:S(2)}, u32[]{:S(2)}) collective-permute-start(bf16[2,128,512]{2,1,0:T(8,128)(2,1)S(1)} %collective-permute-done.3.block), channel_id=1, source_target_pairs={{0,4},{2,6},{4,12},{6,14},{8,0},{10,2},{12,8},{14,10},{1,5},{3,7},... | collective-permute-start | bytes 786440 | tf_op jit(solution)/shard_map/ppermute | solution.py:338
  21.8 11.2 %collective-permute-start.4 = (bf16[2,128,512]{2,1,0:T(8,128)(2,1)S(1)}, bf16[2,128,512]{2,1,0:T(8,128)(2,1)S(1)}, u32[]{:S(2)}, u32[]{:S(2)}) collective-permute-start(bf16[2,128,512]{2,1,0:T(8,128)(2,1)S(1)} %collective-permute-done.1.block), channel_id=1, source_target_pairs={{0,4},{2,6},{4,12},{6,14},{8,0},{10,2},{12,8},{14,10},{1,5},{3,7},... | collective-permute-start | bytes 786440 | tf_op jit(solution)/shard_map/ppermute | solution.py:338
  22.9 12.2 %copy-start.5 = (f32[1,2,2,128]{3,2,1,0:T(2,128)S(1)}, f32[1,2,2,128]{3,2,1,0:T(2,128)}, u32[]{:S(2)}) copy-start(f32[1,2,2,128]{3,2,1,0:T(2,128)} %param.15) | copy-start | bytes 6148
  22.9 14.9 %copy-start.3 = (bf16[1,512,1024]{2,1,0:T(8,128)(2,1)S(1)}, bf16[1,512,1024]{2,1,0:T(8,128)(2,1)}, u32[]{:S(2)}) copy-start(bf16[1,512,1024]{2,1,0:T(8,128)(2,1)} %param.8) | copy-start | bytes 3145732
  22.9 14.9 %copy-start.4 = (bf16[1024,64]{0,1:T(8,128)(2,1)S(1)}, bf16[1024,64]{0,1:T(8,128)(2,1)}, u32[]{:S(2)}) copy-start(bf16[1024,64]{0,1:T(8,128)(2,1)} %param.12) | copy-start | bytes 393220
  27.4 13.4 %collective-permute-start.7 = (bf16[2,128,512]{2,1,0:T(8,128)(2,1)S(1)}, bf16[2,128,512]{2,1,0:T(8,128)(2,1)S(1)}, u32[]{:S(2)}, u32[]{:S(2)}) collective-permute-start(bf16[2,128,512]{2,1,0:T(8,128)(2,1)S(1)} %collective-permute-done.5.block), channel_id=1, source_target_pairs={{0,4},{2,6},{4,12},{6,14},{8,0},{10,2},{12,8},{14,10},{1,5},{3,7},... | collective-permute-start | bytes 786440 | tf_op jit(solution)/shard_map/ppermute | solution.py:338
  30.6 7.9 %copy-start.1 = (bf16[2,64,576]{2,1,0:T(8,128)(2,1)S(1)}, bf16[2,64,576]{2,1,0:T(8,128)(2,1)}, u32[]{:S(2)}) copy-start(bf16[2,64,576]{2,1,0:T(8,128)(2,1)} %weight) | copy-start | bytes 442372
  35.1 5.7 %collective-permute-start.8 = (f32[2,2,128]{2,1,0:T(2,128)S(1)}, f32[2,2,128]{2,1,0:T(2,128)S(1)}, u32[]{:S(2)}, u32[]{:S(2)}) collective-permute-start(f32[2,2,128]{2,1,0:T(2,128)S(1)} %bitcast.27), channel_id=1, source_target_pairs={{0,1},{1,0},{2,3},{3,2},{4,5},{5,4},{6,7},{7,6},{8,9},{9,8},{10,11... | collective-permute-start | bytes 6152 | tf_op jit(solution)/shard_map/ppermute | solution.py:310
  37.0 7.9 %collective-permute-start.6 = (bf16[2,128,512]{2,1,0:T(8,128)(2,1)S(1)}, bf16[2,128,512]{2,1,0:T(8,128)(2,1)S(1)}, u32[]{:S(2)}, u32[]{:S(2)}) collective-permute-start(bf16[2,128,512]{2,1,0:T(8,128)(2,1)S(1)} %collective-permute-done.4.block), channel_id=1, source_target_pairs={{0,4},{2,6},{4,12},{6,14},{8,0},{10,2},{12,8},{14,10},{1,5},{3,7},... | collective-permute-start | bytes 786440 | tf_op jit(solution)/shard_map/ppermute | solution.py:338
  42.9 17.4 %copy-start.2 = (bf16[2,64]{1,0:T(2,128)(2,1)S(1)}, bf16[2,64]{1,0:T(2,128)(2,1)}, u32[]{:S(2)}) copy-start(bf16[2,64]{1,0:T(2,128)(2,1)} %head.1) | copy-start | bytes 772
  46.2 1.4 %collective-permute-start.9 = (f32[64,512]{1,0:T(8,128)S(1)}, f32[64,512]{1,0:T(8,128)S(1)}, u32[]{:S(2)}, u32[]{:S(2)}) collective-permute-start(f32[64,512]{1,0:T(8,128)S(1)} %get-tuple-element.110), channel_id=1, source_target_pairs={{0,2},{2,0},{4,6},{6,4},{8,10},{10,8},{12,14},{14,12},{1,3},{3,1},... | collective-permute-start | bytes 393224 | tf_op jit(solution)/shard_map/ppermute | solution.py:310
  47.6 4.5 %collective-permute-start.10 = (bf16[64,512]{1,0:T(8,128)(2,1)S(1)}, bf16[64,512]{1,0:T(8,128)(2,1)S(1)}, u32[]{:S(2)}, u32[]{:S(2)}) collective-permute-start(bf16[64,512]{1,0:T(8,128)(2,1)S(1)} %add_convert_fusion.1), channel_id=1, source_target_pairs={{0,1},{1,0},{2,3},{3,2},{4,5},{5,4},{6,7},{7,6},{8,9},{9,8},{10,11... | collective-permute-start | bytes 196616 | tf_op jit(solution)/shard_map/ppermute | solution.py:310
  52.2 1.3 %collective-permute-start.11 = (bf16[80,512]{1,0:T(8,128)(2,1)S(1)}, bf16[80,512]{1,0:T(8,128)(2,1)S(1)}, u32[]{:S(2)}, u32[]{:S(2)}) collective-permute-start(bf16[80,512]{1,0:T(8,128)(2,1)S(1)} %pad_maximum_fusion.1), channel_id=1, source_target_pairs={{0,2},{2,0},{4,6},{6,4},{8,10},{10,8},{12,14},{14,12},{1,3},{3,1},... | collective-permute-start | bytes 245768 | tf_op jit(solution)/shard_map/ppermute | solution.py:310
  53.6 5.4 %collective-permute-start.12 = (bf16[80,1024]{1,0:T(8,128)(2,1)S(1)}, bf16[80,1024]{1,0:T(8,128)(2,1)S(1)}, u32[]{:S(2)}, u32[]{:S(2)}) collective-permute-start(bf16[80,1024]{1,0:T(8,128)(2,1)S(1)} %pad_maximum_fusion.chip_map), channel_id=1, source_target_pairs={{0,4},{1,5},{2,3},{3,2},{4,0},{5,1},{6,10},{7,11},{8,12},{9,13},{1... | collective-permute-start | bytes 491528 | tf_op jit(solution)/shard_map/ppermute | solution.py:328
  59.0 1.4 %collective-permute-start.13 = (bf16[80,1024]{1,0:T(8,128)(2,1)S(1)}, bf16[80,1024]{1,0:T(8,128)(2,1)S(1)}, u32[]{:S(2)}, u32[]{:S(2)}) collective-permute-start(bf16[80,1024]{1,0:T(8,128)(2,1)S(1)} %collective-permute-done.12.near), channel_id=1, source_target_pairs={{0,2},{2,0},{4,6},{6,4},{8,10},{10,8},{12,14},{14,12},{1,3},{3,1},... | collective-permute-start | bytes 491528 | tf_op jit(solution)/shard_map/ppermute | solution.py:310
  64.0 4.2 %collective-permute-start.14 = (bf16[32,896]{1,0:T(8,128)(2,1)S(1)}, bf16[32,896]{1,0:T(8,128)(2,1)S(1)}, u32[]{:S(2)}, u32[]{:S(2)}) collective-permute-start(bf16[32,896]{1,0:T(8,128)(2,1)S(1)} %fusion.14), channel_id=1, source_target_pairs={{0,16},{16,0},{1,17},{17,1},{2,18},{18,2},{3,19},{19,3},{4,20},{20... | collective-permute-start | bytes 172040 | tf_op jit(solution)/shard_map/ppermute | solution.py:316
  68.2 6.7 %collective-permute-start.15 = (bf16[32,896]{1,0:T(8,128)(2,1)S(1)}, bf16[32,896]{1,0:T(8,128)(2,1)S(1)}, u32[]{:S(2)}, u32[]{:S(2)}) collective-permute-start(bf16[32,896]{1,0:T(8,128)(2,1)S(1)} %add_convert_fusion.2), channel_id=1, source_target_pairs={{0,8},{2,10},{4,12},{6,14},{8,0},{10,2},{12,4},{14,6},{1,9},{3,11}... | collective-permute-start | bytes 172040 | tf_op jit(solution)/shard_map/ppermute | solution.py:316
  70.4 6.1 %collective-permute-start.16 = (bf16[32,896]{1,0:T(8,128)(2,1)S(1)}, bf16[32,896]{1,0:T(8,128)(2,1)S(1)}, u32[]{:S(2)}, u32[]{:S(2)}) collective-permute-start(bf16[32,896]{1,0:T(8,128)(2,1)S(1)} %add_convert_fusion.2), channel_id=1, source_target_pairs={{0,4},{2,6},{4,8},{6,10},{8,12},{10,14},{12,0},{14,2},{1,5},{3,7},... | collective-permute-start | bytes 172040 | tf_op jit(solution)/shard_map/ppermute | solution.py:316
  72.5 4.7 %collective-permute-start.17 = (bf16[32,896]{1,0:T(8,128)(2,1)S(1)}, bf16[32,896]{1,0:T(8,128)(2,1)S(1)}, u32[]{:S(2)}, u32[]{:S(2)}) collective-permute-start(bf16[32,896]{1,0:T(8,128)(2,1)S(1)} %add_convert_fusion.2), channel_id=1, source_target_pairs={{0,12},{2,14},{4,0},{6,2},{8,4},{10,6},{12,8},{14,10},{1,13},{3,15... | collective-permute-start | bytes 172040 | tf_op jit(solution)/shard_map/ppermute | solution.py:316
  77.2 1.3 %collective-permute-start.19 = (f32[64,128]{1,0:T(8,128)S(1)}, f32[64,128]{1,0:T(8,128)S(1)}, u32[]{:S(2)}, u32[]{:S(2)}) collective-permute-start(f32[64,128]{1,0:T(8,128)S(1)} %pad_maximum_fusion.2), channel_id=1, source_target_pairs={{0,2},{2,0},{4,6},{6,4},{8,10},{10,8},{12,14},{14,12},{1,3},{3,1},... | collective-permute-start | bytes 98312 | tf_op jit(solution)/shard_map/ppermute | solution.py:310
  77.3 4.9 %collective-permute-start.18 = (f32[32,576]{1,0:T(8,128)S(1)}, f32[32,576]{1,0:T(8,128)S(1)}, u32[]{:S(2)}, u32[]{:S(2)}) collective-permute-start(f32[32,576]{1,0:T(8,128)S(1)} %get-tuple-element.124), channel_id=1, source_target_pairs={{0,1},{1,0},{2,3},{3,2},{4,5},{5,4},{6,7},{7,6},{8,9},{9,8},{10,11... | collective-permute-start | bytes 221192 | tf_op jit(solution)/shard_map/ppermute | solution.py:310
  78.0 4.2 %collective-permute-start.20 = (f32[32,576]{1,0:T(8,128)S(1)}, f32[32,576]{1,0:T(8,128)S(1)}, u32[]{:S(2)}, u32[]{:S(2)}) collective-permute-start(f32[32,576]{1,0:T(8,128)S(1)} %get-tuple-element.124), channel_id=1, source_target_pairs={{0,2},{2,0},{4,6},{6,4},{8,10},{10,8},{12,14},{14,12},{1,3},{3,1},... | collective-permute-start | bytes 221192 | tf_op jit(solution)/shard_map/ppermute | solution.py:310
  82.2 1.3 %collective-permute-start.21 = (f32[32,576]{1,0:T(8,128)S(1)}, f32[32,576]{1,0:T(8,128)S(1)}, u32[]{:S(2)}, u32[]{:S(2)}) collective-permute-start(f32[32,576]{1,0:T(8,128)S(1)} %collective-permute-done.18), channel_id=1, source_target_pairs={{0,2},{2,0},{4,6},{6,4},{8,10},{10,8},{12,14},{14,12},{1,3},{3,1},... | collective-permute-start | bytes 221192 | tf_op jit(solution)/shard_map/ppermute | solution.py:310

commit v3 on v1

--- a/solution.py
+++ b/solution.py
@@ -324,6 +324,22 @@
     return terms[0]
 
 
+def sum_frames(values, across):
+    size, cols = lax.axis_size("dp"), lax.axis_size("col")
+    sent = values.astype(BF16)
+    terms = []
+    for step in range(size):
+        pairs = []
+        for i in range(size):
+            other = i ^ step if size & (size - 1) == 0 else (i + step) % size
+            pairs += [(i * cols + j, other * cols + (j ^ 1 if across else j)) for j in range(cols)]
+        moved = lax.ppermute(sent, ("dp", "col"), pairs) if step or across else sent
+        terms.append(moved.astype(F32))
+    while len(terms) > 1:
+        terms = [sum(terms[at : at + 2][1:], terms[at]) for at in range(0, len(terms), 2)]
+    return terms[0]
+
+
 def in_order(core, mine, theirs, axis):
     return jnp.where(
         core == 0, jnp.concatenate([mine, theirs], axis=axis), jnp.concatenate([theirs, mine], axis=axis)
@@ -336,7 +352,7 @@
     frame_rows = tokens[0]
     cotangent = holo_cot[0]
     rows_dev, cols_dev = cotangent.shape[1:]
-    tok_count, col_count, dp_count = (lax.axis_size(axis) for axis in ("tok", "col", "dp"))
+    tok_count, col_count = lax.axis_size("tok"), lax.axis_size("col")
     chips = tok_count // 2
     tok_at, half = lax.axis_index("tok"), lax.axis_index("col")
     core = lax.rem(tok_at, 2)
@@ -416,23 +432,20 @@
     pieces = gradient.shape[0] // rows
     folded_gradient = [gradient[at * rows : (at + 1) * rows] for at in range(pieces)]
     sent = jnp.concatenate([jnp.pad(sums, ((0, 0), (0, lanes - taps_wide))), *folded_gradient], axis=1)
-    summed = everyone(sent, "dp", 1, dp_count)
-    total = everyone(summed, "tok", 2, chips)
-    own_grad = total[:, :taps_wide]
-    col_grad = swapped(own_grad, "col")
+    summed, hologram = lax.optimization_barrier((everyone(sent, "tok", 2, chips), hologram))
+    own_terms = sum_frames(summed, False)
+    far_terms = sum_frames(summed[:, :taps_wide], True)
     wide = gradient.shape[1]
     own_small = jnp.concatenate(
-        [total[:, lanes + at * wide : lanes + (at + 1) * wide] for at in range(pieces)], axis=0
-    )
-    small = in_order(core, own_small, swapped(own_small, "tok"), 1)
+        [own_terms[:, lanes + at * wide : lanes + (at + 1) * wide] for at in range(pieces)], axis=0
+    )
+    other_small = swapped(own_small, "tok")
+    small = in_order(core, own_small, other_small, 1)
     out_grad = lax.dot_general(
         small, readout_weight.astype(F32), (((0,), (1,)), ((), ())), precision=lax.Precision.HIGHEST
     )
-    core_grad = swapped(own_grad, "tok")
-    col_grad, out_grad, core_grad = lax.optimization_barrier((col_grad, out_grad, core_grad))
-    far_grad = swapped(col_grad, "tok")
-    layer_grad = in_order(half, own_grad, col_grad, 0)
-    other_grad = in_order(half, core_grad, far_grad, 0)
+    layer_grad = in_order(half, own_terms[:, :taps_wide], far_terms, 0)
+    other_grad = swapped(layer_grad, "tok")
     conv_grad = in_order(core, layer_grad[None], other_grad[None], 0)
     return (hologram[None], conv_grad, out_grad)
 

time: 84.5 us -> 84.1 us (level)
  waiting for transfers between devices: 30.5 us -> 28.5 us
  starting transfers between devices: 23 us -> 24.5 us
    ppermute x0 -> x3, waiting for transfers between devices: none -> 3.66 us  [sum_frames(): moved = lax.ppermute(sent, ('dp', 'col'), pairs) if step or across else sent]
    ppermute x0 -> x3, starting transfers between devices: none -> 3.55 us  [sum_frames(): moved = lax.ppermute(sent, ('dp', 'col'), pairs) if step or across else sent]
    ppermute x11 -> x9, waiting for transfers between devices: 11.3 us -> 8.34 us  [swapped(): return lax.ppermute(values, axis, [(i, i ^ 1) for i in range(size)])]
    ppermute x4 -> x3, waiting for transfers between devices: 4.85 us -> 2.25 us  [passed(): return lax.ppermute(values, axis, pairs)]
    ppermute x4 -> x3, starting transfers between devices: 7.63 us -> 6.04 us  [passed(): return lax.ppermute(values, axis, pairs)]
    ppermute x11 -> x9, starting transfers between devices: 4.52 us -> 4.11 us  [swapped(): return lax.ppermute(values, axis, [(i, i ^ 1) for i in range(size)])]
  transfers between devices with their start and end apart: 22 -> 22, of which waited for: 16 -> 17; matrix products, arithmetic and copies ran while one was open for 4% -> 4% of each run, Pallas kernels for 20% -> 20%
where the time goes in v3:
time: 84.1 us; the launch traced here: 83.9 us
  waiting for transfers between devices  28.5 us (34%)
  starting transfers between devices  24.5 us (29%)
  Pallas kernels  23.8 us (28%)
  matrix products  2.26 us (3%)
  local copies, waits for them, and re-layouts  1.97 us (2%)
  other arithmetic  1.88 us (2%)
  between operations  1.03 us (1%)
    pallas_call x7, Pallas kernels, absorb(): pl.pallas_call(functools.partial(absorb_kernel, first), out_shape=shapes,...  14.3 us
    ppermute x6, waiting for transfers between devices, round_ring(): lax.ppermute(values, 'tok', [(i, 2 * following[i // 2] + i % 2) for i in...  10.4 us
    ppermute x6, starting transfers between devices, round_ring(): lax.ppermute(values, 'tok', [(i, 2 * following[i // 2] + i % 2) for i in...  9.34 us
    ppermute x9, waiting for transfers between devices, swapped(): return lax.ppermute(values, axis, [(i, i ^ 1) for i in range(size)])  8.34 us
    ppermute x3, starting transfers between devices, passed(): return lax.ppermute(values, axis, pairs)  6.04 us
    ppermute x9, starting transfers between devices, swapped(): return lax.ppermute(values, axis, [(i, i ^ 1) for i in range(size)])  4.11 us
    ppermute x1, waiting for transfers between devices, beside(): return lax.ppermute(values, ('tok', 'col'), pairs)  3.88 us
    ppermute x3, waiting for transfers between devices, sum_frames(): moved = lax.ppermute(sent, ('dp', 'col'), pairs) if step or across else sent  3.66 us
  transfers between devices with their start and end apart: 22, of which 17 were waited for; matrix products, arithmetic and copies ran while one was open for 4% of the time, Pallas kernels for 20%

profile of v3, /device:TPU:0, one launch (start us, length us, event | category | flops | bytes accessed | tf_op | source)
XLA Modules:
  0.0 83.9 jit_solution(15520805085223159312)
XLA Ops:
  1.5 1.2 %copy-done.2 = bf16[1,512,1024]{2,1,0:T(8,128)(2,1)S(1)} copy-done((bf16[1,512,1024]{2,1,0:T(8,128)(2,1)S(1)}, bf16[1,512,1024]{2,1,0:T(8,128)(2,1)}, u32[]{:S(2)}) %copy-start.2) | copy-done | bytes 1048600
  3.5 1.4 %project.2 = (bf16[2,128,512]{2,1,0:T(8,128)(2,1)S(1)}, bf16[2,128,512]{2,1,0:T(8,128)(2,1)S(1)}) custom-call(s32[4]{0:T(128)S(1)} %pad_add_fusion.place, bf16[512,1024]{1,0:T(8,128)(2,1)S(1)} %normalize.1.normed, bf16[3,1024,256]{2,1,0:T(8,128)(2,1)S(1)} %copy-done.1), custom_call_target="tpu_custom_call" | custom-call | tf_op jit(solution)/shard_map/project/pallas_call | solution.py:69
  5.4 2.6 %collective-permute-start.3 = (bf16[2,128,512]{2,1,0:T(8,128)(2,1)S(1)}, bf16[2,128,512]{2,1,0:T(8,128)(2,1)S(1)}, u32[]{:S(2)}, u32[]{:S(2)}) collective-permute-start(bf16[2,128,512]{2,1,0:T(8,128)(2,1)S(1)} %get-tuple-element.75.block), channel_id=1, source_target_pairs={{0,4},{2,6},{4,12},{6,14},{8,0},{10,2},{12,8},{14,10},{1,5},{3,7},... | collective-permute-start | bytes 786440 | tf_op jit(solution)/shard_map/ppermute | solution.py:315
  8.1 2.6 %collective-permute-start.1 = (bf16[2,128,512]{2,1,0:T(8,128)(2,1)S(1)}, bf16[2,128,512]{2,1,0:T(8,128)(2,1)S(1)}, u32[]{:S(2)}, u32[]{:S(2)}) collective-permute-start(bf16[2,128,512]{2,1,0:T(8,128)(2,1)S(1)} %collective-permute-done.block), channel_id=1, source_target_pairs={{0,4},{2,6},{4,12},{6,14},{8,0},{10,2},{12,8},{14,10},{1,5},{3,7},... | collective-permute-start | bytes 786440 | tf_op jit(solution)/shard_map/ppermute | solution.py:315
  11.8 1.3 %collective-permute-done.2.got.queries = bf16[2,64,512]{2,1,0:T(8,128)(2,1)S(1)} collective-permute-done((bf16[2,64,512]{2,1,0:T(8,128)(2,1)S(1)}, bf16[2,64,512]{2,1,0:T(8,128)(2,1)S(1)}, u32[]{:S(2)}, u32[]{:S(2)}) %collective-permute-start.2) | collective-permute-done | bytes 131104 | tf_op jit(solution)/shard_map/ppermute | solution.py:287
  13.1 2.0 %absorb.7 = (f32[2,80,1024]{2,1,0:T(8,128)S(1)}, f32[2,8,1024]{2,1,0:T(8,128)S(1)}) custom-call(bf16[2,64,512]{2,1,0:T(8,128)(2,1)S(1)} %get-tuple-element.72.own.queries, bf16[2,64,512]{2,1,0:T(8,128)(2,1)S(1)} %collective-permute-done.2.got.queries, bf16[2,128,512]{2,1,0:T(8,128)(2,1)S(1)} %get-tuple-element.75.block), custom_call_target="tpu_custom_call" | custom-call | tf_op jit(solution)/shard_map/absorb/pallas_call | solution.py:115
  17.3 2.1 %absorb.8 = (f32[2,80,1024]{2,1,0:T(8,128)S(1)}, f32[2,8,1024]{2,1,0:T(8,128)S(1)}) custom-call(bf16[2,64,512]{2,1,0:T(8,128)(2,1)S(1)} %get-tuple-element.72.own.queries, bf16[2,64,512]{2,1,0:T(8,128)(2,1)S(1)} %collective-permute-done.2.got.queries, ...), custom_call_target="tpu_custom_call", output_to_operand_aliasing={{0}: (3, {}), {1}: (4, {})} | custom-call | tf_op jit(solution)/shard_map/absorb/pallas_call | solution.py:115
  19.4 2.4 %collective-permute-done.1.block = bf16[2,128,512]{2,1,0:T(8,128)(2,1)S(1)} collective-permute-done((bf16[2,128,512]{2,1,0:T(8,128)(2,1)S(1)}, bf16[2,128,512]{2,1,0:T(8,128)(2,1)S(1)}, u32[]{:S(2)}, u32[]{:S(2)}) %collective-permute-start.1) | collective-permute-done | bytes 262176 | tf_op jit(solution)/shard_map/ppermute | solution.py:315
  23.0 2.0 %absorb.9 = (f32[2,80,1024]{2,1,0:T(8,128)S(1)}, f32[2,8,1024]{2,1,0:T(8,128)S(1)}) custom-call(bf16[2,64,512]{2,1,0:T(8,128)(2,1)S(1)} %get-tuple-element.72.own.queries, bf16[2,64,512]{2,1,0:T(8,128)(2,1)S(1)} %collective-permute-done.2.got.queries, ...), custom_call_target="tpu_custom_call", output_to_operand_aliasing={{0}: (3, {}), {1}: (4, {})} | custom-call | tf_op jit(solution)/shard_map/absorb/pallas_call | solution.py:115
  25.0 2.4 %collective-permute-done.5.block = bf16[2,128,512]{2,1,0:T(8,128)(2,1)S(1)} collective-permute-done((bf16[2,128,512]{2,1,0:T(8,128)(2,1)S(1)}, bf16[2,128,512]{2,1,0:T(8,128)(2,1)S(1)}, u32[]{:S(2)}, u32[]{:S(2)}) %collective-permute-start.5) | collective-permute-done | bytes 262176 | tf_op jit(solution)/shard_map/ppermute | solution.py:315
  28.6 2.1 %absorb.10 = (f32[2,80,1024]{2,1,0:T(8,128)S(1)}, f32[2,8,1024]{2,1,0:T(8,128)S(1)}) custom-call(bf16[2,64,512]{2,1,0:T(8,128)(2,1)S(1)} %get-tuple-element.72.own.queries, bf16[2,64,512]{2,1,0:T(8,128)(2,1)S(1)} %collective-permute-done.2.got.queries, ...), custom_call_target="tpu_custom_call", output_to_operand_aliasing={{0}: (3, {}), {1}: (4, {})} | custom-call | tf_op jit(solution)/shard_map/absorb/pallas_call | solution.py:115
  30.6 2.4 %collective-permute-done.4.block = bf16[2,128,512]{2,1,0:T(8,128)(2,1)S(1)} collective-permute-done((bf16[2,128,512]{2,1,0:T(8,128)(2,1)S(1)}, bf16[2,128,512]{2,1,0:T(8,128)(2,1)S(1)}, u32[]{:S(2)}, u32[]{:S(2)}) %collective-permute-start.4) | collective-permute-done | bytes 262176 | tf_op jit(solution)/shard_map/ppermute | solution.py:315
  33.1 2.1 %absorb.11 = (f32[2,80,1024]{2,1,0:T(8,128)S(1)}, f32[2,8,1024]{2,1,0:T(8,128)S(1)}) custom-call(bf16[2,64,512]{2,1,0:T(8,128)(2,1)S(1)} %get-tuple-element.72.own.queries, bf16[2,64,512]{2,1,0:T(8,128)(2,1)S(1)} %collective-permute-done.2.got.queries, ...), custom_call_target="tpu_custom_call", output_to_operand_aliasing={{0}: (3, {}), {1}: (4, {})} | custom-call | tf_op jit(solution)/shard_map/absorb/pallas_call | solution.py:115
  35.1 1.9 %collective-permute-start.8 = (f32[2,2,128]{2,1,0:T(2,128)S(1)}, f32[2,2,128]{2,1,0:T(2,128)S(1)}, u32[]{:S(2)}, u32[]{:S(2)}) collective-permute-start(f32[2,2,128]{2,1,0:T(2,128)S(1)} %bitcast.26), channel_id=1, source_target_pairs={{0,1},{1,0},{2,3},{3,2},{4,5},{5,4},{6,7},{7,6},{8,9},{9,8},{10,11... | collective-permute-start | bytes 6152 | tf_op jit(solution)/shard_map/ppermute | solution.py:287
  38.8 2.0 %absorb.12 = (f32[2,80,1024]{2,1,0:T(8,128)S(1)}, f32[2,8,1024]{2,1,0:T(8,128)S(1)}) custom-call(bf16[2,64,512]{2,1,0:T(8,128)(2,1)S(1)} %get-tuple-element.72.own.queries, bf16[2,64,512]{2,1,0:T(8,128)(2,1)S(1)} %collective-permute-done.2.got.queries, ...), custom_call_target="tpu_custom_call", output_to_operand_aliasing={{0}: (3, {}), {1}: (4, {})} | custom-call | tf_op jit(solution)/shard_map/absorb/pallas_call | solution.py:115
  40.9 2.0 %absorb.13 = (f32[2,80,1024]{2,1,0:T(8,128)S(1)}, f32[2,8,1024]{2,1,0:T(8,128)S(1)}) custom-call(bf16[2,64,512]{2,1,0:T(8,128)(2,1)S(1)} %get-tuple-element.72.own.queries, bf16[2,64,512]{2,1,0:T(8,128)(2,1)S(1)} %collective-permute-done.2.got.queries, ...), custom_call_target="tpu_custom_call", output_to_operand_aliasing={{0}: (3, {}), {1}: (4, {})} | custom-call | tf_op jit(solution)/shard_map/absorb/pallas_call | solution.py:115
  43.0 1.9 %collective-permute-done.6.block = bf16[2,128,512]{2,1,0:T(8,128)(2,1)S(1)} collective-permute-done((bf16[2,128,512]{2,1,0:T(8,128)(2,1)S(1)}, bf16[2,128,512]{2,1,0:T(8,128)(2,1)S(1)}, u32[]{:S(2)}, u32[]{:S(2)}) %collective-permute-start.6) | collective-permute-done | bytes 262176 | tf_op jit(solution)/shard_map/ppermute | solution.py:315
  44.9 1.3 %closing.3 = (bf16[128,512]{1,0:T(8,128)(2,1)S(1)}, f32[64,512]{1,0:T(8,128)S(1)}) custom-call(bf16[2,64,512]{2,1,0:T(8,128)(2,1)S(1)} %collective-permute-done.2.got.queries, bf16[2,128,512]{2,1,0:T(8,128)(2,1)S(1)} %collective-permute-done.6.block, f32[2,80,1024]{2,1,0:T(8,128)S(1)} %get-tuple-element.115.carried, ...), custom_call_target="tpu_custom_call" | custom-call | tf_op jit(solution)/shard_map/closing/pallas_call | solution.py:138
  46.3 1.3 %closing.2 = (bf16[128,512]{1,0:T(8,128)(2,1)S(1)}, f32[64,512]{1,0:T(8,128)S(1)}) custom-call(bf16[2,64,512]{2,1,0:T(8,128)(2,1)S(1)} %get-tuple-element.72.own.queries, bf16[2,128,512]{2,1,0:T(8,128)(2,1)S(1)} %collective-permute-done.6.block, f32[2,80,1024]{2,1,0:T(8,128)S(1)} %get-tuple-element.115.carried, ...), custom_call_target="tpu_custom_call" | custom-call | tf_op jit(solution)/shard_map/closing/pallas_call | solution.py:138
  48.5 3.7 %collective-permute-done.10 = bf16[64,512]{1,0:T(8,128)(2,1)S(1)} collective-permute-done((bf16[64,512]{1,0:T(8,128)(2,1)S(1)}, bf16[64,512]{1,0:T(8,128)(2,1)S(1)}, u32[]{:S(2)}, u32[]{:S(2)}) %collective-permute-start.10) | collective-permute-done | bytes 65568 | tf_op jit(solution)/shard_map/ppermute | solution.py:287
  52.3 1.3 %collective-permute-done.11 = bf16[80,512]{1,0:T(8,128)(2,1)S(1)} collective-permute-done((bf16[80,512]{1,0:T(8,128)(2,1)S(1)}, bf16[80,512]{1,0:T(8,128)(2,1)S(1)}, u32[]{:S(2)}, u32[]{:S(2)}) %collective-permute-start.11) | collective-permute-done | bytes 81952 | tf_op jit(solution)/shard_map/ppermute | solution.py:287
  53.6 1.5 %collective-permute-start.12 = (bf16[80,1024]{1,0:T(8,128)(2,1)S(1)}, bf16[80,1024]{1,0:T(8,128)(2,1)S(1)}, u32[]{:S(2)}, u32[]{:S(2)}) collective-permute-start(bf16[80,1024]{1,0:T(8,128)(2,1)S(1)} %pad_maximum_fusion.chip_map), channel_id=1, source_target_pairs={{0,4},{1,5},{2,3},{3,2},{4,0},{5,1},{6,10},{7,11},{8,12},{9,13},{1... | collective-permute-start | bytes 491528 | tf_op jit(solution)/shard_map/ppermute | solution.py:305
  55.1 3.9 %collective-permute-done.12.near = bf16[80,1024]{1,0:T(8,128)(2,1)S(1)} collective-permute-done((bf16[80,1024]{1,0:T(8,128)(2,1)S(1)}, bf16[80,1024]{1,0:T(8,128)(2,1)S(1)}, u32[]{:S(2)}, u32[]{:S(2)}) %collective-permute-start.12) | collective-permute-done | bytes 163872 | tf_op jit(solution)/shard_map/ppermute | solution.py:305
  59.0 1.4 %collective-permute-done.13.far = bf16[80,1024]{1,0:T(8,128)(2,1)S(1)} collective-permute-done((bf16[80,1024]{1,0:T(8,128)(2,1)S(1)}, bf16[80,1024]{1,0:T(8,128)(2,1)S(1)}, u32[]{:S(2)}, u32[]{:S(2)}) %collective-permute-start.13) | collective-permute-done | bytes 163872 | tf_op jit(solution)/shard_map/ppermute | solution.py:287
  60.4 3.5 %network.1 = (f32[2,1024]{1,0:T(2,128)S(1)}, f32[32,576]{1,0:T(8,128)S(1)}, f32[64,128]{1,0:T(8,128)S(1)}) custom-call(s32[4]{0:T(128)S(1)} %pad_add_fusion.place, bf16[80,1024]{1,0:T(8,128)(2,1)S(1)} %pad_maximum_fusion.chip_map, bf16[80,1024]{1,0:T(8,128)(2,1)S(1)} %collective-permute-done.12.near, bf16[80,1024]{1,0:T(8,128)(2,1)S(1)} %collective-permute-done.13.far, ...), custom_call_target="tpu_custom_call" | custom-call | tf_op jit(solution)/shard_map/network/pallas_call | solution.py:270
  64.0 2.2 %collective-permute-start.14 = (bf16[32,896]{1,0:T(8,128)(2,1)S(1)}, bf16[32,896]{1,0:T(8,128)(2,1)S(1)}, u32[]{:S(2)}, u32[]{:S(2)}) collective-permute-start(bf16[32,896]{1,0:T(8,128)(2,1)S(1)} %fusion.14), channel_id=1, source_target_pairs={{0,8},{2,10},{4,12},{6,14},{8,0},{10,2},{12,4},{14,6},{1,9},{3,11}... | collective-permute-start | bytes 172040 | tf_op jit(solution)/shard_map/ppermute | solution.py:293
  66.2 2.0 %collective-permute-start.15 = (bf16[32,896]{1,0:T(8,128)(2,1)S(1)}, bf16[32,896]{1,0:T(8,128)(2,1)S(1)}, u32[]{:S(2)}, u32[]{:S(2)}) collective-permute-start(bf16[32,896]{1,0:T(8,128)(2,1)S(1)} %fusion.14), channel_id=1, source_target_pairs={{0,4},{2,6},{4,8},{6,10},{8,12},{10,14},{12,0},{14,2},{1,5},{3,7},... | collective-permute-start | bytes 172040 | tf_op jit(solution)/shard_map/ppermute | solution.py:293
  68.2 1.8 %collective-permute-start.16 = (bf16[32,896]{1,0:T(8,128)(2,1)S(1)}, bf16[32,896]{1,0:T(8,128)(2,1)S(1)}, u32[]{:S(2)}, u32[]{:S(2)}) collective-permute-start(bf16[32,896]{1,0:T(8,128)(2,1)S(1)} %fusion.14), channel_id=1, source_target_pairs={{0,12},{2,14},{4,0},{6,2},{8,4},{10,6},{12,8},{14,10},{1,13},{3,15... | collective-permute-start | bytes 172040 | tf_op jit(solution)/shard_map/ppermute | solution.py:293
  73.8 2.2 %collective-permute-start.19 = (bf16[32,576]{1,0:T(8,128)(2,1)S(1)}, bf16[32,576]{1,0:T(8,128)(2,1)S(1)}, u32[]{:S(2)}, u32[]{:S(2)}) collective-permute-start(bf16[32,576]{1,0:T(8,128)(2,1)S(1)} %slice.30), channel_id=1, source_target_pairs={{0,17},{1,16},{16,1},{17,0},{2,19},{3,18},{18,3},{19,2},{4,21},{5,... | collective-permute-start | bytes 110600 | tf_op jit(solution)/shard_map/ppermute | solution.py:336
  77.4 1.3 %collective-permute-done.19 = bf16[32,576]{1,0:T(8,128)(2,1)S(1)} collective-permute-done((bf16[32,576]{1,0:T(8,128)(2,1)S(1)}, bf16[32,576]{1,0:T(8,128)(2,1)S(1)}, u32[]{:S(2)}, u32[]{:S(2)}) %collective-permute-start.19) | collective-permute-done | bytes 36896 | tf_op jit(solution)/shard_map/ppermute | solution.py:336
  78.7 1.5 %collective-permute-done.17 = bf16[32,896]{1,0:T(8,128)(2,1)S(1)} collective-permute-done((bf16[32,896]{1,0:T(8,128)(2,1)S(1)}, bf16[32,896]{1,0:T(8,128)(2,1)S(1)}, u32[]{:S(2)}, u32[]{:S(2)}) %collective-permute-start.17) | collective-permute-done | bytes 57376 | tf_op jit(solution)/shard_map/ppermute | solution.py:336
  81.6 1.6 %fusion.3 = f32[256,1024]{1,0:T(8,128)} fusion(bf16[1024,64]{0,1:T(8,128)(2,1)S(1)} %copy-done.6, f32[64,128]{1,0:T(8,128)S(1)} %collective-permute-done.21, f32[32,128]{1,0:T(8,128)S(1)} %get-tuple-element.132, f32[32,128]{1,0:T(8,128)S(1)} %get-tuple-element.131, pred[]{:T(512)S(6)} %eq.10), kind=kOutput, calls=%fused_computation.15 | convolution fusion | flops 201408512 | bytes 1245185 | tf_op jit(solution)/shard_map/dot_general | solution.py:444
  (72 shorter events, 17.8 us)
Async XLA Ops:
  0.6 37.6 %copy-start = (bf16[256,1024]{1,0:T(8,128)(2,1)S(1)}, bf16[256,1024]{1,0:T(8,128)(2,1)}, u32[]{:S(2)}) copy-start(bf16[256,1024]{1,0:T(8,128)(2,1)} %param.11) | copy-start | bytes 1572868
  0.6 2.8 %copy-start.1 = (bf16[3,1024,256]{2,1,0:T(8,128)(2,1)S(1)}, bf16[3,1024,256]{2,1,0:T(8,128)(2,1)}, u32[]{:S(2)}) copy-start(bf16[3,1024,256]{2,1,0:T(8,128)(2,1)} %weight.1) | copy-start | bytes 4718596
  1.5 1.2 %copy-start.2 = (bf16[1,512,1024]{2,1,0:T(8,128)(2,1)S(1)}, bf16[1,512,1024]{2,1,0:T(8,128)(2,1)}, u32[]{:S(2)}) copy-start(bf16[1,512,1024]{2,1,0:T(8,128)(2,1)} %param.8) | copy-start | bytes 3145732
  4.9 3.2 %collective-permute-start = (bf16[2,128,512]{2,1,0:T(8,128)(2,1)S(1)}, bf16[2,128,512]{2,1,0:T(8,128)(2,1)S(1)}, u32[]{:S(2)}, u32[]{:S(2)}) collective-permute-start(bf16[2,128,512]{2,1,0:T(8,128)(2,1)S(1)} %get-tuple-element.73), channel_id=1, source_target_pairs={{0,2},{2,0},{4,6},{6,4},{8,10},{10,8},{12,14},{14,12},{1,3},{3,1},... | collective-permute-start | bytes 786440 | tf_op jit(solution)/shard_map/ppermute | solution.py:287
  5.4 10.8 %collective-permute-start.3 = (bf16[2,128,512]{2,1,0:T(8,128)(2,1)S(1)}, bf16[2,128,512]{2,1,0:T(8,128)(2,1)S(1)}, u32[]{:S(2)}, u32[]{:S(2)}) collective-permute-start(bf16[2,128,512]{2,1,0:T(8,128)(2,1)S(1)} %get-tuple-element.75.block), channel_id=1, source_target_pairs={{0,4},{2,6},{4,12},{6,14},{8,0},{10,2},{12,8},{14,10},{1,5},{3,7},... | collective-permute-start | bytes 786440 | tf_op jit(solution)/shard_map/ppermute | solution.py:315
  8.1 13.8 %collective-permute-start.1 = (bf16[2,128,512]{2,1,0:T(8,128)(2,1)S(1)}, bf16[2,128,512]{2,1,0:T(8,128)(2,1)S(1)}, u32[]{:S(2)}, u32[]{:S(2)}) collective-permute-start(bf16[2,128,512]{2,1,0:T(8,128)(2,1)S(1)} %collective-permute-done.block), channel_id=1, source_target_pairs={{0,4},{2,6},{4,12},{6,14},{8,0},{10,2},{12,8},{14,10},{1,5},{3,7},... | collective-permute-start | bytes 786440 | tf_op jit(solution)/shard_map/ppermute | solution.py:315
  11.7 1.4 %collective-permute-start.2 = (bf16[2,64,512]{2,1,0:T(8,128)(2,1)S(1)}, bf16[2,64,512]{2,1,0:T(8,128)(2,1)S(1)}, u32[]{:S(2)}, u32[]{:S(2)}) collective-permute-start(bf16[2,64,512]{2,1,0:T(8,128)(2,1)S(1)} %get-tuple-element.74), channel_id=1, source_target_pairs={{0,2},{2,0},{4,6},{6,4},{8,10},{10,8},{12,14},{14,12},{1,3},{3,1},... | collective-permute-start | bytes 393224 | tf_op jit(solution)/shard_map/ppermute | solution.py:287
  16.2 11.2 %collective-permute-start.5 = (bf16[2,128,512]{2,1,0:T(8,128)(2,1)S(1)}, bf16[2,128,512]{2,1,0:T(8,128)(2,1)S(1)}, u32[]{:S(2)}, u32[]{:S(2)}) collective-permute-start(bf16[2,128,512]{2,1,0:T(8,128)(2,1)S(1)} %collective-permute-done.3.block), channel_id=1, source_target_pairs={{0,4},{2,6},{4,12},{6,14},{8,0},{10,2},{12,8},{14,10},{1,5},{3,7},... | collective-permute-start | bytes 786440 | tf_op jit(solution)/shard_map/ppermute | solution.py:315
  21.8 11.2 %collective-permute-start.4 = (bf16[2,128,512]{2,1,0:T(8,128)(2,1)S(1)}, bf16[2,128,512]{2,1,0:T(8,128)(2,1)S(1)}, u32[]{:S(2)}, u32[]{:S(2)}) collective-permute-start(bf16[2,128,512]{2,1,0:T(8,128)(2,1)S(1)} %collective-permute-done.1.block), channel_id=1, source_target_pairs={{0,4},{2,6},{4,12},{6,14},{8,0},{10,2},{12,8},{14,10},{1,5},{3,7},... | collective-permute-start | bytes 786440 | tf_op jit(solution)/shard_map/ppermute | solution.py:315
  23.0 12.2 %copy-start.7 = (f32[1,2,2,128]{3,2,1,0:T(2,128)S(1)}, f32[1,2,2,128]{3,2,1,0:T(2,128)}, u32[]{:S(2)}) copy-start(f32[1,2,2,128]{3,2,1,0:T(2,128)} %param.15) | copy-start | bytes 6148
  23.0 14.9 %copy-start.3 = (bf16[1,512,1024]{2,1,0:T(8,128)(2,1)S(1)}, bf16[1,512,1024]{2,1,0:T(8,128)(2,1)}, u32[]{:S(2)}) copy-start(bf16[1,512,1024]{2,1,0:T(8,128)(2,1)} %param.8) | copy-start | bytes 3145732
  23.0 14.9 %copy-start.6 = (bf16[1024,64]{0,1:T(8,128)(2,1)S(1)}, bf16[1024,64]{0,1:T(8,128)(2,1)}, u32[]{:S(2)}) copy-start(bf16[1024,64]{0,1:T(8,128)(2,1)} %param.12) | copy-start | bytes 393220
  27.5 13.4 %collective-permute-start.7 = (bf16[2,128,512]{2,1,0:T(8,128)(2,1)S(1)}, bf16[2,128,512]{2,1,0:T(8,128)(2,1)S(1)}, u32[]{:S(2)}, u32[]{:S(2)}) collective-permute-start(bf16[2,128,512]{2,1,0:T(8,128)(2,1)S(1)} %collective-permute-done.5.block), channel_id=1, source_target_pairs={{0,4},{2,6},{4,12},{6,14},{8,0},{10,2},{12,8},{14,10},{1,5},{3,7},... | collective-permute-start | bytes 786440 | tf_op jit(solution)/shard_map/ppermute | solution.py:315
  30.6 7.9 %copy-start.4 = (bf16[2,64,576]{2,1,0:T(8,128)(2,1)S(1)}, bf16[2,64,576]{2,1,0:T(8,128)(2,1)}, u32[]{:S(2)}) copy-start(bf16[2,64,576]{2,1,0:T(8,128)(2,1)} %weight.2) | copy-start | bytes 442372
  35.1 5.7 %collective-permute-start.8 = (f32[2,2,128]{2,1,0:T(2,128)S(1)}, f32[2,2,128]{2,1,0:T(2,128)S(1)}, u32[]{:S(2)}, u32[]{:S(2)}) collective-permute-start(f32[2,2,128]{2,1,0:T(2,128)S(1)} %bitcast.26), channel_id=1, source_target_pairs={{0,1},{1,0},{2,3},{3,2},{4,5},{5,4},{6,7},{7,6},{8,9},{9,8},{10,11... | collective-permute-start | bytes 6152 | tf_op jit(solution)/shard_map/ppermute | solution.py:287
  37.0 7.9 %collective-permute-start.6 = (bf16[2,128,512]{2,1,0:T(8,128)(2,1)S(1)}, bf16[2,128,512]{2,1,0:T(8,128)(2,1)S(1)}, u32[]{:S(2)}, u32[]{:S(2)}) collective-permute-start(bf16[2,128,512]{2,1,0:T(8,128)(2,1)S(1)} %collective-permute-done.4.block), channel_id=1, source_target_pairs={{0,4},{2,6},{4,12},{6,14},{8,0},{10,2},{12,8},{14,10},{1,5},{3,7},... | collective-permute-start | bytes 786440 | tf_op jit(solution)/shard_map/ppermute | solution.py:315
  43.0 17.4 %copy-start.5 = (bf16[2,64]{1,0:T(2,128)(2,1)S(1)}, bf16[2,64]{1,0:T(2,128)(2,1)}, u32[]{:S(2)}) copy-start(bf16[2,64]{1,0:T(2,128)(2,1)} %head.1) | copy-start | bytes 772
  46.2 1.4 %collective-permute-start.9 = (f32[64,512]{1,0:T(8,128)S(1)}, f32[64,512]{1,0:T(8,128)S(1)}, u32[]{:S(2)}, u32[]{:S(2)}) collective-permute-start(f32[64,512]{1,0:T(8,128)S(1)} %get-tuple-element.119), channel_id=1, source_target_pairs={{0,2},{2,0},{4,6},{6,4},{8,10},{10,8},{12,14},{14,12},{1,3},{3,1},... | collective-permute-start | bytes 393224 | tf_op jit(solution)/shard_map/ppermute | solution.py:287
  47.7 4.5 %collective-permute-start.10 = (bf16[64,512]{1,0:T(8,128)(2,1)S(1)}, bf16[64,512]{1,0:T(8,128)(2,1)S(1)}, u32[]{:S(2)}, u32[]{:S(2)}) collective-permute-start(bf16[64,512]{1,0:T(8,128)(2,1)S(1)} %add_convert_fusion.1), channel_id=1, source_target_pairs={{0,1},{1,0},{2,3},{3,2},{4,5},{5,4},{6,7},{7,6},{8,9},{9,8},{10,11... | collective-permute-start | bytes 196616 | tf_op jit(solution)/shard_map/ppermute | solution.py:287
  52.2 1.3 %collective-permute-start.11 = (bf16[80,512]{1,0:T(8,128)(2,1)S(1)}, bf16[80,512]{1,0:T(8,128)(2,1)S(1)}, u32[]{:S(2)}, u32[]{:S(2)}) collective-permute-start(bf16[80,512]{1,0:T(8,128)(2,1)S(1)} %pad_maximum_fusion.1), channel_id=1, source_target_pairs={{0,2},{2,0},{4,6},{6,4},{8,10},{10,8},{12,14},{14,12},{1,3},{3,1},... | collective-permute-start | bytes 245768 | tf_op jit(solution)/shard_map/ppermute | solution.py:287
  53.6 5.4 %collective-permute-start.12 = (bf16[80,1024]{1,0:T(8,128)(2,1)S(1)}, bf16[80,1024]{1,0:T(8,128)(2,1)S(1)}, u32[]{:S(2)}, u32[]{:S(2)}) collective-permute-start(bf16[80,1024]{1,0:T(8,128)(2,1)S(1)} %pad_maximum_fusion.chip_map), channel_id=1, source_target_pairs={{0,4},{1,5},{2,3},{3,2},{4,0},{5,1},{6,10},{7,11},{8,12},{9,13},{1... | collective-permute-start | bytes 491528 | tf_op jit(solution)/shard_map/ppermute | solution.py:305
  59.0 1.4 %collective-permute-start.13 = (bf16[80,1024]{1,0:T(8,128)(2,1)S(1)}, bf16[80,1024]{1,0:T(8,128)(2,1)S(1)}, u32[]{:S(2)}, u32[]{:S(2)}) collective-permute-start(bf16[80,1024]{1,0:T(8,128)(2,1)S(1)} %collective-permute-done.12.near), channel_id=1, source_target_pairs={{0,2},{2,0},{4,6},{6,4},{8,10},{10,8},{12,14},{14,12},{1,3},{3,1},... | collective-permute-start | bytes 491528 | tf_op jit(solution)/shard_map/ppermute | solution.py:287
  64.0 7.3 %collective-permute-start.14 = (bf16[32,896]{1,0:T(8,128)(2,1)S(1)}, bf16[32,896]{1,0:T(8,128)(2,1)S(1)}, u32[]{:S(2)}, u32[]{:S(2)}) collective-permute-start(bf16[32,896]{1,0:T(8,128)(2,1)S(1)} %fusion.14), channel_id=1, source_target_pairs={{0,8},{2,10},{4,12},{6,14},{8,0},{10,2},{12,4},{14,6},{1,9},{3,11}... | collective-permute-start | bytes 172040 | tf_op jit(solution)/shard_map/ppermute | solution.py:293
  66.2 6.1 %collective-permute-start.15 = (bf16[32,896]{1,0:T(8,128)(2,1)S(1)}, bf16[32,896]{1,0:T(8,128)(2,1)S(1)}, u32[]{:S(2)}, u32[]{:S(2)}) collective-permute-start(bf16[32,896]{1,0:T(8,128)(2,1)S(1)} %fusion.14), channel_id=1, source_target_pairs={{0,4},{2,6},{4,8},{6,10},{8,12},{10,14},{12,0},{14,2},{1,5},{3,7},... | collective-permute-start | bytes 172040 | tf_op jit(solution)/shard_map/ppermute | solution.py:293
  68.2 4.7 %collective-permute-start.16 = (bf16[32,896]{1,0:T(8,128)(2,1)S(1)}, bf16[32,896]{1,0:T(8,128)(2,1)S(1)}, u32[]{:S(2)}, u32[]{:S(2)}) collective-permute-start(bf16[32,896]{1,0:T(8,128)(2,1)S(1)} %fusion.14), channel_id=1, source_target_pairs={{0,12},{2,14},{4,0},{6,2},{8,4},{10,6},{12,8},{14,10},{1,13},{3,15... | collective-permute-start | bytes 172040 | tf_op jit(solution)/shard_map/ppermute | solution.py:293
  73.0 4.4 %collective-permute-start.18 = (bf16[32,576]{1,0:T(8,128)(2,1)S(1)}, bf16[32,576]{1,0:T(8,128)(2,1)S(1)}, u32[]{:S(2)}, u32[]{:S(2)}) collective-permute-start(bf16[32,576]{1,0:T(8,128)(2,1)S(1)} %slice.30), channel_id=1, source_target_pairs={{0,1},{1,0},{16,17},{17,16},{2,3},{3,2},{18,19},{19,18},{4,5},{5,4... | collective-permute-start | bytes 110600 | tf_op jit(solution)/shard_map/ppermute | solution.py:336
  73.8 4.9 %collective-permute-start.19 = (bf16[32,576]{1,0:T(8,128)(2,1)S(1)}, bf16[32,576]{1,0:T(8,128)(2,1)S(1)}, u32[]{:S(2)}, u32[]{:S(2)}) collective-permute-start(bf16[32,576]{1,0:T(8,128)(2,1)S(1)} %slice.30), channel_id=1, source_target_pairs={{0,17},{1,16},{16,1},{17,0},{2,19},{3,18},{18,3},{19,2},{4,21},{5,... | collective-permute-start | bytes 110600 | tf_op jit(solution)/shard_map/ppermute | solution.py:336
  76.1 4.2 %collective-permute-start.17 = (bf16[32,896]{1,0:T(8,128)(2,1)S(1)}, bf16[32,896]{1,0:T(8,128)(2,1)S(1)}, u32[]{:S(2)}, u32[]{:S(2)}) collective-permute-start(bf16[32,896]{1,0:T(8,128)(2,1)S(1)} %add_add_fusion), channel_id=1, source_target_pairs={{0,16},{1,17},{16,0},{17,1},{2,18},{3,19},{18,2},{19,3},{4,20},{5,... | collective-permute-start | bytes 172040 | tf_op jit(solution)/shard_map/ppermute | solution.py:336
  80.3 1.3 %collective-permute-start.21 = (f32[64,128]{1,0:T(8,128)S(1)}, f32[64,128]{1,0:T(8,128)S(1)}, u32[]{:S(2)}, u32[]{:S(2)}) collective-permute-start(f32[64,128]{1,0:T(8,128)S(1)} %pad_maximum_fusion.2), channel_id=1, source_target_pairs={{0,2},{2,0},{4,6},{6,4},{8,10},{10,8},{12,14},{14,12},{1,3},{3,1},... | collective-permute-start | bytes 98312 | tf_op jit(solution)/shard_map/ppermute | solution.py:287
  80.4 2.8 %collective-permute-start.20 = (f32[64,576]{1,0:T(8,128)S(1)}, f32[64,576]{1,0:T(8,128)S(1)}, u32[]{:S(2)}, u32[]{:S(2)}) collective-permute-start(f32[64,576]{1,0:T(8,128)S(1)} %maximum_select_fusion.2), channel_id=1, source_target_pairs={{0,2},{2,0},{4,6},{6,4},{8,10},{10,8},{12,14},{14,12},{1,3},{3,1},... | collective-permute-start | bytes 442376 | tf_op jit(solution)/shard_map/ppermute | solution.py:287

commit v4 on v3

--- a/solution.py
+++ b/solution.py
@@ -387,10 +387,13 @@
     for turn in range(chips):
         arriving = []
         if turn < chips - 1:
-            for block in blocks:
+            leaving = blocks
+            if turn == chips - 2:
+                leaving = blocks[:-1] + jnp.split(blocks[-1], 2, axis=2)
+            for block in leaving:
                 arriving.append(round_ring(block))
         for at, block in enumerate(blocks):
-            if turn == chips - 1 and at == 1:
+            if turn == chips - 1 and at == len(blocks) - 1:
                 break
             state = absorb(queries, block, state)
             if at == 0 and turn == chips - 2:
@@ -408,8 +411,8 @@
         blocks = arriving if turn < chips - 1 else blocks
     forward, backward, folded, direct = prepared
 
-    their_context, their_share = closing(1, queries, blocks[1], state, folded)
-    own_context, own_share = closing(0, queries, blocks[1], state, folded)
+    their_context, their_share = closing(1, queries, blocks[-1], state, folded)
+    own_context, own_share = closing(0, queries, blocks[-1], state, folded)
     partial = own_share + swapped(their_share, "tok")
     partial = (partial + jnp.where(half == 0, direct, 0.0)).astype(BF16)
     own_map = (partial.astype(F32) + swapped(partial, "col").astype(F32)).astype(BF16)
@@ -432,21 +435,19 @@
     pieces = gradient.shape[0] // rows
     folded_gradient = [gradient[at * rows : (at + 1) * rows] for at in range(pieces)]
     sent = jnp.concatenate([jnp.pad(sums, ((0, 0), (0, lanes - taps_wide))), *folded_gradient], axis=1)
-    summed, hologram = lax.optimization_barrier((everyone(sent, "tok", 2, chips), hologram))
+    summed = everyone(sent, "tok", 2, chips)
     own_terms = sum_frames(summed, False)
     far_terms = sum_frames(summed[:, :taps_wide], True)
     wide = gradient.shape[1]
     own_small = jnp.concatenate(
         [own_terms[:, lanes + at * wide : lanes + (at + 1) * wide] for at in range(pieces)], axis=0
     )
-    other_small = swapped(own_small, "tok")
-    small = in_order(core, own_small, other_small, 1)
+    small = in_order(core, own_small, swapped(own_small, "tok"), 1)
     out_grad = lax.dot_general(
         small, readout_weight.astype(F32), (((0,), (1,)), ((), ())), precision=lax.Precision.HIGHEST
     )
     layer_grad = in_order(half, own_terms[:, :taps_wide], far_terms, 0)
-    other_grad = swapped(layer_grad, "tok")
-    conv_grad = in_order(core, layer_grad[None], other_grad[None], 0)
+    conv_grad = in_order(core, layer_grad[None], swapped(layer_grad, "tok")[None], 0)
     return (hologram[None], conv_grad, out_grad)
 
 

time: 84.1 us -> 85.9 us (1.021)
  waiting for transfers between devices: 28.5 us -> 29.5 us
    ppermute x6 -> x7, starting transfers between devices: 9.34 us -> 12.8 us  [round_ring(): lax.ppermute(values, 'tok', [(i, 2 * following[i // 2] + i % 2) for i in...]
    ppermute x3, starting transfers between devices: 6.04 us -> 3.95 us  [passed(): return lax.ppermute(values, axis, pairs)]
    ppermute x6 -> x7, waiting for transfers between devices: 10.4 us -> 8.4 us  [round_ring(): lax.ppermute(values, 'tok', [(i, 2 * following[i // 2] + i % 2) for i in...]
    ppermute x3, waiting for transfers between devices: 2.25 us -> 3.71 us  [passed(): return lax.ppermute(values, axis, pairs)]
    pallas_call x7 -> x8, Pallas kernels: 14.3 us -> 15.7 us  [absorb(): pl.pallas_call(functools.partial(absorb_kernel, first), out_shape=shapes,...]
    ppermute x1, waiting for transfers between devices: 3.88 us -> 5.07 us  [beside(): return lax.ppermute(values, ('tok', 'col'), pairs)]
    ppermute x1, starting transfers between devices: 1.5 us -> 0.31 us  [beside(): return lax.ppermute(values, ('tok', 'col'), pairs)]
  transfers between devices with their start and end apart: 22 -> 23, of which waited for: 17 -> 15; matrix products, arithmetic and copies ran while one was open for 4% -> 4% of each run, Pallas kernels for 20% -> 21%
where the time goes in v4:
time: 85.9 us; the launch traced here: 85.7 us
  waiting for transfers between devices  29.5 us (34%)
  Pallas kernels  24.6 us (29%)
  starting transfers between devices  24.5 us (29%)
  matrix products  2.24 us (3%)
  local copies, waits for them, and re-layouts  1.98 us (2%)
  other arithmetic  1.88 us (2%)
  between operations  1.07 us (1%)
    pallas_call x8, Pallas kernels, absorb(): pl.pallas_call(functools.partial(absorb_kernel, first), out_shape=shapes,...  15.7 us
    ppermute x7, starting transfers between devices, round_ring(): lax.ppermute(values, 'tok', [(i, 2 * following[i // 2] + i % 2) for i in...  12.8 us
    ppermute x9, waiting for transfers between devices, swapped(): return lax.ppermute(values, axis, [(i, i ^ 1) for i in range(size)])  8.68 us
    ppermute x7, waiting for transfers between devices, round_ring(): lax.ppermute(values, 'tok', [(i, 2 * following[i // 2] + i % 2) for i in...  8.4 us
    ppermute x1, waiting for transfers between devices, beside(): return lax.ppermute(values, ('tok', 'col'), pairs)  5.07 us
    ppermute x3, starting transfers between devices, passed(): return lax.ppermute(values, axis, pairs)  3.95 us
    ppermute x9, starting transfers between devices, swapped(): return lax.ppermute(values, axis, [(i, i ^ 1) for i in range(size)])  3.87 us
    ppermute x3, waiting for transfers between devices, passed(): return lax.ppermute(values, axis, pairs)  3.71 us
  transfers between devices with their start and end apart: 23, of which 15 were waited for; matrix products, arithmetic and copies ran while one was open for 4% of the time, Pallas kernels for 21%

profile of v4, /device:TPU:0, one launch (start us, length us, event | category | flops | bytes accessed | tf_op | source)
XLA Modules:
  0.0 85.7 jit_solution(8218293366851733398)
XLA Ops:
  1.5 1.2 %copy-done.2 = bf16[1,512,1024]{2,1,0:T(8,128)(2,1)S(1)} copy-done((bf16[1,512,1024]{2,1,0:T(8,128)(2,1)S(1)}, bf16[1,512,1024]{2,1,0:T(8,128)(2,1)}, u32[]{:S(2)}) %copy-start.2) | copy-done | bytes 1048600
  3.5 1.4 %project.2 = (bf16[2,128,512]{2,1,0:T(8,128)(2,1)S(1)}, bf16[2,128,512]{2,1,0:T(8,128)(2,1)S(1)}) custom-call(s32[4]{0:T(128)S(1)} %pad_add_fusion.place, bf16[512,1024]{1,0:T(8,128)(2,1)S(1)} %normalize.1.normed, bf16[3,1024,256]{2,1,0:T(8,128)(2,1)S(1)} %copy-done.1), custom_call_target="tpu_custom_call" | custom-call | tf_op jit(solution)/shard_map/project/pallas_call | solution.py:69
  5.4 2.6 %collective-permute-start.3 = (bf16[2,128,512]{2,1,0:T(8,128)(2,1)S(1)}, bf16[2,128,512]{2,1,0:T(8,128)(2,1)S(1)}, u32[]{:S(2)}, u32[]{:S(2)}) collective-permute-start(bf16[2,128,512]{2,1,0:T(8,128)(2,1)S(1)} %get-tuple-element.75.block), channel_id=1, source_target_pairs={{0,4},{2,6},{4,12},{6,14},{8,0},{10,2},{12,8},{14,10},{1,5},{3,7},... | collective-permute-start | bytes 786440 | tf_op jit(solution)/shard_map/ppermute | solution.py:315
  8.1 2.6 %collective-permute-start.1 = (bf16[2,128,512]{2,1,0:T(8,128)(2,1)S(1)}, bf16[2,128,512]{2,1,0:T(8,128)(2,1)S(1)}, u32[]{:S(2)}, u32[]{:S(2)}) collective-permute-start(bf16[2,128,512]{2,1,0:T(8,128)(2,1)S(1)} %collective-permute-done.block), channel_id=1, source_target_pairs={{0,4},{2,6},{4,12},{6,14},{8,0},{10,2},{12,8},{14,10},{1,5},{3,7},... | collective-permute-start | bytes 786440 | tf_op jit(solution)/shard_map/ppermute | solution.py:315
  11.8 1.3 %collective-permute-done.2.got.queries = bf16[2,64,512]{2,1,0:T(8,128)(2,1)S(1)} collective-permute-done((bf16[2,64,512]{2,1,0:T(8,128)(2,1)S(1)}, bf16[2,64,512]{2,1,0:T(8,128)(2,1)S(1)}, u32[]{:S(2)}, u32[]{:S(2)}) %collective-permute-start.2) | collective-permute-done | bytes 131104 | tf_op jit(solution)/shard_map/ppermute | solution.py:287
  13.1 2.0 %absorb.8 = (f32[2,80,1024]{2,1,0:T(8,128)S(1)}, f32[2,8,1024]{2,1,0:T(8,128)S(1)}) custom-call(bf16[2,64,512]{2,1,0:T(8,128)(2,1)S(1)} %get-tuple-element.72.own.queries, bf16[2,64,512]{2,1,0:T(8,128)(2,1)S(1)} %collective-permute-done.2.got.queries, bf16[2,128,512]{2,1,0:T(8,128)(2,1)S(1)} %get-tuple-element.75.block), custom_call_target="tpu_custom_call" | custom-call | tf_op jit(solution)/shard_map/absorb/pallas_call | solution.py:115
  16.2 1.1 %collective-permute-start.5 = (bf16[2,128,512]{2,1,0:T(8,128)(2,1)S(1)}, bf16[2,128,512]{2,1,0:T(8,128)(2,1)S(1)}, u32[]{:S(2)}, u32[]{:S(2)}) collective-permute-start(bf16[2,128,512]{2,1,0:T(8,128)(2,1)S(1)} %collective-permute-done.3.block), channel_id=1, source_target_pairs={{0,4},{2,6},{4,12},{6,14},{8,0},{10,2},{12,8},{14,10},{1,5},{3,7},... | collective-permute-start | bytes 786440 | tf_op jit(solution)/shard_map/ppermute | solution.py:315
  17.3 2.1 %absorb.9 = (f32[2,80,1024]{2,1,0:T(8,128)S(1)}, f32[2,8,1024]{2,1,0:T(8,128)S(1)}) custom-call(bf16[2,64,512]{2,1,0:T(8,128)(2,1)S(1)} %get-tuple-element.72.own.queries, bf16[2,64,512]{2,1,0:T(8,128)(2,1)S(1)} %collective-permute-done.2.got.queries, ...), custom_call_target="tpu_custom_call", output_to_operand_aliasing={{0}: (3, {}), {1}: (4, {})} | custom-call | tf_op jit(solution)/shard_map/absorb/pallas_call | solution.py:115
  19.4 2.4 %collective-permute-done.1.block = bf16[2,128,512]{2,1,0:T(8,128)(2,1)S(1)} collective-permute-done((bf16[2,128,512]{2,1,0:T(8,128)(2,1)S(1)}, bf16[2,128,512]{2,1,0:T(8,128)(2,1)S(1)}, u32[]{:S(2)}, u32[]{:S(2)}) %collective-permute-start.1) | collective-permute-done | bytes 262176 | tf_op jit(solution)/shard_map/ppermute | solution.py:315
  23.0 2.0 %absorb.10 = (f32[2,80,1024]{2,1,0:T(8,128)S(1)}, f32[2,8,1024]{2,1,0:T(8,128)S(1)}) custom-call(bf16[2,64,512]{2,1,0:T(8,128)(2,1)S(1)} %get-tuple-element.72.own.queries, bf16[2,64,512]{2,1,0:T(8,128)(2,1)S(1)} %collective-permute-done.2.got.queries, ...), custom_call_target="tpu_custom_call", output_to_operand_aliasing={{0}: (3, {}), {1}: (4, {})} | custom-call | tf_op jit(solution)/shard_map/absorb/pallas_call | solution.py:115
  25.0 2.4 %collective-permute-done.5.block = bf16[2,128,512]{2,1,0:T(8,128)(2,1)S(1)} collective-permute-done((bf16[2,128,512]{2,1,0:T(8,128)(2,1)S(1)}, bf16[2,128,512]{2,1,0:T(8,128)(2,1)S(1)}, u32[]{:S(2)}, u32[]{:S(2)}) %collective-permute-start.5) | collective-permute-done | bytes 262176 | tf_op jit(solution)/shard_map/ppermute | solution.py:315
  27.5 1.1 %collective-permute-start.8 = (bf16[2,128,512]{2,1,0:T(8,128)(2,1)S(1)}, bf16[2,128,512]{2,1,0:T(8,128)(2,1)S(1)}, u32[]{:S(2)}, u32[]{:S(2)}) collective-permute-start(bf16[2,128,512]{2,1,0:T(8,128)(2,1)S(1)} %collective-permute-done.5.block), channel_id=1, source_target_pairs={{0,4},{2,6},{4,12},{6,14},{8,0},{10,2},{12,8},{14,10},{1,5},{3,7},... | collective-permute-start | bytes 786440 | tf_op jit(solution)/shard_map/ppermute | solution.py:315
  28.6 2.1 %absorb.11 = (f32[2,80,1024]{2,1,0:T(8,128)S(1)}, f32[2,8,1024]{2,1,0:T(8,128)S(1)}) custom-call(bf16[2,64,512]{2,1,0:T(8,128)(2,1)S(1)} %get-tuple-element.72.own.queries, bf16[2,64,512]{2,1,0:T(8,128)(2,1)S(1)} %collective-permute-done.2.got.queries, ...), custom_call_target="tpu_custom_call", output_to_operand_aliasing={{0}: (3, {}), {1}: (4, {})} | custom-call | tf_op jit(solution)/shard_map/absorb/pallas_call | solution.py:115
  30.6 2.4 %collective-permute-done.4.block = bf16[2,128,512]{2,1,0:T(8,128)(2,1)S(1)} collective-permute-done((bf16[2,128,512]{2,1,0:T(8,128)(2,1)S(1)}, bf16[2,128,512]{2,1,0:T(8,128)(2,1)S(1)}, u32[]{:S(2)}, u32[]{:S(2)}) %collective-permute-start.4) | collective-permute-done | bytes 262176 | tf_op jit(solution)/shard_map/ppermute | solution.py:315
  33.1 2.0 %absorb.12 = (f32[2,80,1024]{2,1,0:T(8,128)S(1)}, f32[2,8,1024]{2,1,0:T(8,128)S(1)}) custom-call(bf16[2,64,512]{2,1,0:T(8,128)(2,1)S(1)} %get-tuple-element.72.own.queries, bf16[2,64,512]{2,1,0:T(8,128)(2,1)S(1)} %collective-permute-done.2.got.queries, ...), custom_call_target="tpu_custom_call", output_to_operand_aliasing={{0}: (3, {}), {1}: (4, {})} | custom-call | tf_op jit(solution)/shard_map/absorb/pallas_call | solution.py:115
  35.1 1.9 %collective-permute-start.9 = (f32[2,2,128]{2,1,0:T(2,128)S(1)}, f32[2,2,128]{2,1,0:T(2,128)S(1)}, u32[]{:S(2)}, u32[]{:S(2)}) collective-permute-start(f32[2,2,128]{2,1,0:T(2,128)S(1)} %bitcast.27), channel_id=1, source_target_pairs={{0,1},{1,0},{2,3},{3,2},{4,5},{5,4},{6,7},{7,6},{8,9},{9,8},{10,11... | collective-permute-start | bytes 6152 | tf_op jit(solution)/shard_map/ppermute | solution.py:287
  37.9 3.4 %collective-permute-start.6 = (bf16[2,128,256]{2,1,0:T(8,128)(2,1)S(1)}, bf16[2,128,256]{2,1,0:T(8,128)(2,1)S(1)}, u32[]{:S(2)}, u32[]{:S(2)}) collective-permute-start(bf16[2,128,256]{2,1,0:T(8,128)(2,1)S(1)} %get-tuple-element.132), channel_id=1, source_target_pairs={{0,4},{2,6},{4,12},{6,14},{8,0},{10,2},{12,8},{14,10},{1,5},{3,7},... | collective-permute-start | bytes 393224 | tf_op jit(solution)/shard_map/ppermute | solution.py:315
  42.2 2.1 %absorb.13 = (f32[2,80,1024]{2,1,0:T(8,128)S(1)}, f32[2,8,1024]{2,1,0:T(8,128)S(1)}) custom-call(bf16[2,64,512]{2,1,0:T(8,128)(2,1)S(1)} %get-tuple-element.72.own.queries, bf16[2,64,512]{2,1,0:T(8,128)(2,1)S(1)} %collective-permute-done.2.got.queries, ...), custom_call_target="tpu_custom_call", output_to_operand_aliasing={{0}: (3, {}), {1}: (4, {})} | custom-call | tf_op jit(solution)/shard_map/absorb/pallas_call | solution.py:115
  44.3 2.0 %absorb.14 = (f32[2,80,1024]{2,1,0:T(8,128)S(1)}, f32[2,8,1024]{2,1,0:T(8,128)S(1)}) custom-call(bf16[2,64,512]{2,1,0:T(8,128)(2,1)S(1)} %get-tuple-element.72.own.queries, bf16[2,64,512]{2,1,0:T(8,128)(2,1)S(1)} %collective-permute-done.2.got.queries, ...), custom_call_target="tpu_custom_call", output_to_operand_aliasing={{0}: (3, {}), {1}: (4, {})} | custom-call | tf_op jit(solution)/shard_map/absorb/pallas_call | solution.py:115
  46.4 1.4 %absorb.15 = (f32[2,80,1024]{2,1,0:T(8,128)S(1)}, f32[2,8,1024]{2,1,0:T(8,128)S(1)}) custom-call(bf16[2,64,512]{2,1,0:T(8,128)(2,1)S(1)} %get-tuple-element.72.own.queries, bf16[2,64,512]{2,1,0:T(8,128)(2,1)S(1)} %collective-permute-done.2.got.queries, ...), custom_call_target="tpu_custom_call", output_to_operand_aliasing={{0}: (3, {}), {1}: (4, {})} | custom-call | tf_op jit(solution)/shard_map/absorb/pallas_call | solution.py:115
  50.9 3.7 %collective-permute-done.11 = bf16[64,512]{1,0:T(8,128)(2,1)S(1)} collective-permute-done((bf16[64,512]{1,0:T(8,128)(2,1)S(1)}, bf16[64,512]{1,0:T(8,128)(2,1)S(1)}, u32[]{:S(2)}, u32[]{:S(2)}) %collective-permute-start.11) | collective-permute-done | bytes 65568 | tf_op jit(solution)/shard_map/ppermute | solution.py:287
  54.8 1.3 %collective-permute-done.12 = bf16[80,512]{1,0:T(8,128)(2,1)S(1)} collective-permute-done((bf16[80,512]{1,0:T(8,128)(2,1)S(1)}, bf16[80,512]{1,0:T(8,128)(2,1)S(1)}, u32[]{:S(2)}, u32[]{:S(2)}) %collective-permute-start.12) | collective-permute-done | bytes 81952 | tf_op jit(solution)/shard_map/ppermute | solution.py:287
  56.4 5.1 %collective-permute-done.13.near = bf16[80,1024]{1,0:T(8,128)(2,1)S(1)} collective-permute-done((bf16[80,1024]{1,0:T(8,128)(2,1)S(1)}, bf16[80,1024]{1,0:T(8,128)(2,1)S(1)}, u32[]{:S(2)}, u32[]{:S(2)}) %collective-permute-start.13) | collective-permute-done | bytes 163872 | tf_op jit(solution)/shard_map/ppermute | solution.py:305
  61.4 1.4 %collective-permute-done.14.far = bf16[80,1024]{1,0:T(8,128)(2,1)S(1)} collective-permute-done((bf16[80,1024]{1,0:T(8,128)(2,1)S(1)}, bf16[80,1024]{1,0:T(8,128)(2,1)S(1)}, u32[]{:S(2)}, u32[]{:S(2)}) %collective-permute-start.14) | collective-permute-done | bytes 163872 | tf_op jit(solution)/shard_map/ppermute | solution.py:287
  62.8 3.5 %network.1 = (f32[2,1024]{1,0:T(2,128)S(1)}, f32[32,576]{1,0:T(8,128)S(1)}, f32[64,128]{1,0:T(8,128)S(1)}) custom-call(s32[4]{0:T(128)S(1)} %pad_add_fusion.place, bf16[80,1024]{1,0:T(8,128)(2,1)S(1)} %pad_maximum_fusion.chip_map, bf16[80,1024]{1,0:T(8,128)(2,1)S(1)} %collective-permute-done.13.near, bf16[80,1024]{1,0:T(8,128)(2,1)S(1)} %collective-permute-done.14.far, ...), custom_call_target="tpu_custom_call" | custom-call | tf_op jit(solution)/shard_map/network/pallas_call | solution.py:270
  66.5 1.3 %collective-permute-start.16 = (bf16[32,896]{1,0:T(8,128)(2,1)S(1)}, bf16[32,896]{1,0:T(8,128)(2,1)S(1)}, u32[]{:S(2)}, u32[]{:S(2)}) collective-permute-start(bf16[32,896]{1,0:T(8,128)(2,1)S(1)} %fusion.14), channel_id=1, source_target_pairs={{0,4},{2,6},{4,8},{6,10},{8,12},{10,14},{12,0},{14,2},{1,5},{3,7},... | collective-permute-start | bytes 172040 | tf_op jit(solution)/shard_map/ppermute | solution.py:293
  67.8 2.6 %collective-permute-start.17 = (bf16[32,896]{1,0:T(8,128)(2,1)S(1)}, bf16[32,896]{1,0:T(8,128)(2,1)S(1)}, u32[]{:S(2)}, u32[]{:S(2)}) collective-permute-start(bf16[32,896]{1,0:T(8,128)(2,1)S(1)} %fusion.14), channel_id=1, source_target_pairs={{0,12},{2,14},{4,0},{6,2},{8,4},{10,6},{12,8},{14,10},{1,13},{3,15... | collective-permute-start | bytes 172040 | tf_op jit(solution)/shard_map/ppermute | solution.py:293
  70.4 3.3 %collective-permute-done.15 = bf16[32,896]{1,0:T(8,128)(2,1)S(1)} collective-permute-done((bf16[32,896]{1,0:T(8,128)(2,1)S(1)}, bf16[32,896]{1,0:T(8,128)(2,1)S(1)}, u32[]{:S(2)}, u32[]{:S(2)}) %collective-permute-start.15) | collective-permute-done | bytes 57376 | tf_op jit(solution)/shard_map/ppermute | solution.py:293
  74.8 2.5 %collective-permute-start.20 = (bf16[32,576]{1,0:T(8,128)(2,1)S(1)}, bf16[32,576]{1,0:T(8,128)(2,1)S(1)}, u32[]{:S(2)}, u32[]{:S(2)}) collective-permute-start(bf16[32,576]{1,0:T(8,128)(2,1)S(1)} %slice.30), channel_id=1, source_target_pairs={{0,17},{1,16},{16,1},{17,0},{2,19},{3,18},{18,3},{19,2},{4,21},{5,... | collective-permute-start | bytes 110600 | tf_op jit(solution)/shard_map/ppermute | solution.py:336
  78.4 1.4 %collective-permute-done.20 = bf16[32,576]{1,0:T(8,128)(2,1)S(1)} collective-permute-done((bf16[32,576]{1,0:T(8,128)(2,1)S(1)}, bf16[32,576]{1,0:T(8,128)(2,1)S(1)}, u32[]{:S(2)}, u32[]{:S(2)}) %collective-permute-start.20) | collective-permute-done | bytes 36896 | tf_op jit(solution)/shard_map/ppermute | solution.py:336
  79.8 2.3 %collective-permute-done.18 = bf16[32,896]{1,0:T(8,128)(2,1)S(1)} collective-permute-done((bf16[32,896]{1,0:T(8,128)(2,1)S(1)}, bf16[32,896]{1,0:T(8,128)(2,1)S(1)}, u32[]{:S(2)}, u32[]{:S(2)}) %collective-permute-start.18) | collective-permute-done | bytes 57376 | tf_op jit(solution)/shard_map/ppermute | solution.py:336
  83.4 1.6 %fusion.3 = f32[256,1024]{1,0:T(8,128)} fusion(bf16[1024,64]{0,1:T(8,128)(2,1)S(1)} %copy-done.6, f32[64,128]{1,0:T(8,128)S(1)} %collective-permute-done.22, f32[32,128]{1,0:T(8,128)S(1)} %get-tuple-element.134, f32[32,128]{1,0:T(8,128)S(1)} %get-tuple-element.133, pred[]{:T(512)S(6)} %eq.10), kind=kOutput, calls=%fused_computation.15 | convolution fusion | flops 201408512 | bytes 1245185 | tf_op jit(solution)/shard_map/dot_general | solution.py:446
  (76 shorter events, 15.1 us)
Async XLA Ops:
  0.6 41.1 %copy-start = (bf16[256,1024]{1,0:T(8,128)(2,1)S(1)}, bf16[256,1024]{1,0:T(8,128)(2,1)}, u32[]{:S(2)}) copy-start(bf16[256,1024]{1,0:T(8,128)(2,1)} %param.11) | copy-start | bytes 1572868
  0.6 2.8 %copy-start.1 = (bf16[3,1024,256]{2,1,0:T(8,128)(2,1)S(1)}, bf16[3,1024,256]{2,1,0:T(8,128)(2,1)}, u32[]{:S(2)}) copy-start(bf16[3,1024,256]{2,1,0:T(8,128)(2,1)} %weight.1) | copy-start | bytes 4718596
  1.5 1.2 %copy-start.2 = (bf16[1,512,1024]{2,1,0:T(8,128)(2,1)S(1)}, bf16[1,512,1024]{2,1,0:T(8,128)(2,1)}, u32[]{:S(2)}) copy-start(bf16[1,512,1024]{2,1,0:T(8,128)(2,1)} %param.8) | copy-start | bytes 3145732
  4.9 3.2 %collective-permute-start = (bf16[2,128,512]{2,1,0:T(8,128)(2,1)S(1)}, bf16[2,128,512]{2,1,0:T(8,128)(2,1)S(1)}, u32[]{:S(2)}, u32[]{:S(2)}) collective-permute-start(bf16[2,128,512]{2,1,0:T(8,128)(2,1)S(1)} %get-tuple-element.73), channel_id=1, source_target_pairs={{0,2},{2,0},{4,6},{6,4},{8,10},{10,8},{12,14},{14,12},{1,3},{3,1},... | collective-permute-start | bytes 786440 | tf_op jit(solution)/shard_map/ppermute | solution.py:287
  5.4 10.8 %collective-permute-start.3 = (bf16[2,128,512]{2,1,0:T(8,128)(2,1)S(1)}, bf16[2,128,512]{2,1,0:T(8,128)(2,1)S(1)}, u32[]{:S(2)}, u32[]{:S(2)}) collective-permute-start(bf16[2,128,512]{2,1,0:T(8,128)(2,1)S(1)} %get-tuple-element.75.block), channel_id=1, source_target_pairs={{0,4},{2,6},{4,12},{6,14},{8,0},{10,2},{12,8},{14,10},{1,5},{3,7},... | collective-permute-start | bytes 786440 | tf_op jit(solution)/shard_map/ppermute | solution.py:315
  8.1 13.8 %collective-permute-start.1 = (bf16[2,128,512]{2,1,0:T(8,128)(2,1)S(1)}, bf16[2,128,512]{2,1,0:T(8,128)(2,1)S(1)}, u32[]{:S(2)}, u32[]{:S(2)}) collective-permute-start(bf16[2,128,512]{2,1,0:T(8,128)(2,1)S(1)} %collective-permute-done.block), channel_id=1, source_target_pairs={{0,4},{2,6},{4,12},{6,14},{8,0},{10,2},{12,8},{14,10},{1,5},{3,7},... | collective-permute-start | bytes 786440 | tf_op jit(solution)/shard_map/ppermute | solution.py:315
  11.7 1.4 %collective-permute-start.2 = (bf16[2,64,512]{2,1,0:T(8,128)(2,1)S(1)}, bf16[2,64,512]{2,1,0:T(8,128)(2,1)S(1)}, u32[]{:S(2)}, u32[]{:S(2)}) collective-permute-start(bf16[2,64,512]{2,1,0:T(8,128)(2,1)S(1)} %get-tuple-element.74), channel_id=1, source_target_pairs={{0,2},{2,0},{4,6},{6,4},{8,10},{10,8},{12,14},{14,12},{1,3},{3,1},... | collective-permute-start | bytes 393224 | tf_op jit(solution)/shard_map/ppermute | solution.py:287
  16.2 11.2 %collective-permute-start.5 = (bf16[2,128,512]{2,1,0:T(8,128)(2,1)S(1)}, bf16[2,128,512]{2,1,0:T(8,128)(2,1)S(1)}, u32[]{:S(2)}, u32[]{:S(2)}) collective-permute-start(bf16[2,128,512]{2,1,0:T(8,128)(2,1)S(1)} %collective-permute-done.3.block), channel_id=1, source_target_pairs={{0,4},{2,6},{4,12},{6,14},{8,0},{10,2},{12,8},{14,10},{1,5},{3,7},... | collective-permute-start | bytes 786440 | tf_op jit(solution)/shard_map/ppermute | solution.py:315
  21.8 11.2 %collective-permute-start.4 = (bf16[2,128,512]{2,1,0:T(8,128)(2,1)S(1)}, bf16[2,128,512]{2,1,0:T(8,128)(2,1)S(1)}, u32[]{:S(2)}, u32[]{:S(2)}) collective-permute-start(bf16[2,128,512]{2,1,0:T(8,128)(2,1)S(1)} %collective-permute-done.1.block), channel_id=1, source_target_pairs={{0,4},{2,6},{4,12},{6,14},{8,0},{10,2},{12,8},{14,10},{1,5},{3,7},... | collective-permute-start | bytes 786440 | tf_op jit(solution)/shard_map/ppermute | solution.py:315
  23.0 12.2 %copy-start.7 = (f32[1,2,2,128]{3,2,1,0:T(2,128)S(1)}, f32[1,2,2,128]{3,2,1,0:T(2,128)}, u32[]{:S(2)}) copy-start(f32[1,2,2,128]{3,2,1,0:T(2,128)} %param.15) | copy-start | bytes 6148
  25.0 16.3 %copy-start.3 = (bf16[1,512,1024]{2,1,0:T(8,128)(2,1)S(1)}, bf16[1,512,1024]{2,1,0:T(8,128)(2,1)}, u32[]{:S(2)}) copy-start(bf16[1,512,1024]{2,1,0:T(8,128)(2,1)} %param.8) | copy-start | bytes 3145732
  25.0 16.3 %copy-start.6 = (bf16[1024,64]{0,1:T(8,128)(2,1)S(1)}, bf16[1024,64]{0,1:T(8,128)(2,1)}, u32[]{:S(2)}) copy-start(bf16[1024,64]{0,1:T(8,128)(2,1)} %param.12) | copy-start | bytes 393220
  27.5 16.9 %collective-permute-start.8 = (bf16[2,128,512]{2,1,0:T(8,128)(2,1)S(1)}, bf16[2,128,512]{2,1,0:T(8,128)(2,1)S(1)}, u32[]{:S(2)}, u32[]{:S(2)}) collective-permute-start(bf16[2,128,512]{2,1,0:T(8,128)(2,1)S(1)} %collective-permute-done.5.block), channel_id=1, source_target_pairs={{0,4},{2,6},{4,12},{6,14},{8,0},{10,2},{12,8},{14,10},{1,5},{3,7},... | collective-permute-start | bytes 786440 | tf_op jit(solution)/shard_map/ppermute | solution.py:315
  33.1 8.9 %copy-start.4 = (bf16[2,64,576]{2,1,0:T(8,128)(2,1)S(1)}, bf16[2,64,576]{2,1,0:T(8,128)(2,1)}, u32[]{:S(2)}) copy-start(bf16[2,64,576]{2,1,0:T(8,128)(2,1)} %weight.2) | copy-start | bytes 442372
  35.1 9.1 %collective-permute-start.9 = (f32[2,2,128]{2,1,0:T(2,128)S(1)}, f32[2,2,128]{2,1,0:T(2,128)S(1)}, u32[]{:S(2)}, u32[]{:S(2)}) collective-permute-start(f32[2,2,128]{2,1,0:T(2,128)S(1)} %bitcast.27), channel_id=1, source_target_pairs={{0,1},{1,0},{2,3},{3,2},{4,5},{5,4},{6,7},{7,6},{8,9},{9,8},{10,11... | collective-permute-start | bytes 6152 | tf_op jit(solution)/shard_map/ppermute | solution.py:287
  37.0 9.4 %collective-permute-start.7 = (bf16[2,128,256]{2,1,0:T(8,128)(2,1)S(1)}, bf16[2,128,256]{2,1,0:T(8,128)(2,1)S(1)}, u32[]{:S(2)}, u32[]{:S(2)}) collective-permute-start(bf16[2,128,256]{2,1,0:T(8,128)(2,1)S(1)} %get-tuple-element.131), channel_id=1, source_target_pairs={{0,4},{2,6},{4,12},{6,14},{8,0},{10,2},{12,8},{14,10},{1,5},{3,7},... | collective-permute-start | bytes 393224 | tf_op jit(solution)/shard_map/ppermute | solution.py:315
  37.9 10.0 %collective-permute-start.6 = (bf16[2,128,256]{2,1,0:T(8,128)(2,1)S(1)}, bf16[2,128,256]{2,1,0:T(8,128)(2,1)S(1)}, u32[]{:S(2)}, u32[]{:S(2)}) collective-permute-start(bf16[2,128,256]{2,1,0:T(8,128)(2,1)S(1)} %get-tuple-element.132), channel_id=1, source_target_pairs={{0,4},{2,6},{4,12},{6,14},{8,0},{10,2},{12,8},{14,10},{1,5},{3,7},... | collective-permute-start | bytes 393224 | tf_op jit(solution)/shard_map/ppermute | solution.py:315
  47.9 15.0 %copy-start.5 = (bf16[2,64]{1,0:T(2,128)(2,1)S(1)}, bf16[2,64]{1,0:T(2,128)(2,1)}, u32[]{:S(2)}) copy-start(bf16[2,64]{1,0:T(2,128)(2,1)} %head.1) | copy-start | bytes 772
  48.9 1.4 %collective-permute-start.10 = (f32[64,512]{1,0:T(8,128)S(1)}, f32[64,512]{1,0:T(8,128)S(1)}, u32[]{:S(2)}, u32[]{:S(2)}) collective-permute-start(f32[64,512]{1,0:T(8,128)S(1)} %get-tuple-element.121), channel_id=1, source_target_pairs={{0,2},{2,0},{4,6},{6,4},{8,10},{10,8},{12,14},{14,12},{1,3},{3,1},... | collective-permute-start | bytes 393224 | tf_op jit(solution)/shard_map/ppermute | solution.py:287
  50.3 4.3 %collective-permute-start.11 = (bf16[64,512]{1,0:T(8,128)(2,1)S(1)}, bf16[64,512]{1,0:T(8,128)(2,1)S(1)}, u32[]{:S(2)}, u32[]{:S(2)}) collective-permute-start(bf16[64,512]{1,0:T(8,128)(2,1)S(1)} %add_convert_fusion.1), channel_id=1, source_target_pairs={{0,1},{1,0},{2,3},{3,2},{4,5},{5,4},{6,7},{7,6},{8,9},{9,8},{10,11... | collective-permute-start | bytes 196616 | tf_op jit(solution)/shard_map/ppermute | solution.py:287
  54.7 1.3 %collective-permute-start.12 = (bf16[80,512]{1,0:T(8,128)(2,1)S(1)}, bf16[80,512]{1,0:T(8,128)(2,1)S(1)}, u32[]{:S(2)}, u32[]{:S(2)}) collective-permute-start(bf16[80,512]{1,0:T(8,128)(2,1)S(1)} %pad_maximum_fusion.1), channel_id=1, source_target_pairs={{0,2},{2,0},{4,6},{6,4},{8,10},{10,8},{12,14},{14,12},{1,3},{3,1},... | collective-permute-start | bytes 245768 | tf_op jit(solution)/shard_map/ppermute | solution.py:287
  56.0 5.4 %collective-permute-start.13 = (bf16[80,1024]{1,0:T(8,128)(2,1)S(1)}, bf16[80,1024]{1,0:T(8,128)(2,1)S(1)}, u32[]{:S(2)}, u32[]{:S(2)}) collective-permute-start(bf16[80,1024]{1,0:T(8,128)(2,1)S(1)} %pad_maximum_fusion.chip_map), channel_id=1, source_target_pairs={{0,4},{1,5},{2,3},{3,2},{4,0},{5,1},{6,10},{7,11},{8,12},{9,13},{1... | collective-permute-start | bytes 491528 | tf_op jit(solution)/shard_map/ppermute | solution.py:305
  61.4 1.4 %collective-permute-start.14 = (bf16[80,1024]{1,0:T(8,128)(2,1)S(1)}, bf16[80,1024]{1,0:T(8,128)(2,1)S(1)}, u32[]{:S(2)}, u32[]{:S(2)}) collective-permute-start(bf16[80,1024]{1,0:T(8,128)(2,1)S(1)} %collective-permute-done.13.near), channel_id=1, source_target_pairs={{0,2},{2,0},{4,6},{6,4},{8,10},{10,8},{12,14},{14,12},{1,3},{3,1},... | collective-permute-start | bytes 491528 | tf_op jit(solution)/shard_map/ppermute | solution.py:287
  66.4 7.3 %collective-permute-start.15 = (bf16[32,896]{1,0:T(8,128)(2,1)S(1)}, bf16[32,896]{1,0:T(8,128)(2,1)S(1)}, u32[]{:S(2)}, u32[]{:S(2)}) collective-permute-start(bf16[32,896]{1,0:T(8,128)(2,1)S(1)} %fusion.14), channel_id=1, source_target_pairs={{0,8},{2,10},{4,12},{6,14},{8,0},{10,2},{12,4},{14,6},{1,9},{3,11}... | collective-permute-start | bytes 172040 | tf_op jit(solution)/shard_map/ppermute | solution.py:293
  66.5 7.2 %collective-permute-start.16 = (bf16[32,896]{1,0:T(8,128)(2,1)S(1)}, bf16[32,896]{1,0:T(8,128)(2,1)S(1)}, u32[]{:S(2)}, u32[]{:S(2)}) collective-permute-start(bf16[32,896]{1,0:T(8,128)(2,1)S(1)} %fusion.14), channel_id=1, source_target_pairs={{0,4},{2,6},{4,8},{6,10},{8,12},{10,14},{12,0},{14,2},{1,5},{3,7},... | collective-permute-start | bytes 172040 | tf_op jit(solution)/shard_map/ppermute | solution.py:293
  67.8 6.3 %collective-permute-start.17 = (bf16[32,896]{1,0:T(8,128)(2,1)S(1)}, bf16[32,896]{1,0:T(8,128)(2,1)S(1)}, u32[]{:S(2)}, u32[]{:S(2)}) collective-permute-start(bf16[32,896]{1,0:T(8,128)(2,1)S(1)} %fusion.14), channel_id=1, source_target_pairs={{0,12},{2,14},{4,0},{6,2},{8,4},{10,6},{12,8},{14,10},{1,13},{3,15... | collective-permute-start | bytes 172040 | tf_op jit(solution)/shard_map/ppermute | solution.py:293
  74.2 4.2 %collective-permute-start.19 = (bf16[32,576]{1,0:T(8,128)(2,1)S(1)}, bf16[32,576]{1,0:T(8,128)(2,1)S(1)}, u32[]{:S(2)}, u32[]{:S(2)}) collective-permute-start(bf16[32,576]{1,0:T(8,128)(2,1)S(1)} %slice.30), channel_id=1, source_target_pairs={{0,1},{1,0},{16,17},{17,16},{2,3},{3,2},{18,19},{19,18},{4,5},{5,4... | collective-permute-start | bytes 110600 | tf_op jit(solution)/shard_map/ppermute | solution.py:336
  74.8 5.0 %collective-permute-start.20 = (bf16[32,576]{1,0:T(8,128)(2,1)S(1)}, bf16[32,576]{1,0:T(8,128)(2,1)S(1)}, u32[]{:S(2)}, u32[]{:S(2)}) collective-permute-start(bf16[32,576]{1,0:T(8,128)(2,1)S(1)} %slice.30), channel_id=1, source_target_pairs={{0,17},{1,16},{16,1},{17,0},{2,19},{3,18},{18,3},{19,2},{4,21},{5,... | collective-permute-start | bytes 110600 | tf_op jit(solution)/shard_map/ppermute | solution.py:336
  77.9 4.2 %collective-permute-start.18 = (bf16[32,896]{1,0:T(8,128)(2,1)S(1)}, bf16[32,896]{1,0:T(8,128)(2,1)S(1)}, u32[]{:S(2)}, u32[]{:S(2)}) collective-permute-start(bf16[32,896]{1,0:T(8,128)(2,1)S(1)} %add_convert_fusion.2), channel_id=1, source_target_pairs={{0,16},{1,17},{16,0},{17,1},{2,18},{3,19},{18,2},{19,3},{4,20},{5,... | collective-permute-start | bytes 172040 | tf_op jit(solution)/shard_map/ppermute | solution.py:336
  82.1 1.3 %collective-permute-start.22 = (f32[64,128]{1,0:T(8,128)S(1)}, f32[64,128]{1,0:T(8,128)S(1)}, u32[]{:S(2)}, u32[]{:S(2)}) collective-permute-start(f32[64,128]{1,0:T(8,128)S(1)} %pad_maximum_fusion.2), channel_id=1, source_target_pairs={{0,2},{2,0},{4,6},{6,4},{8,10},{10,8},{12,14},{14,12},{1,3},{3,1},... | collective-permute-start | bytes 98312 | tf_op jit(solution)/shard_map/ppermute | solution.py:287
  82.2 2.8 %collective-permute-start.21 = (f32[64,576]{1,0:T(8,128)S(1)}, f32[64,576]{1,0:T(8,128)S(1)}, u32[]{:S(2)}, u32[]{:S(2)}) collective-permute-start(f32[64,576]{1,0:T(8,128)S(1)} %maximum_select_fusion.2), channel_id=1, source_target_pairs={{0,2},{2,0},{4,6},{6,4},{8,10},{10,8},{12,14},{14,12},{1,3},{3,1},... | collective-permute-start | bytes 442376 | tf_op jit(solution)/shard_map/ppermute | solution.py:287

commit v5 on v3

--- a/solution.py
+++ b/solution.py
@@ -30,30 +30,27 @@
     return high, mid, low
 
 
-def normalize_kernel(tokens, gain, normed):
-    values = tokens[...].astype(F32)
-    center = values - jnp.mean(values, axis=-1, keepdims=True)
-    spread = jnp.mean(center * center, axis=-1, keepdims=True)
-    normed[...] = (center * lax.rsqrt(spread + EPSILON) * gain[...]).astype(BF16)
-
-
-def normalize(tokens, gain):
-    return pl.pallas_call(
-        normalize_kernel,
-        out_shape=jax.ShapeDtypeStruct(tokens.shape, BF16),
-        in_specs=[VMEM, VMEM],
-        out_specs=VMEM,
-        compiler_params=PARAMS,
-        name="normalize",
-    )(tokens, gain)
-
-
-def project_kernel(members, place, normed, weight, mine, theirs, turned):
+def project_kernel(members, raw, place, rows, *refs):
+    if raw:
+        gain, weight, normed, mine, theirs, parts, turned, sems = refs
+    else:
+        weight, mine, theirs, parts, turned, sems = refs
+    copies = [
+        pltpu.make_async_copy(weight.at[member], parts.at[at], sems.at[at]) for at, member in enumerate(members)
+    ]
+    for copy in copies:
+        copy.start()
+    if raw:
+        values = rows[...].astype(F32)
+        center = values - jnp.mean(values, axis=-1, keepdims=True)
+        spread = jnp.mean(center * center, axis=-1, keepdims=True)
+        normed[...] = (center * lax.rsqrt(spread + EPSILON) * gain[...]).astype(BF16)
+        rows = normed
     core = place[0]
     kept = mine.shape[0] * HEAD
-    rows = normed[...]
     for at, member in enumerate(members):
-        product = dot(rows, weight[member]).astype(BF16)
+        copies[at].wait()
+        product = dot(rows[...], parts[at]).astype(BF16)
         if member == 0:
             product = product * jnp.asarray(1.0 / HEAD**0.5, BF16)
         turned[at] = product.T
@@ -63,18 +60,23 @@
                 out[head, at * HEAD : (at + 1) * HEAD, :] = turned[at, pl.ds(start, HEAD), :]
 
 
-def project(members, place, normed, weight):
-    count, length = weight.shape[2] // HEAD // 2, normed.shape[0]
-    shape = jax.ShapeDtypeStruct((count, len(members) * HEAD, length), BF16)
-    return pl.pallas_call(
-        functools.partial(project_kernel, members),
-        out_shape=(shape, shape),
-        in_specs=[SMEM, VMEM, VMEM],
-        out_specs=(VMEM,) * 2,
-        scratch_shapes=[pltpu.VMEM((len(members), weight.shape[2], length), BF16)],
+def project(members, place, rows, weight, gain=None):
+    length, width = rows.shape[0], weight.shape[2]
+    shape = jax.ShapeDtypeStruct((width // HEAD // 2, len(members) * HEAD, length), BF16)
+    raw = gain is not None
+    return pl.pallas_call(
+        functools.partial(project_kernel, members, raw),
+        out_shape=((jax.ShapeDtypeStruct(rows.shape, BF16),) if raw else ()) + (shape, shape),
+        in_specs=[SMEM, VMEM] + [VMEM] * raw + [pl.BlockSpec(memory_space=pltpu.HBM)],
+        out_specs=(VMEM,) * (2 + raw),
+        scratch_shapes=[
+            pltpu.VMEM((len(members),) + weight.shape[1:], BF16),
+            pltpu.VMEM((len(members), width, length), BF16),
+            pltpu.SemaphoreType.DMA((len(members),)),
+        ],
         compiler_params=PARAMS,
         name="project",
-    )(place, normed, weight)
+    )(place, rows, *((gain,) if raw else ()), weight)
 
 
 def attend(queries, block, running, best):
@@ -172,6 +174,27 @@
         compiler_params=PARAMS,
         name="arrange",
     )(weight)
+
+
+def fold_kernel(place, out_weight, readout_weight, folded, rows, sem):
+    kept = rows.shape[0]
+    start = pl.multiple_of(place[0] * kept, kept)
+    copy = pltpu.make_async_copy(out_weight.at[pl.ds(start, kept)], rows, sem.at[0])
+    copy.start()
+    copy.wait()
+    folded[...] = dot(rows[...], readout_weight[...]).T
+
+
+def fold(place, out_weight, readout_weight, kept):
+    return pl.pallas_call(
+        fold_kernel,
+        out_shape=jax.ShapeDtypeStruct((readout_weight.shape[1], kept), F32),
+        in_specs=[SMEM, pl.BlockSpec(memory_space=pltpu.HBM), VMEM],
+        out_specs=VMEM,
+        scratch_shapes=[pltpu.VMEM((kept, out_weight.shape[1]), BF16), pltpu.SemaphoreType.DMA((1,))],
+        compiler_params=PARAMS,
+        name="fold",
+    )(place, pltpu.with_memory_space_constraint(out_weight, pltpu.HBM), readout_weight)
 
 
 def turned(values, step):
@@ -360,11 +383,9 @@
     place = jnp.stack([core, half, chip_row, lax.rem(tok_at // 2, 2)]).astype(jnp.int32)
     cols = cols_dev * col_count
 
-    gain, qkv_weight, out_weight = lax.optimization_barrier(
-        (ln_gain.astype(F32).reshape(1, -1), qkv_weight, out_weight)
-    )
-    normed = normalize(frame_rows, gain)
-    own_keyed, their_keyed = project((1, 2), place, normed, qkv_weight)
+    qkv_weight = pltpu.with_memory_space_constraint(qkv_weight, pltpu.HBM)
+    gain = ln_gain.astype(F32).reshape(1, -1)
+    normed, own_keyed, their_keyed = project((1, 2), place, frame_rows, qkv_weight, gain)
     own_keyed, their_keyed, normed = lax.optimization_barrier((own_keyed, their_keyed, normed))
     got_keyed = swapped(their_keyed, "tok")
     own_queries, their_queries = project((0,), place, normed, qkv_weight)
@@ -373,8 +394,7 @@
 
     def prepare(conv_weight, out_weight, readout_weight, frame_rows):
         forward, backward = arrange(conv_weight)
-        own_out = lax.dynamic_slice_in_dim(out_weight, core * kept, kept, 0)
-        folded = lax.dot_general(readout_weight, own_out, (((0,), (1,)), ((), ())), preferred_element_type=F32)
+        folded = fold(place, out_weight, readout_weight, kept)
         direct = lax.dot_general(readout_weight, frame_rows, (((0,), (1,)), ((), ())), preferred_element_type=F32)
         return (forward, backward, folded, direct)
 
@@ -432,21 +452,19 @@
     pieces = gradient.shape[0] // rows
     folded_gradient = [gradient[at * rows : (at + 1) * rows] for at in range(pieces)]
     sent = jnp.concatenate([jnp.pad(sums, ((0, 0), (0, lanes - taps_wide))), *folded_gradient], axis=1)
-    summed, hologram = lax.optimization_barrier((everyone(sent, "tok", 2, chips), hologram))
+    summed = everyone(sent, "tok", 2, chips)
     own_terms = sum_frames(summed, False)
     far_terms = sum_frames(summed[:, :taps_wide], True)
     wide = gradient.shape[1]
     own_small = jnp.concatenate(
         [own_terms[:, lanes + at * wide : lanes + (at + 1) * wide] for at in range(pieces)], axis=0
     )
-    other_small = swapped(own_small, "tok")
-    small = in_order(core, own_small, other_small, 1)
+    small = in_order(core, own_small, swapped(own_small, "tok"), 1)
     out_grad = lax.dot_general(
         small, readout_weight.astype(F32), (((0,), (1,)), ((), ())), precision=lax.Precision.HIGHEST
     )
     layer_grad = in_order(half, own_terms[:, :taps_wide], far_terms, 0)
-    other_grad = swapped(layer_grad, "tok")
-    conv_grad = in_order(core, layer_grad[None], other_grad[None], 0)
+    conv_grad = in_order(core, layer_grad[None], swapped(layer_grad, "tok")[None], 0)
     return (hologram[None], conv_grad, out_grad)
 
 

time: 84.1 us -> 86.9 us (1.033)
  Pallas kernels: 23.8 us -> 27.7 us
  waiting for transfers between devices: 28.5 us -> 26.3 us
  starting transfers between devices: 24.5 us -> 25.7 us
    pallas_call x3, Pallas kernels: 3.09 us -> 7.02 us  [the longest x2 5.24 us: project(): pl.pallas_call(functools.partial(project_kernel, members, raw), out_shape...]
    ppermute x6, waiting for transfers between devices: 10.4 us -> 8.11 us  [round_ring(): lax.ppermute(values, 'tok', [(i, 2 * following[i // 2] + i % 2) for i in...]
  transfers between devices with their start and end apart: 22 -> 22, of which waited for: 17 -> 14; matrix products, arithmetic and copies ran while one was open for 4% -> 3% of each run, Pallas kernels for 20% -> 23%
where the time goes in v5:
time: 86.9 us; the launch traced here: 86.6 us
  Pallas kernels  27.7 us (32%)
  waiting for transfers between devices  26.3 us (30%)
  starting transfers between devices  25.7 us (30%)
  local copies, waits for them, and re-layouts  2.12 us (2%)
  matrix products  2.04 us (2%)
  other arithmetic  1.74 us (2%)
  between operations  1.02 us (1%)
    pallas_call x7, Pallas kernels, absorb(): pl.pallas_call(functools.partial(absorb_kernel, first), out_shape=shapes,...  14.3 us
    ppermute x6, starting transfers between devices, round_ring(): lax.ppermute(values, 'tok', [(i, 2 * following[i // 2] + i % 2) for i in...  9.94 us
    ppermute x9, waiting for transfers between devices, swapped(): return lax.ppermute(values, axis, [(i, i ^ 1) for i in range(size)])  8.34 us
    ppermute x6, waiting for transfers between devices, round_ring(): lax.ppermute(values, 'tok', [(i, 2 * following[i // 2] + i % 2) for i in...  8.11 us
    ppermute x3, starting transfers between devices, passed(): return lax.ppermute(values, axis, pairs)  5.77 us
    pallas_call x2, Pallas kernels, project(): pl.pallas_call(functools.partial(project_kernel, members, raw), out_shape...  5.24 us
    ppermute x9, starting transfers between devices, swapped(): return lax.ppermute(values, axis, [(i, i ^ 1) for i in range(size)])  4.11 us
    ppermute x3, waiting for transfers between devices, sum_frames(): moved = lax.ppermute(sent, ('dp', 'col'), pairs) if step or across else sent  3.65 us
  transfers between devices with their start and end apart: 22, of which 14 were waited for; matrix products, arithmetic and copies ran while one was open for 3% of the time, Pallas kernels for 23%

profile of v5, /device:TPU:0, one launch (start us, length us, event | category | flops | bytes accessed | tf_op | source)
XLA Modules:
  0.0 86.6 jit_solution(12486739773980396391)
XLA Ops:
  2.6 3.1 %project.2 = (bf16[512,1024]{1,0:T(8,128)(2,1)S(1)}, bf16[2,128,512]{2,1,0:T(8,128)(2,1)S(1)}, bf16[2,128,512]{2,1,0:T(8,128)(2,1)S(1)}) custom-call(s32[4]{0:T(128)S(1)} %pad_add_fusion.place, bf16[512,1024]{1,0:T(8,128)(2,1)S(1)} %bitcast.20, f32[1,1024]{1,0:T(1,128)S(1)} %bitcast.22, bf16[3,1024,256]{2,1,0:T(8,128)(2,1)} %refs_0_.1), custom_call_target="tpu_custom_call" | custom-call | tf_op jit(solution)/shard_map/project/pallas_call | solution.py:67
  6.3 2.6 %collective-permute-start.3 = (bf16[2,128,512]{2,1,0:T(8,128)(2,1)S(1)}, bf16[2,128,512]{2,1,0:T(8,128)(2,1)S(1)}, u32[]{:S(2)}, u32[]{:S(2)}) collective-permute-start(bf16[2,128,512]{2,1,0:T(8,128)(2,1)S(1)} %get-tuple-element.70.block), channel_id=1, source_target_pairs={{0,4},{2,6},{4,12},{6,14},{8,0},{10,2},{12,8},{14,10},{1,5},{3,7},... | collective-permute-start | bytes 786440 | tf_op jit(solution)/shard_map/ppermute | solution.py:338
  9.0 2.6 %collective-permute-start.1 = (bf16[2,128,512]{2,1,0:T(8,128)(2,1)S(1)}, bf16[2,128,512]{2,1,0:T(8,128)(2,1)S(1)}, u32[]{:S(2)}, u32[]{:S(2)}) collective-permute-start(bf16[2,128,512]{2,1,0:T(8,128)(2,1)S(1)} %collective-permute-done.block), channel_id=1, source_target_pairs={{0,4},{2,6},{4,12},{6,14},{8,0},{10,2},{12,8},{14,10},{1,5},{3,7},... | collective-permute-start | bytes 786440 | tf_op jit(solution)/shard_map/ppermute | solution.py:338
  11.6 2.1 %project.3 = (bf16[2,64,512]{2,1,0:T(8,128)(2,1)S(1)}, bf16[2,64,512]{2,1,0:T(8,128)(2,1)S(1)}) custom-call(s32[4]{0:T(128)S(1)} %pad_add_fusion.place, bf16[512,1024]{1,0:T(8,128)(2,1)S(1)} %get-tuple-element.66.rows, bf16[3,1024,256]{2,1,0:T(8,128)(2,1)} %refs_0_.1), custom_call_target="tpu_custom_call" | custom-call | tf_op jit(solution)/shard_map/project/pallas_call | solution.py:67
  13.8 1.3 %collective-permute-done.2.got.queries = bf16[2,64,512]{2,1,0:T(8,128)(2,1)S(1)} collective-permute-done((bf16[2,64,512]{2,1,0:T(8,128)(2,1)S(1)}, bf16[2,64,512]{2,1,0:T(8,128)(2,1)S(1)}, u32[]{:S(2)}, u32[]{:S(2)}) %collective-permute-start.2) | collective-permute-done | bytes 131104 | tf_op jit(solution)/shard_map/ppermute | solution.py:310
  15.1 2.0 %absorb.7 = (f32[2,80,1024]{2,1,0:T(8,128)S(1)}, f32[2,8,1024]{2,1,0:T(8,128)S(1)}) custom-call(bf16[2,64,512]{2,1,0:T(8,128)(2,1)S(1)} %get-tuple-element.67.own.queries, bf16[2,64,512]{2,1,0:T(8,128)(2,1)S(1)} %collective-permute-done.2.got.queries, bf16[2,128,512]{2,1,0:T(8,128)(2,1)S(1)} %get-tuple-element.70.block), custom_call_target="tpu_custom_call" | custom-call | tf_op jit(solution)/shard_map/absorb/pallas_call | solution.py:117
  17.1 1.5 %collective-permute-start.5 = (bf16[2,128,512]{2,1,0:T(8,128)(2,1)S(1)}, bf16[2,128,512]{2,1,0:T(8,128)(2,1)S(1)}, u32[]{:S(2)}, u32[]{:S(2)}) collective-permute-start(bf16[2,128,512]{2,1,0:T(8,128)(2,1)S(1)} %collective-permute-done.3.block), channel_id=1, source_target_pairs={{0,4},{2,6},{4,12},{6,14},{8,0},{10,2},{12,8},{14,10},{1,5},{3,7},... | collective-permute-start | bytes 786440 | tf_op jit(solution)/shard_map/ppermute | solution.py:338
  18.6 2.1 %absorb.8 = (f32[2,80,1024]{2,1,0:T(8,128)S(1)}, f32[2,8,1024]{2,1,0:T(8,128)S(1)}) custom-call(bf16[2,64,512]{2,1,0:T(8,128)(2,1)S(1)} %get-tuple-element.67.own.queries, bf16[2,64,512]{2,1,0:T(8,128)(2,1)S(1)} %collective-permute-done.2.got.queries, ...), custom_call_target="tpu_custom_call", output_to_operand_aliasing={{0}: (3, {}), {1}: (4, {})} | custom-call | tf_op jit(solution)/shard_map/absorb/pallas_call | solution.py:117
  20.7 2.1 %collective-permute-done.1.block = bf16[2,128,512]{2,1,0:T(8,128)(2,1)S(1)} collective-permute-done((bf16[2,128,512]{2,1,0:T(8,128)(2,1)S(1)}, bf16[2,128,512]{2,1,0:T(8,128)(2,1)S(1)}, u32[]{:S(2)}, u32[]{:S(2)}) %collective-permute-start.1) | collective-permute-done | bytes 262176 | tf_op jit(solution)/shard_map/ppermute | solution.py:338
  23.9 2.0 %absorb.9 = (f32[2,80,1024]{2,1,0:T(8,128)S(1)}, f32[2,8,1024]{2,1,0:T(8,128)S(1)}) custom-call(bf16[2,64,512]{2,1,0:T(8,128)(2,1)S(1)} %get-tuple-element.67.own.queries, bf16[2,64,512]{2,1,0:T(8,128)(2,1)S(1)} %collective-permute-done.2.got.queries, ...), custom_call_target="tpu_custom_call", output_to_operand_aliasing={{0}: (3, {}), {1}: (4, {})} | custom-call | tf_op jit(solution)/shard_map/absorb/pallas_call | solution.py:117
  25.9 2.4 %collective-permute-done.5.block = bf16[2,128,512]{2,1,0:T(8,128)(2,1)S(1)} collective-permute-done((bf16[2,128,512]{2,1,0:T(8,128)(2,1)S(1)}, bf16[2,128,512]{2,1,0:T(8,128)(2,1)S(1)}, u32[]{:S(2)}, u32[]{:S(2)}) %collective-permute-start.5) | collective-permute-done | bytes 262176 | tf_op jit(solution)/shard_map/ppermute | solution.py:338
  29.5 2.0 %absorb.10 = (f32[2,80,1024]{2,1,0:T(8,128)S(1)}, f32[2,8,1024]{2,1,0:T(8,128)S(1)}) custom-call(bf16[2,64,512]{2,1,0:T(8,128)(2,1)S(1)} %get-tuple-element.67.own.queries, bf16[2,64,512]{2,1,0:T(8,128)(2,1)S(1)} %collective-permute-done.2.got.queries, ...), custom_call_target="tpu_custom_call", output_to_operand_aliasing={{0}: (3, {}), {1}: (4, {})} | custom-call | tf_op jit(solution)/shard_map/absorb/pallas_call | solution.py:117
  31.6 2.4 %collective-permute-done.4.block = bf16[2,128,512]{2,1,0:T(8,128)(2,1)S(1)} collective-permute-done((bf16[2,128,512]{2,1,0:T(8,128)(2,1)S(1)}, bf16[2,128,512]{2,1,0:T(8,128)(2,1)S(1)}, u32[]{:S(2)}, u32[]{:S(2)}) %collective-permute-start.4) | collective-permute-done | bytes 262176 | tf_op jit(solution)/shard_map/ppermute | solution.py:338
  34.0 2.0 %absorb.11 = (f32[2,80,1024]{2,1,0:T(8,128)S(1)}, f32[2,8,1024]{2,1,0:T(8,128)S(1)}) custom-call(bf16[2,64,512]{2,1,0:T(8,128)(2,1)S(1)} %get-tuple-element.67.own.queries, bf16[2,64,512]{2,1,0:T(8,128)(2,1)S(1)} %collective-permute-done.2.got.queries, ...), custom_call_target="tpu_custom_call", output_to_operand_aliasing={{0}: (3, {}), {1}: (4, {})} | custom-call | tf_op jit(solution)/shard_map/absorb/pallas_call | solution.py:117
  36.1 1.9 %collective-permute-start.8 = (f32[2,2,128]{2,1,0:T(2,128)S(1)}, f32[2,2,128]{2,1,0:T(2,128)S(1)}, u32[]{:S(2)}, u32[]{:S(2)}) collective-permute-start(f32[2,2,128]{2,1,0:T(2,128)S(1)} %bitcast.26), channel_id=1, source_target_pairs={{0,1},{1,0},{2,3},{3,2},{4,5},{5,4},{6,7},{7,6},{8,9},{9,8},{10,11... | collective-permute-start | bytes 6152 | tf_op jit(solution)/shard_map/ppermute | solution.py:310
  39.9 1.8 %fold.1.folded = f32[64,128]{1,0:T(8,128)S(1)} custom-call(s32[4]{0:T(128)S(1)} %pad_add_fusion.place, bf16[256,1024]{1,0:T(8,128)(2,1)} %out_weight, bf16[1024,64]{1,0:T(8,128)(2,1)S(1)} %copy.23.readout_weight), custom_call_target="tpu_custom_call" | custom-call | tf_op jit(solution)/shard_map/fold/pallas_call | solution.py:189
  41.6 2.1 %absorb.12 = (f32[2,80,1024]{2,1,0:T(8,128)S(1)}, f32[2,8,1024]{2,1,0:T(8,128)S(1)}) custom-call(bf16[2,64,512]{2,1,0:T(8,128)(2,1)S(1)} %get-tuple-element.67.own.queries, bf16[2,64,512]{2,1,0:T(8,128)(2,1)S(1)} %collective-permute-done.2.got.queries, ...), custom_call_target="tpu_custom_call", output_to_operand_aliasing={{0}: (3, {}), {1}: (4, {})} | custom-call | tf_op jit(solution)/shard_map/absorb/pallas_call | solution.py:117
  43.8 2.1 %absorb.13 = (f32[2,80,1024]{2,1,0:T(8,128)S(1)}, f32[2,8,1024]{2,1,0:T(8,128)S(1)}) custom-call(bf16[2,64,512]{2,1,0:T(8,128)(2,1)S(1)} %get-tuple-element.67.own.queries, bf16[2,64,512]{2,1,0:T(8,128)(2,1)S(1)} %collective-permute-done.2.got.queries, ...), custom_call_target="tpu_custom_call", output_to_operand_aliasing={{0}: (3, {}), {1}: (4, {})} | custom-call | tf_op jit(solution)/shard_map/absorb/pallas_call | solution.py:117
  47.0 1.3 %closing.3 = (bf16[128,512]{1,0:T(8,128)(2,1)S(1)}, f32[64,512]{1,0:T(8,128)S(1)}) custom-call(bf16[2,64,512]{2,1,0:T(8,128)(2,1)S(1)} %collective-permute-done.2.got.queries, bf16[2,128,512]{2,1,0:T(8,128)(2,1)S(1)} %collective-permute-done.6.block, f32[2,80,1024]{2,1,0:T(8,128)S(1)} %get-tuple-element.109.carried, ...), custom_call_target="tpu_custom_call" | custom-call | tf_op jit(solution)/shard_map/closing/pallas_call | solution.py:140
  48.4 1.3 %closing.2 = (bf16[128,512]{1,0:T(8,128)(2,1)S(1)}, f32[64,512]{1,0:T(8,128)S(1)}) custom-call(bf16[2,64,512]{2,1,0:T(8,128)(2,1)S(1)} %get-tuple-element.67.own.queries, bf16[2,128,512]{2,1,0:T(8,128)(2,1)S(1)} %collective-permute-done.6.block, f32[2,80,1024]{2,1,0:T(8,128)S(1)} %get-tuple-element.109.carried, ...), custom_call_target="tpu_custom_call" | custom-call | tf_op jit(solution)/shard_map/closing/pallas_call | solution.py:140
  50.5 3.7 %collective-permute-done.10 = bf16[64,512]{1,0:T(8,128)(2,1)S(1)} collective-permute-done((bf16[64,512]{1,0:T(8,128)(2,1)S(1)}, bf16[64,512]{1,0:T(8,128)(2,1)S(1)}, u32[]{:S(2)}, u32[]{:S(2)}) %collective-permute-start.10) | collective-permute-done | bytes 65568 | tf_op jit(solution)/shard_map/ppermute | solution.py:310
  55.7 2.3 %collective-permute-start.12 = (bf16[80,1024]{1,0:T(8,128)(2,1)S(1)}, bf16[80,1024]{1,0:T(8,128)(2,1)S(1)}, u32[]{:S(2)}, u32[]{:S(2)}) collective-permute-start(bf16[80,1024]{1,0:T(8,128)(2,1)S(1)} %pad_maximum_fusion.chip_map), channel_id=1, source_target_pairs={{0,4},{1,5},{2,3},{3,2},{4,0},{5,1},{6,10},{7,11},{8,12},{9,13},{1... | collective-permute-start | bytes 491528 | tf_op jit(solution)/shard_map/ppermute | solution.py:328
  58.0 3.3 %collective-permute-done.12.near = bf16[80,1024]{1,0:T(8,128)(2,1)S(1)} collective-permute-done((bf16[80,1024]{1,0:T(8,128)(2,1)S(1)}, bf16[80,1024]{1,0:T(8,128)(2,1)S(1)}, u32[]{:S(2)}, u32[]{:S(2)}) %collective-permute-start.12) | collective-permute-done | bytes 163872 | tf_op jit(solution)/shard_map/ppermute | solution.py:328
  61.3 1.4 %collective-permute-done.13.far = bf16[80,1024]{1,0:T(8,128)(2,1)S(1)} collective-permute-done((bf16[80,1024]{1,0:T(8,128)(2,1)S(1)}, bf16[80,1024]{1,0:T(8,128)(2,1)S(1)}, u32[]{:S(2)}, u32[]{:S(2)}) %collective-permute-start.13) | collective-permute-done | bytes 163872 | tf_op jit(solution)/shard_map/ppermute | solution.py:310
  62.7 3.5 %network.1 = (f32[2,1024]{1,0:T(2,128)S(1)}, f32[32,576]{1,0:T(8,128)S(1)}, f32[64,128]{1,0:T(8,128)S(1)}) custom-call(s32[4]{0:T(128)S(1)} %pad_add_fusion.place, bf16[80,1024]{1,0:T(8,128)(2,1)S(1)} %pad_maximum_fusion.chip_map, bf16[80,1024]{1,0:T(8,128)(2,1)S(1)} %collective-permute-done.12.near, bf16[80,1024]{1,0:T(8,128)(2,1)S(1)} %collective-permute-done.13.far, ...), custom_call_target="tpu_custom_call" | custom-call | tf_op jit(solution)/shard_map/network/pallas_call | solution.py:293
  66.3 1.9 %collective-permute-start.14 = (bf16[32,896]{1,0:T(8,128)(2,1)S(1)}, bf16[32,896]{1,0:T(8,128)(2,1)S(1)}, u32[]{:S(2)}, u32[]{:S(2)}) collective-permute-start(bf16[32,896]{1,0:T(8,128)(2,1)S(1)} %fusion.12), channel_id=1, source_target_pairs={{0,8},{2,10},{4,12},{6,14},{8,0},{10,2},{12,4},{14,6},{1,9},{3,11}... | collective-permute-start | bytes 172040 | tf_op jit(solution)/shard_map/ppermute | solution.py:316
  68.3 2.0 %collective-permute-start.15 = (bf16[32,896]{1,0:T(8,128)(2,1)S(1)}, bf16[32,896]{1,0:T(8,128)(2,1)S(1)}, u32[]{:S(2)}, u32[]{:S(2)}) collective-permute-start(bf16[32,896]{1,0:T(8,128)(2,1)S(1)} %fusion.12), channel_id=1, source_target_pairs={{0,4},{2,6},{4,8},{6,10},{8,12},{10,14},{12,0},{14,2},{1,5},{3,7},... | collective-permute-start | bytes 172040 | tf_op jit(solution)/shard_map/ppermute | solution.py:316
  70.3 1.8 %collective-permute-start.16 = (bf16[32,896]{1,0:T(8,128)(2,1)S(1)}, bf16[32,896]{1,0:T(8,128)(2,1)S(1)}, u32[]{:S(2)}, u32[]{:S(2)}) collective-permute-start(bf16[32,896]{1,0:T(8,128)(2,1)S(1)} %fusion.12), channel_id=1, source_target_pairs={{0,12},{2,14},{4,0},{6,2},{8,4},{10,6},{12,8},{14,10},{1,13},{3,15... | collective-permute-start | bytes 172040 | tf_op jit(solution)/shard_map/ppermute | solution.py:316
  72.1 2.7 %collective-permute-done.15 = bf16[32,896]{1,0:T(8,128)(2,1)S(1)} collective-permute-done((bf16[32,896]{1,0:T(8,128)(2,1)S(1)}, bf16[32,896]{1,0:T(8,128)(2,1)S(1)}, u32[]{:S(2)}, u32[]{:S(2)}) %collective-permute-start.15) | collective-permute-done | bytes 57376 | tf_op jit(solution)/shard_map/ppermute | solution.py:316
  75.6 2.4 %collective-permute-start.19 = (bf16[32,576]{1,0:T(8,128)(2,1)S(1)}, bf16[32,576]{1,0:T(8,128)(2,1)S(1)}, u32[]{:S(2)}, u32[]{:S(2)}) collective-permute-start(bf16[32,576]{1,0:T(8,128)(2,1)S(1)} %slice.30), channel_id=1, source_target_pairs={{0,17},{1,16},{16,1},{17,0},{2,19},{3,18},{18,3},{19,2},{4,21},{5,... | collective-permute-start | bytes 110600 | tf_op jit(solution)/shard_map/ppermute | solution.py:359
  80.5 2.4 %collective-permute-done.17 = bf16[32,896]{1,0:T(8,128)(2,1)S(1)} collective-permute-done((bf16[32,896]{1,0:T(8,128)(2,1)S(1)}, bf16[32,896]{1,0:T(8,128)(2,1)S(1)}, u32[]{:S(2)}, u32[]{:S(2)}) %collective-permute-start.17) | collective-permute-done | bytes 57376 | tf_op jit(solution)/shard_map/ppermute | solution.py:359
  84.2 1.6 %fusion.1 = f32[256,1024]{1,0:T(8,128)} fusion(bf16[1024,64]{0,1:T(8,128)(2,1)S(1)} %copy-done.4, f32[64,128]{1,0:T(8,128)S(1)} %collective-permute-done.21, f32[32,128]{1,0:T(8,128)S(1)} %get-tuple-element.124, f32[32,128]{1,0:T(8,128)S(1)} %get-tuple-element.123, pred[]{:T(512)S(6)} %eq.10), kind=kOutput, calls=%fused_computation.13 | convolution fusion | flops 201408512 | bytes 1245185 | tf_op jit(solution)/shard_map/dot_general | solution.py:463
  (68 shorter events, 15.6 us)
Async XLA Ops:
  1.4 1.2 %copy-start = (bf16[1,512,1024]{2,1,0:T(8,128)(2,1)S(1)}, bf16[1,512,1024]{2,1,0:T(8,128)(2,1)}, u32[]{:S(2)}) copy-start(bf16[1,512,1024]{2,1,0:T(8,128)(2,1)} %param.8) | copy-start | bytes 3145732
  5.8 3.2 %collective-permute-start = (bf16[2,128,512]{2,1,0:T(8,128)(2,1)S(1)}, bf16[2,128,512]{2,1,0:T(8,128)(2,1)S(1)}, u32[]{:S(2)}, u32[]{:S(2)}) collective-permute-start(bf16[2,128,512]{2,1,0:T(8,128)(2,1)S(1)} %get-tuple-element.68), channel_id=1, source_target_pairs={{0,2},{2,0},{4,6},{6,4},{8,10},{10,8},{12,14},{14,12},{1,3},{3,1},... | collective-permute-start | bytes 786440 | tf_op jit(solution)/shard_map/ppermute | solution.py:310
  6.3 10.8 %collective-permute-start.3 = (bf16[2,128,512]{2,1,0:T(8,128)(2,1)S(1)}, bf16[2,128,512]{2,1,0:T(8,128)(2,1)S(1)}, u32[]{:S(2)}, u32[]{:S(2)}) collective-permute-start(bf16[2,128,512]{2,1,0:T(8,128)(2,1)S(1)} %get-tuple-element.70.block), channel_id=1, source_target_pairs={{0,4},{2,6},{4,12},{6,14},{8,0},{10,2},{12,8},{14,10},{1,5},{3,7},... | collective-permute-start | bytes 786440 | tf_op jit(solution)/shard_map/ppermute | solution.py:338
  9.0 13.8 %collective-permute-start.1 = (bf16[2,128,512]{2,1,0:T(8,128)(2,1)S(1)}, bf16[2,128,512]{2,1,0:T(8,128)(2,1)S(1)}, u32[]{:S(2)}, u32[]{:S(2)}) collective-permute-start(bf16[2,128,512]{2,1,0:T(8,128)(2,1)S(1)} %collective-permute-done.block), channel_id=1, source_target_pairs={{0,4},{2,6},{4,12},{6,14},{8,0},{10,2},{12,8},{14,10},{1,5},{3,7},... | collective-permute-start | bytes 786440 | tf_op jit(solution)/shard_map/ppermute | solution.py:338
  13.7 1.4 %collective-permute-start.2 = (bf16[2,64,512]{2,1,0:T(8,128)(2,1)S(1)}, bf16[2,64,512]{2,1,0:T(8,128)(2,1)S(1)}, u32[]{:S(2)}, u32[]{:S(2)}) collective-permute-start(bf16[2,64,512]{2,1,0:T(8,128)(2,1)S(1)} %get-tuple-element.69), channel_id=1, source_target_pairs={{0,2},{2,0},{4,6},{6,4},{8,10},{10,8},{12,14},{14,12},{1,3},{3,1},... | collective-permute-start | bytes 393224 | tf_op jit(solution)/shard_map/ppermute | solution.py:310
  17.1 11.2 %collective-permute-start.5 = (bf16[2,128,512]{2,1,0:T(8,128)(2,1)S(1)}, bf16[2,128,512]{2,1,0:T(8,128)(2,1)S(1)}, u32[]{:S(2)}, u32[]{:S(2)}) collective-permute-start(bf16[2,128,512]{2,1,0:T(8,128)(2,1)S(1)} %collective-permute-done.3.block), channel_id=1, source_target_pairs={{0,4},{2,6},{4,12},{6,14},{8,0},{10,2},{12,8},{14,10},{1,5},{3,7},... | collective-permute-start | bytes 786440 | tf_op jit(solution)/shard_map/ppermute | solution.py:338
  22.8 11.2 %collective-permute-start.4 = (bf16[2,128,512]{2,1,0:T(8,128)(2,1)S(1)}, bf16[2,128,512]{2,1,0:T(8,128)(2,1)S(1)}, u32[]{:S(2)}, u32[]{:S(2)}) collective-permute-start(bf16[2,128,512]{2,1,0:T(8,128)(2,1)S(1)} %collective-permute-done.1.block), channel_id=1, source_target_pairs={{0,4},{2,6},{4,12},{6,14},{8,0},{10,2},{12,8},{14,10},{1,5},{3,7},... | collective-permute-start | bytes 786440 | tf_op jit(solution)/shard_map/ppermute | solution.py:338
  23.9 12.2 %copy-start.5 = (f32[1,2,2,128]{3,2,1,0:T(2,128)S(1)}, f32[1,2,2,128]{3,2,1,0:T(2,128)}, u32[]{:S(2)}) copy-start(f32[1,2,2,128]{3,2,1,0:T(2,128)} %param.15) | copy-start | bytes 6148
  23.9 14.1 %copy-start.1 = (bf16[1,512,1024]{2,1,0:T(8,128)(2,1)S(1)}, bf16[1,512,1024]{2,1,0:T(8,128)(2,1)}, u32[]{:S(2)}) copy-start(bf16[1,512,1024]{2,1,0:T(8,128)(2,1)} %param.8) | copy-start | bytes 3145732
  23.9 14.1 %copy-start.4 = (bf16[1024,64]{0,1:T(8,128)(2,1)S(1)}, bf16[1024,64]{0,1:T(8,128)(2,1)}, u32[]{:S(2)}) copy-start(bf16[1024,64]{0,1:T(8,128)(2,1)} %param.12) | copy-start | bytes 393220
  28.4 15.4 %collective-permute-start.7 = (bf16[2,128,512]{2,1,0:T(8,128)(2,1)S(1)}, bf16[2,128,512]{2,1,0:T(8,128)(2,1)S(1)}, u32[]{:S(2)}, u32[]{:S(2)}) collective-permute-start(bf16[2,128,512]{2,1,0:T(8,128)(2,1)S(1)} %collective-permute-done.5.block), channel_id=1, source_target_pairs={{0,4},{2,6},{4,12},{6,14},{8,0},{10,2},{12,8},{14,10},{1,5},{3,7},... | collective-permute-start | bytes 786440 | tf_op jit(solution)/shard_map/ppermute | solution.py:338
  31.5 7.0 %copy-start.2 = (bf16[2,64,576]{2,1,0:T(8,128)(2,1)S(1)}, bf16[2,64,576]{2,1,0:T(8,128)(2,1)}, u32[]{:S(2)}) copy-start(bf16[2,64,576]{2,1,0:T(8,128)(2,1)} %weight) | copy-start | bytes 442372
  36.1 7.6 %collective-permute-start.8 = (f32[2,2,128]{2,1,0:T(2,128)S(1)}, f32[2,2,128]{2,1,0:T(2,128)S(1)}, u32[]{:S(2)}, u32[]{:S(2)}) collective-permute-start(f32[2,2,128]{2,1,0:T(2,128)S(1)} %bitcast.26), channel_id=1, source_target_pairs={{0,1},{1,0},{2,3},{3,2},{4,5},{5,4},{6,7},{7,6},{8,9},{9,8},{10,11... | collective-permute-start | bytes 6152 | tf_op jit(solution)/shard_map/ppermute | solution.py:310
  38.8 8.1 %collective-permute-start.6 = (bf16[2,128,512]{2,1,0:T(8,128)(2,1)S(1)}, bf16[2,128,512]{2,1,0:T(8,128)(2,1)S(1)}, u32[]{:S(2)}, u32[]{:S(2)}) collective-permute-start(bf16[2,128,512]{2,1,0:T(8,128)(2,1)S(1)} %collective-permute-done.4.block), channel_id=1, source_target_pairs={{0,4},{2,6},{4,12},{6,14},{8,0},{10,2},{12,8},{14,10},{1,5},{3,7},... | collective-permute-start | bytes 786440 | tf_op jit(solution)/shard_map/ppermute | solution.py:338
  45.9 16.9 %copy-start.3 = (bf16[2,64]{1,0:T(2,128)(2,1)S(1)}, bf16[2,64]{1,0:T(2,128)(2,1)}, u32[]{:S(2)}) copy-start(bf16[2,64]{1,0:T(2,128)(2,1)} %head.1) | copy-start | bytes 772
  48.3 1.4 %collective-permute-start.9 = (f32[64,512]{1,0:T(8,128)S(1)}, f32[64,512]{1,0:T(8,128)S(1)}, u32[]{:S(2)}, u32[]{:S(2)}) collective-permute-start(f32[64,512]{1,0:T(8,128)S(1)} %get-tuple-element.113), channel_id=1, source_target_pairs={{0,2},{2,0},{4,6},{6,4},{8,10},{10,8},{12,14},{14,12},{1,3},{3,1},... | collective-permute-start | bytes 393224 | tf_op jit(solution)/shard_map/ppermute | solution.py:310
  49.7 4.5 %collective-permute-start.10 = (bf16[64,512]{1,0:T(8,128)(2,1)S(1)}, bf16[64,512]{1,0:T(8,128)(2,1)S(1)}, u32[]{:S(2)}, u32[]{:S(2)}) collective-permute-start(bf16[64,512]{1,0:T(8,128)(2,1)S(1)} %add_convert_fusion.1), channel_id=1, source_target_pairs={{0,1},{1,0},{2,3},{3,2},{4,5},{5,4},{6,7},{7,6},{8,9},{9,8},{10,11... | collective-permute-start | bytes 196616 | tf_op jit(solution)/shard_map/ppermute | solution.py:310
  54.3 1.3 %collective-permute-start.11 = (bf16[80,512]{1,0:T(8,128)(2,1)S(1)}, bf16[80,512]{1,0:T(8,128)(2,1)S(1)}, u32[]{:S(2)}, u32[]{:S(2)}) collective-permute-start(bf16[80,512]{1,0:T(8,128)(2,1)S(1)} %pad_maximum_fusion.1), channel_id=1, source_target_pairs={{0,2},{2,0},{4,6},{6,4},{8,10},{10,8},{12,14},{14,12},{1,3},{3,1},... | collective-permute-start | bytes 245768 | tf_op jit(solution)/shard_map/ppermute | solution.py:310
  55.7 5.6 %collective-permute-start.12 = (bf16[80,1024]{1,0:T(8,128)(2,1)S(1)}, bf16[80,1024]{1,0:T(8,128)(2,1)S(1)}, u32[]{:S(2)}, u32[]{:S(2)}) collective-permute-start(bf16[80,1024]{1,0:T(8,128)(2,1)S(1)} %pad_maximum_fusion.chip_map), channel_id=1, source_target_pairs={{0,4},{1,5},{2,3},{3,2},{4,0},{5,1},{6,10},{7,11},{8,12},{9,13},{1... | collective-permute-start | bytes 491528 | tf_op jit(solution)/shard_map/ppermute | solution.py:328
  61.3 1.4 %collective-permute-start.13 = (bf16[80,1024]{1,0:T(8,128)(2,1)S(1)}, bf16[80,1024]{1,0:T(8,128)(2,1)S(1)}, u32[]{:S(2)}, u32[]{:S(2)}) collective-permute-start(bf16[80,1024]{1,0:T(8,128)(2,1)S(1)} %collective-permute-done.12.near), channel_id=1, source_target_pairs={{0,2},{2,0},{4,6},{6,4},{8,10},{10,8},{12,14},{14,12},{1,3},{3,1},... | collective-permute-start | bytes 491528 | tf_op jit(solution)/shard_map/ppermute | solution.py:310
  66.3 5.8 %collective-permute-start.14 = (bf16[32,896]{1,0:T(8,128)(2,1)S(1)}, bf16[32,896]{1,0:T(8,128)(2,1)S(1)}, u32[]{:S(2)}, u32[]{:S(2)}) collective-permute-start(bf16[32,896]{1,0:T(8,128)(2,1)S(1)} %fusion.12), channel_id=1, source_target_pairs={{0,8},{2,10},{4,12},{6,14},{8,0},{10,2},{12,4},{14,6},{1,9},{3,11}... | collective-permute-start | bytes 172040 | tf_op jit(solution)/shard_map/ppermute | solution.py:316
  68.3 6.5 %collective-permute-start.15 = (bf16[32,896]{1,0:T(8,128)(2,1)S(1)}, bf16[32,896]{1,0:T(8,128)(2,1)S(1)}, u32[]{:S(2)}, u32[]{:S(2)}) collective-permute-start(bf16[32,896]{1,0:T(8,128)(2,1)S(1)} %fusion.12), channel_id=1, source_target_pairs={{0,4},{2,6},{4,8},{6,10},{8,12},{10,14},{12,0},{14,2},{1,5},{3,7},... | collective-permute-start | bytes 172040 | tf_op jit(solution)/shard_map/ppermute | solution.py:316
  70.3 4.7 %collective-permute-start.16 = (bf16[32,896]{1,0:T(8,128)(2,1)S(1)}, bf16[32,896]{1,0:T(8,128)(2,1)S(1)}, u32[]{:S(2)}, u32[]{:S(2)}) collective-permute-start(bf16[32,896]{1,0:T(8,128)(2,1)S(1)} %fusion.12), channel_id=1, source_target_pairs={{0,12},{2,14},{4,0},{6,2},{8,4},{10,6},{12,8},{14,10},{1,13},{3,15... | collective-permute-start | bytes 172040 | tf_op jit(solution)/shard_map/ppermute | solution.py:316
  75.0 4.2 %collective-permute-start.18 = (bf16[32,576]{1,0:T(8,128)(2,1)S(1)}, bf16[32,576]{1,0:T(8,128)(2,1)S(1)}, u32[]{:S(2)}, u32[]{:S(2)}) collective-permute-start(bf16[32,576]{1,0:T(8,128)(2,1)S(1)} %slice.30), channel_id=1, source_target_pairs={{0,1},{1,0},{16,17},{17,16},{2,3},{3,2},{18,19},{19,18},{4,5},{5,4... | collective-permute-start | bytes 110600 | tf_op jit(solution)/shard_map/ppermute | solution.py:359
  75.6 4.9 %collective-permute-start.19 = (bf16[32,576]{1,0:T(8,128)(2,1)S(1)}, bf16[32,576]{1,0:T(8,128)(2,1)S(1)}, u32[]{:S(2)}, u32[]{:S(2)}) collective-permute-start(bf16[32,576]{1,0:T(8,128)(2,1)S(1)} %slice.30), channel_id=1, source_target_pairs={{0,17},{1,16},{16,1},{17,0},{2,19},{3,18},{18,3},{19,2},{4,21},{5,... | collective-permute-start | bytes 110600 | tf_op jit(solution)/shard_map/ppermute | solution.py:359
  78.7 4.2 %collective-permute-start.17 = (bf16[32,896]{1,0:T(8,128)(2,1)S(1)}, bf16[32,896]{1,0:T(8,128)(2,1)S(1)}, u32[]{:S(2)}, u32[]{:S(2)}) collective-permute-start(bf16[32,896]{1,0:T(8,128)(2,1)S(1)} %add_convert_fusion.2), channel_id=1, source_target_pairs={{0,16},{1,17},{16,0},{17,1},{2,18},{3,19},{18,2},{19,3},{4,20},{5,... | collective-permute-start | bytes 172040 | tf_op jit(solution)/shard_map/ppermute | solution.py:359
  83.0 1.3 %collective-permute-start.21 = (f32[64,128]{1,0:T(8,128)S(1)}, f32[64,128]{1,0:T(8,128)S(1)}, u32[]{:S(2)}, u32[]{:S(2)}) collective-permute-start(f32[64,128]{1,0:T(8,128)S(1)} %pad_maximum_fusion.2), channel_id=1, source_target_pairs={{0,2},{2,0},{4,6},{6,4},{8,10},{10,8},{12,14},{14,12},{1,3},{3,1},... | collective-permute-start | bytes 98312 | tf_op jit(solution)/shard_map/ppermute | solution.py:310
  83.1 2.8 %collective-permute-start.20 = (f32[64,576]{1,0:T(8,128)S(1)}, f32[64,576]{1,0:T(8,128)S(1)}, u32[]{:S(2)}, u32[]{:S(2)}) collective-permute-start(f32[64,576]{1,0:T(8,128)S(1)} %maximum_select_fusion.2), channel_id=1, source_target_pairs={{0,2},{2,0},{4,6},{6,4},{8,10},{10,8},{12,14},{14,12},{1,3},{3,1},... | collective-permute-start | bytes 442376 | tf_op jit(solution)/shard_map/ppermute | solution.py:310

commit v6 on v3

--- a/solution.py
+++ b/solution.py
@@ -61,6 +61,28 @@
             for head in range(mine.shape[0]):
                 start = pl.multiple_of(which * kept + head * HEAD, HEAD)
                 out[head, at * HEAD : (at + 1) * HEAD, :] = turned[at, pl.ds(start, HEAD), :]
+
+
+def project_side_kernel(members, their, place, normed, weight, out):
+    kept = out.shape[0] * HEAD
+    which = 1 - place[0] if their else place[0]
+    for at, member in enumerate(members):
+        part = weight[member, :, pl.ds(pl.multiple_of(which * kept, 128), kept)]
+        columns = dot(normed[...], part).astype(BF16).T
+        for head in range(out.shape[0]):
+            out[head, at * HEAD : (at + 1) * HEAD, :] = columns[head * HEAD : (head + 1) * HEAD, :]
+
+
+def project_side(members, their, place, normed, weight):
+    shape = (weight.shape[2] // HEAD // 2, len(members) * HEAD, normed.shape[0])
+    return pl.pallas_call(
+        functools.partial(project_side_kernel, members, their),
+        out_shape=jax.ShapeDtypeStruct(shape, BF16),
+        in_specs=[SMEM, VMEM, VMEM],
+        out_specs=VMEM,
+        compiler_params=PARAMS,
+        name="project_side",
+    )(place, normed, weight)
 
 
 def project(members, place, normed, weight):
@@ -364,8 +386,10 @@
         (ln_gain.astype(F32).reshape(1, -1), qkv_weight, out_weight)
     )
     normed = normalize(frame_rows, gain)
-    own_keyed, their_keyed = project((1, 2), place, normed, qkv_weight)
-    own_keyed, their_keyed, normed = lax.optimization_barrier((own_keyed, their_keyed, normed))
+    own_keyed = project_side((1, 2), False, place, normed, qkv_weight)
+    own_keyed, normed = lax.optimization_barrier((own_keyed, normed))
+    their_keyed = project_side((1, 2), True, place, normed, qkv_weight)
+    their_keyed, normed = lax.optimization_barrier((their_keyed, normed))
     got_keyed = swapped(their_keyed, "tok")
     own_queries, their_queries = project((0,), place, normed, qkv_weight)
     queries = (own_queries, swapped(their_queries, "tok"))
@@ -432,21 +456,19 @@
     pieces = gradient.shape[0] // rows
     folded_gradient = [gradient[at * rows : (at + 1) * rows] for at in range(pieces)]
     sent = jnp.concatenate([jnp.pad(sums, ((0, 0), (0, lanes - taps_wide))), *folded_gradient], axis=1)
-    summed, hologram = lax.optimization_barrier((everyone(sent, "tok", 2, chips), hologram))
+    summed = everyone(sent, "tok", 2, chips)
     own_terms = sum_frames(summed, False)
     far_terms = sum_frames(summed[:, :taps_wide], True)
     wide = gradient.shape[1]
     own_small = jnp.concatenate(
         [own_terms[:, lanes + at * wide : lanes + (at + 1) * wide] for at in range(pieces)], axis=0
     )
-    other_small = swapped(own_small, "tok")
-    small = in_order(core, own_small, other_small, 1)
+    small = in_order(core, own_small, swapped(own_small, "tok"), 1)
     out_grad = lax.dot_general(
         small, readout_weight.astype(F32), (((0,), (1,)), ((), ())), precision=lax.Precision.HIGHEST
     )
     layer_grad = in_order(half, own_terms[:, :taps_wide], far_terms, 0)
-    other_grad = swapped(layer_grad, "tok")
-    conv_grad = in_order(core, layer_grad[None], other_grad[None], 0)
+    conv_grad = in_order(core, layer_grad[None], swapped(layer_grad, "tok")[None], 0)
     return (hologram[None], conv_grad, out_grad)
 
 

time: 84.1 us -> 86.1 us (1.024)
  Pallas kernels: 23.8 us -> 25 us
    pallas_call x0 -> x2, Pallas kernels: none -> 2.65 us  [project_side(): pl.pallas_call(functools.partial(project_side_kernel, members, their), ou...]
    pallas_call x2 -> x1, Pallas kernels: 2.41 us -> 1.05 us  [project(): pl.pallas_call(functools.partial(project_kernel, members), out_shape=(sha...]
where the time goes in v6:
time: 86.1 us; the launch traced here: 85.9 us
  waiting for transfers between devices  29.2 us (34%)
  Pallas kernels  25 us (29%)
  starting transfers between devices  24.5 us (28%)
  matrix products  2.26 us (3%)
  local copies, waits for them, and re-layouts  1.96 us (2%)
  other arithmetic  1.88 us (2%)
  between operations  1.04 us (1%)
    pallas_call x7, Pallas kernels, absorb(): pl.pallas_call(functools.partial(absorb_kernel, first), out_shape=shapes,...  14.3 us
    ppermute x6, waiting for transfers between devices, round_ring(): lax.ppermute(values, 'tok', [(i, 2 * following[i // 2] + i % 2) for i in...  10.4 us
    ppermute x6, starting transfers between devices, round_ring(): lax.ppermute(values, 'tok', [(i, 2 * following[i // 2] + i % 2) for i in...  9.3 us
    ppermute x9, waiting for transfers between devices, swapped(): return lax.ppermute(values, axis, [(i, i ^ 1) for i in range(size)])  8.35 us
    ppermute x3, starting transfers between devices, passed(): return lax.ppermute(values, axis, pairs)  6.03 us
    ppermute x9, starting transfers between devices, swapped(): return lax.ppermute(values, axis, [(i, i ^ 1) for i in range(size)])  4.11 us
    ppermute x1, waiting for transfers between devices, beside(): return lax.ppermute(values, ('tok', 'col'), pairs)  3.89 us
    ppermute x3, waiting for transfers between devices, sum_frames(): moved = lax.ppermute(sent, ('dp', 'col'), pairs) if step or across else sent  3.66 us
  transfers between devices with their start and end apart: 22, of which 17 were waited for; matrix products, arithmetic and copies ran while one was open for 4% of the time, Pallas kernels for 20%

profile of v6, /device:TPU:0, one launch (start us, length us, event | category | flops | bytes accessed | tf_op | source)
XLA Modules:
  0.0 85.9 jit_solution(13566810388705920842)
XLA Ops:
  3.5 1.3 %project_side.2.block = bf16[2,128,512]{2,1,0:T(8,128)(2,1)S(1)} custom-call(s32[4]{0:T(128)S(1)} %pad_add_fusion.place, bf16[512,1024]{1,0:T(8,128)(2,1)S(1)} %normalize.1.normed, bf16[3,1024,256]{2,1,0:T(8,128)(2,1)S(1)} %copy-done.1), custom_call_target="tpu_custom_call" | custom-call | tf_op jit(solution)/shard_map/project_side/pallas_call | solution.py:78
  4.8 1.3 %project_side.3 = bf16[2,128,512]{2,1,0:T(8,128)(2,1)S(1)} custom-call(s32[4]{0:T(128)S(1)} %pad_add_fusion.place, bf16[512,1024]{1,0:T(8,128)(2,1)S(1)} %normalize.1.normed, bf16[3,1024,256]{2,1,0:T(8,128)(2,1)S(1)} %copy-done.1), custom_call_target="tpu_custom_call" | custom-call | tf_op jit(solution)/shard_map/project_side/pallas_call | solution.py:78
  6.7 2.6 %collective-permute-start.3 = (bf16[2,128,512]{2,1,0:T(8,128)(2,1)S(1)}, bf16[2,128,512]{2,1,0:T(8,128)(2,1)S(1)}, u32[]{:S(2)}, u32[]{:S(2)}) collective-permute-start(bf16[2,128,512]{2,1,0:T(8,128)(2,1)S(1)} %project_side.2.block), channel_id=1, source_target_pairs={{0,4},{2,6},{4,12},{6,14},{8,0},{10,2},{12,8},{14,10},{1,5},{3,7},... | collective-permute-start | bytes 786440 | tf_op jit(solution)/shard_map/ppermute | solution.py:337
  9.3 2.6 %collective-permute-start.1 = (bf16[2,128,512]{2,1,0:T(8,128)(2,1)S(1)}, bf16[2,128,512]{2,1,0:T(8,128)(2,1)S(1)}, u32[]{:S(2)}, u32[]{:S(2)}) collective-permute-start(bf16[2,128,512]{2,1,0:T(8,128)(2,1)S(1)} %collective-permute-done.block), channel_id=1, source_target_pairs={{0,4},{2,6},{4,12},{6,14},{8,0},{10,2},{12,8},{14,10},{1,5},{3,7},... | collective-permute-start | bytes 786440 | tf_op jit(solution)/shard_map/ppermute | solution.py:337
  13.1 1.3 %collective-permute-done.2.got.queries = bf16[2,64,512]{2,1,0:T(8,128)(2,1)S(1)} collective-permute-done((bf16[2,64,512]{2,1,0:T(8,128)(2,1)S(1)}, bf16[2,64,512]{2,1,0:T(8,128)(2,1)S(1)}, u32[]{:S(2)}, u32[]{:S(2)}) %collective-permute-start.2) | collective-permute-done | bytes 131104 | tf_op jit(solution)/shard_map/ppermute | solution.py:309
  14.4 2.0 %absorb.7 = (f32[2,80,1024]{2,1,0:T(8,128)S(1)}, f32[2,8,1024]{2,1,0:T(8,128)S(1)}) custom-call(bf16[2,64,512]{2,1,0:T(8,128)(2,1)S(1)} %get-tuple-element.68.own.queries, bf16[2,64,512]{2,1,0:T(8,128)(2,1)S(1)} %collective-permute-done.2.got.queries, bf16[2,128,512]{2,1,0:T(8,128)(2,1)S(1)} %project_side.2.block), custom_call_target="tpu_custom_call" | custom-call | tf_op jit(solution)/shard_map/absorb/pallas_call | solution.py:137
  18.6 2.0 %absorb.8 = (f32[2,80,1024]{2,1,0:T(8,128)S(1)}, f32[2,8,1024]{2,1,0:T(8,128)S(1)}) custom-call(bf16[2,64,512]{2,1,0:T(8,128)(2,1)S(1)} %get-tuple-element.68.own.queries, bf16[2,64,512]{2,1,0:T(8,128)(2,1)S(1)} %collective-permute-done.2.got.queries, ...), custom_call_target="tpu_custom_call", output_to_operand_aliasing={{0}: (3, {}), {1}: (4, {})} | custom-call | tf_op jit(solution)/shard_map/absorb/pallas_call | solution.py:137
  20.7 2.5 %collective-permute-done.1.block = bf16[2,128,512]{2,1,0:T(8,128)(2,1)S(1)} collective-permute-done((bf16[2,128,512]{2,1,0:T(8,128)(2,1)S(1)}, bf16[2,128,512]{2,1,0:T(8,128)(2,1)S(1)}, u32[]{:S(2)}, u32[]{:S(2)}) %collective-permute-start.1) | collective-permute-done | bytes 262176 | tf_op jit(solution)/shard_map/ppermute | solution.py:337
  24.2 2.0 %absorb.9 = (f32[2,80,1024]{2,1,0:T(8,128)S(1)}, f32[2,8,1024]{2,1,0:T(8,128)S(1)}) custom-call(bf16[2,64,512]{2,1,0:T(8,128)(2,1)S(1)} %get-tuple-element.68.own.queries, bf16[2,64,512]{2,1,0:T(8,128)(2,1)S(1)} %collective-permute-done.2.got.queries, ...), custom_call_target="tpu_custom_call", output_to_operand_aliasing={{0}: (3, {}), {1}: (4, {})} | custom-call | tf_op jit(solution)/shard_map/absorb/pallas_call | solution.py:137
  26.3 2.4 %collective-permute-done.5.block = bf16[2,128,512]{2,1,0:T(8,128)(2,1)S(1)} collective-permute-done((bf16[2,128,512]{2,1,0:T(8,128)(2,1)S(1)}, bf16[2,128,512]{2,1,0:T(8,128)(2,1)S(1)}, u32[]{:S(2)}, u32[]{:S(2)}) %collective-permute-start.5) | collective-permute-done | bytes 262176 | tf_op jit(solution)/shard_map/ppermute | solution.py:337
  29.9 2.0 %absorb.10 = (f32[2,80,1024]{2,1,0:T(8,128)S(1)}, f32[2,8,1024]{2,1,0:T(8,128)S(1)}) custom-call(bf16[2,64,512]{2,1,0:T(8,128)(2,1)S(1)} %get-tuple-element.68.own.queries, bf16[2,64,512]{2,1,0:T(8,128)(2,1)S(1)} %collective-permute-done.2.got.queries, ...), custom_call_target="tpu_custom_call", output_to_operand_aliasing={{0}: (3, {}), {1}: (4, {})} | custom-call | tf_op jit(solution)/shard_map/absorb/pallas_call | solution.py:137
  31.9 2.4 %collective-permute-done.4.block = bf16[2,128,512]{2,1,0:T(8,128)(2,1)S(1)} collective-permute-done((bf16[2,128,512]{2,1,0:T(8,128)(2,1)S(1)}, bf16[2,128,512]{2,1,0:T(8,128)(2,1)S(1)}, u32[]{:S(2)}, u32[]{:S(2)}) %collective-permute-start.4) | collective-permute-done | bytes 262176 | tf_op jit(solution)/shard_map/ppermute | solution.py:337
  34.4 2.0 %absorb.11 = (f32[2,80,1024]{2,1,0:T(8,128)S(1)}, f32[2,8,1024]{2,1,0:T(8,128)S(1)}) custom-call(bf16[2,64,512]{2,1,0:T(8,128)(2,1)S(1)} %get-tuple-element.68.own.queries, bf16[2,64,512]{2,1,0:T(8,128)(2,1)S(1)} %collective-permute-done.2.got.queries, ...), custom_call_target="tpu_custom_call", output_to_operand_aliasing={{0}: (3, {}), {1}: (4, {})} | custom-call | tf_op jit(solution)/shard_map/absorb/pallas_call | solution.py:137
  36.4 1.9 %collective-permute-start.8 = (f32[2,2,128]{2,1,0:T(2,128)S(1)}, f32[2,2,128]{2,1,0:T(2,128)S(1)}, u32[]{:S(2)}, u32[]{:S(2)}) collective-permute-start(f32[2,2,128]{2,1,0:T(2,128)S(1)} %bitcast.27), channel_id=1, source_target_pairs={{0,1},{1,0},{2,3},{3,2},{4,5},{5,4},{6,7},{7,6},{8,9},{9,8},{10,11... | collective-permute-start | bytes 6152 | tf_op jit(solution)/shard_map/ppermute | solution.py:309
  40.0 2.1 %absorb.12 = (f32[2,80,1024]{2,1,0:T(8,128)S(1)}, f32[2,8,1024]{2,1,0:T(8,128)S(1)}) custom-call(bf16[2,64,512]{2,1,0:T(8,128)(2,1)S(1)} %get-tuple-element.68.own.queries, bf16[2,64,512]{2,1,0:T(8,128)(2,1)S(1)} %collective-permute-done.2.got.queries, ...), custom_call_target="tpu_custom_call", output_to_operand_aliasing={{0}: (3, {}), {1}: (4, {})} | custom-call | tf_op jit(solution)/shard_map/absorb/pallas_call | solution.py:137
  42.2 2.1 %absorb.13 = (f32[2,80,1024]{2,1,0:T(8,128)S(1)}, f32[2,8,1024]{2,1,0:T(8,128)S(1)}) custom-call(bf16[2,64,512]{2,1,0:T(8,128)(2,1)S(1)} %get-tuple-element.68.own.queries, bf16[2,64,512]{2,1,0:T(8,128)(2,1)S(1)} %collective-permute-done.2.got.queries, ...), custom_call_target="tpu_custom_call", output_to_operand_aliasing={{0}: (3, {}), {1}: (4, {})} | custom-call | tf_op jit(solution)/shard_map/absorb/pallas_call | solution.py:137
  44.3 2.0 %collective-permute-done.6.block = bf16[2,128,512]{2,1,0:T(8,128)(2,1)S(1)} collective-permute-done((bf16[2,128,512]{2,1,0:T(8,128)(2,1)S(1)}, bf16[2,128,512]{2,1,0:T(8,128)(2,1)S(1)}, u32[]{:S(2)}, u32[]{:S(2)}) %collective-permute-start.6) | collective-permute-done | bytes 262176 | tf_op jit(solution)/shard_map/ppermute | solution.py:337
  46.2 1.3 %closing.3 = (bf16[128,512]{1,0:T(8,128)(2,1)S(1)}, f32[64,512]{1,0:T(8,128)S(1)}) custom-call(bf16[2,64,512]{2,1,0:T(8,128)(2,1)S(1)} %collective-permute-done.2.got.queries, bf16[2,128,512]{2,1,0:T(8,128)(2,1)S(1)} %collective-permute-done.6.block, f32[2,80,1024]{2,1,0:T(8,128)S(1)} %get-tuple-element.111.carried, ...), custom_call_target="tpu_custom_call" | custom-call | tf_op jit(solution)/shard_map/closing/pallas_call | solution.py:160
  47.6 1.3 %closing.2 = (bf16[128,512]{1,0:T(8,128)(2,1)S(1)}, f32[64,512]{1,0:T(8,128)S(1)}) custom-call(bf16[2,64,512]{2,1,0:T(8,128)(2,1)S(1)} %get-tuple-element.68.own.queries, bf16[2,128,512]{2,1,0:T(8,128)(2,1)S(1)} %collective-permute-done.6.block, f32[2,80,1024]{2,1,0:T(8,128)S(1)} %get-tuple-element.111.carried, ...), custom_call_target="tpu_custom_call" | custom-call | tf_op jit(solution)/shard_map/closing/pallas_call | solution.py:160
  49.8 3.7 %collective-permute-done.10 = bf16[64,512]{1,0:T(8,128)(2,1)S(1)} collective-permute-done((bf16[64,512]{1,0:T(8,128)(2,1)S(1)}, bf16[64,512]{1,0:T(8,128)(2,1)S(1)}, u32[]{:S(2)}, u32[]{:S(2)}) %collective-permute-start.10) | collective-permute-done | bytes 65568 | tf_op jit(solution)/shard_map/ppermute | solution.py:309
  53.6 1.3 %collective-permute-done.11 = bf16[80,512]{1,0:T(8,128)(2,1)S(1)} collective-permute-done((bf16[80,512]{1,0:T(8,128)(2,1)S(1)}, bf16[80,512]{1,0:T(8,128)(2,1)S(1)}, u32[]{:S(2)}, u32[]{:S(2)}) %collective-permute-start.11) | collective-permute-done | bytes 81952 | tf_op jit(solution)/shard_map/ppermute | solution.py:309
  54.9 1.5 %collective-permute-start.12 = (bf16[80,1024]{1,0:T(8,128)(2,1)S(1)}, bf16[80,1024]{1,0:T(8,128)(2,1)S(1)}, u32[]{:S(2)}, u32[]{:S(2)}) collective-permute-start(bf16[80,1024]{1,0:T(8,128)(2,1)S(1)} %pad_maximum_fusion.chip_map), channel_id=1, source_target_pairs={{0,4},{1,5},{2,3},{3,2},{4,0},{5,1},{6,10},{7,11},{8,12},{9,13},{1... | collective-permute-start | bytes 491528 | tf_op jit(solution)/shard_map/ppermute | solution.py:327
  56.4 3.9 %collective-permute-done.12.near = bf16[80,1024]{1,0:T(8,128)(2,1)S(1)} collective-permute-done((bf16[80,1024]{1,0:T(8,128)(2,1)S(1)}, bf16[80,1024]{1,0:T(8,128)(2,1)S(1)}, u32[]{:S(2)}, u32[]{:S(2)}) %collective-permute-start.12) | collective-permute-done | bytes 163872 | tf_op jit(solution)/shard_map/ppermute | solution.py:327
  60.3 1.4 %collective-permute-done.13.far = bf16[80,1024]{1,0:T(8,128)(2,1)S(1)} collective-permute-done((bf16[80,1024]{1,0:T(8,128)(2,1)S(1)}, bf16[80,1024]{1,0:T(8,128)(2,1)S(1)}, u32[]{:S(2)}, u32[]{:S(2)}) %collective-permute-start.13) | collective-permute-done | bytes 163872 | tf_op jit(solution)/shard_map/ppermute | solution.py:309
  61.7 3.6 %network.1 = (f32[2,1024]{1,0:T(2,128)S(1)}, f32[32,576]{1,0:T(8,128)S(1)}, f32[64,128]{1,0:T(8,128)S(1)}) custom-call(s32[4]{0:T(128)S(1)} %pad_add_fusion.place, bf16[80,1024]{1,0:T(8,128)(2,1)S(1)} %pad_maximum_fusion.chip_map, bf16[80,1024]{1,0:T(8,128)(2,1)S(1)} %collective-permute-done.12.near, bf16[80,1024]{1,0:T(8,128)(2,1)S(1)} %collective-permute-done.13.far, ...), custom_call_target="tpu_custom_call" | custom-call | tf_op jit(solution)/shard_map/network/pallas_call | solution.py:292
  65.3 2.2 %collective-permute-start.14 = (bf16[32,896]{1,0:T(8,128)(2,1)S(1)}, bf16[32,896]{1,0:T(8,128)(2,1)S(1)}, u32[]{:S(2)}, u32[]{:S(2)}) collective-permute-start(bf16[32,896]{1,0:T(8,128)(2,1)S(1)} %fusion.14), channel_id=1, source_target_pairs={{0,8},{2,10},{4,12},{6,14},{8,0},{10,2},{12,4},{14,6},{1,9},{3,11}... | collective-permute-start | bytes 172040 | tf_op jit(solution)/shard_map/ppermute | solution.py:315
  67.5 2.0 %collective-permute-start.15 = (bf16[32,896]{1,0:T(8,128)(2,1)S(1)}, bf16[32,896]{1,0:T(8,128)(2,1)S(1)}, u32[]{:S(2)}, u32[]{:S(2)}) collective-permute-start(bf16[32,896]{1,0:T(8,128)(2,1)S(1)} %fusion.14), channel_id=1, source_target_pairs={{0,4},{2,6},{4,8},{6,10},{8,12},{10,14},{12,0},{14,2},{1,5},{3,7},... | collective-permute-start | bytes 172040 | tf_op jit(solution)/shard_map/ppermute | solution.py:315
  69.5 1.8 %collective-permute-start.16 = (bf16[32,896]{1,0:T(8,128)(2,1)S(1)}, bf16[32,896]{1,0:T(8,128)(2,1)S(1)}, u32[]{:S(2)}, u32[]{:S(2)}) collective-permute-start(bf16[32,896]{1,0:T(8,128)(2,1)S(1)} %fusion.14), channel_id=1, source_target_pairs={{0,12},{2,14},{4,0},{6,2},{8,4},{10,6},{12,8},{14,10},{1,13},{3,15... | collective-permute-start | bytes 172040 | tf_op jit(solution)/shard_map/ppermute | solution.py:315
  75.1 2.2 %collective-permute-start.19 = (bf16[32,576]{1,0:T(8,128)(2,1)S(1)}, bf16[32,576]{1,0:T(8,128)(2,1)S(1)}, u32[]{:S(2)}, u32[]{:S(2)}) collective-permute-start(bf16[32,576]{1,0:T(8,128)(2,1)S(1)} %slice.30), channel_id=1, source_target_pairs={{0,17},{1,16},{16,1},{17,0},{2,19},{3,18},{18,3},{19,2},{4,21},{5,... | collective-permute-start | bytes 110600 | tf_op jit(solution)/shard_map/ppermute | solution.py:358
  78.8 1.3 %collective-permute-done.19 = bf16[32,576]{1,0:T(8,128)(2,1)S(1)} collective-permute-done((bf16[32,576]{1,0:T(8,128)(2,1)S(1)}, bf16[32,576]{1,0:T(8,128)(2,1)S(1)}, u32[]{:S(2)}, u32[]{:S(2)}) %collective-permute-start.19) | collective-permute-done | bytes 36896 | tf_op jit(solution)/shard_map/ppermute | solution.py:358
  80.1 2.1 %collective-permute-done.17 = bf16[32,896]{1,0:T(8,128)(2,1)S(1)} collective-permute-done((bf16[32,896]{1,0:T(8,128)(2,1)S(1)}, bf16[32,896]{1,0:T(8,128)(2,1)S(1)}, u32[]{:S(2)}, u32[]{:S(2)}) %collective-permute-start.17) | collective-permute-done | bytes 57376 | tf_op jit(solution)/shard_map/ppermute | solution.py:358
  83.5 1.6 %fusion.3 = f32[256,1024]{1,0:T(8,128)} fusion(bf16[1024,64]{0,1:T(8,128)(2,1)S(1)} %copy-done.6, f32[64,128]{1,0:T(8,128)S(1)} %collective-permute-done.21, f32[32,128]{1,0:T(8,128)S(1)} %get-tuple-element.126, f32[32,128]{1,0:T(8,128)S(1)} %get-tuple-element.125, pred[]{:T(512)S(6)} %eq.10), kind=kOutput, calls=%fused_computation.15 | convolution fusion | flops 201408512 | bytes 1245185 | tf_op jit(solution)/shard_map/dot_general | solution.py:467
  (73 shorter events, 19.0 us)
Async XLA Ops:
  0.6 38.9 %copy-start = (bf16[256,1024]{1,0:T(8,128)(2,1)S(1)}, bf16[256,1024]{1,0:T(8,128)(2,1)}, u32[]{:S(2)}) copy-start(bf16[256,1024]{1,0:T(8,128)(2,1)} %param.11) | copy-start | bytes 1572868
  0.6 2.8 %copy-start.1 = (bf16[3,1024,256]{2,1,0:T(8,128)(2,1)S(1)}, bf16[3,1024,256]{2,1,0:T(8,128)(2,1)}, u32[]{:S(2)}) copy-start(bf16[3,1024,256]{2,1,0:T(8,128)(2,1)} %weight.2) | copy-start | bytes 4718596
  1.5 1.2 %copy-start.2 = (bf16[1,512,1024]{2,1,0:T(8,128)(2,1)S(1)}, bf16[1,512,1024]{2,1,0:T(8,128)(2,1)}, u32[]{:S(2)}) copy-start(bf16[1,512,1024]{2,1,0:T(8,128)(2,1)} %param.8) | copy-start | bytes 3145732
  6.2 3.2 %collective-permute-start = (bf16[2,128,512]{2,1,0:T(8,128)(2,1)S(1)}, bf16[2,128,512]{2,1,0:T(8,128)(2,1)S(1)}, u32[]{:S(2)}, u32[]{:S(2)}) collective-permute-start(bf16[2,128,512]{2,1,0:T(8,128)(2,1)S(1)} %project_side.3), channel_id=1, source_target_pairs={{0,2},{2,0},{4,6},{6,4},{8,10},{10,8},{12,14},{14,12},{1,3},{3,1},... | collective-permute-start | bytes 786440 | tf_op jit(solution)/shard_map/ppermute | solution.py:309
  6.7 10.8 %collective-permute-start.3 = (bf16[2,128,512]{2,1,0:T(8,128)(2,1)S(1)}, bf16[2,128,512]{2,1,0:T(8,128)(2,1)S(1)}, u32[]{:S(2)}, u32[]{:S(2)}) collective-permute-start(bf16[2,128,512]{2,1,0:T(8,128)(2,1)S(1)} %project_side.2.block), channel_id=1, source_target_pairs={{0,4},{2,6},{4,12},{6,14},{8,0},{10,2},{12,8},{14,10},{1,5},{3,7},... | collective-permute-start | bytes 786440 | tf_op jit(solution)/shard_map/ppermute | solution.py:337
  9.3 13.8 %collective-permute-start.1 = (bf16[2,128,512]{2,1,0:T(8,128)(2,1)S(1)}, bf16[2,128,512]{2,1,0:T(8,128)(2,1)S(1)}, u32[]{:S(2)}, u32[]{:S(2)}) collective-permute-start(bf16[2,128,512]{2,1,0:T(8,128)(2,1)S(1)} %collective-permute-done.block), channel_id=1, source_target_pairs={{0,4},{2,6},{4,12},{6,14},{8,0},{10,2},{12,8},{14,10},{1,5},{3,7},... | collective-permute-start | bytes 786440 | tf_op jit(solution)/shard_map/ppermute | solution.py:337
  13.0 1.4 %collective-permute-start.2 = (bf16[2,64,512]{2,1,0:T(8,128)(2,1)S(1)}, bf16[2,64,512]{2,1,0:T(8,128)(2,1)S(1)}, u32[]{:S(2)}, u32[]{:S(2)}) collective-permute-start(bf16[2,64,512]{2,1,0:T(8,128)(2,1)S(1)} %get-tuple-element.70), channel_id=1, source_target_pairs={{0,2},{2,0},{4,6},{6,4},{8,10},{10,8},{12,14},{14,12},{1,3},{3,1},... | collective-permute-start | bytes 393224 | tf_op jit(solution)/shard_map/ppermute | solution.py:309
  17.5 11.2 %collective-permute-start.5 = (bf16[2,128,512]{2,1,0:T(8,128)(2,1)S(1)}, bf16[2,128,512]{2,1,0:T(8,128)(2,1)S(1)}, u32[]{:S(2)}, u32[]{:S(2)}) collective-permute-start(bf16[2,128,512]{2,1,0:T(8,128)(2,1)S(1)} %collective-permute-done.3.block), channel_id=1, source_target_pairs={{0,4},{2,6},{4,12},{6,14},{8,0},{10,2},{12,8},{14,10},{1,5},{3,7},... | collective-permute-start | bytes 786440 | tf_op jit(solution)/shard_map/ppermute | solution.py:337
  23.1 11.2 %collective-permute-start.4 = (bf16[2,128,512]{2,1,0:T(8,128)(2,1)S(1)}, bf16[2,128,512]{2,1,0:T(8,128)(2,1)S(1)}, u32[]{:S(2)}, u32[]{:S(2)}) collective-permute-start(bf16[2,128,512]{2,1,0:T(8,128)(2,1)S(1)} %collective-permute-done.1.block), channel_id=1, source_target_pairs={{0,4},{2,6},{4,12},{6,14},{8,0},{10,2},{12,8},{14,10},{1,5},{3,7},... | collective-permute-start | bytes 786440 | tf_op jit(solution)/shard_map/ppermute | solution.py:337
  24.2 12.2 %copy-start.7 = (f32[1,2,2,128]{3,2,1,0:T(2,128)S(1)}, f32[1,2,2,128]{3,2,1,0:T(2,128)}, u32[]{:S(2)}) copy-start(f32[1,2,2,128]{3,2,1,0:T(2,128)} %param.15) | copy-start | bytes 6148
  24.2 14.9 %copy-start.3 = (bf16[1,512,1024]{2,1,0:T(8,128)(2,1)S(1)}, bf16[1,512,1024]{2,1,0:T(8,128)(2,1)}, u32[]{:S(2)}) copy-start(bf16[1,512,1024]{2,1,0:T(8,128)(2,1)} %param.8) | copy-start | bytes 3145732
  24.2 14.9 %copy-start.6 = (bf16[1024,64]{0,1:T(8,128)(2,1)S(1)}, bf16[1024,64]{0,1:T(8,128)(2,1)}, u32[]{:S(2)}) copy-start(bf16[1024,64]{0,1:T(8,128)(2,1)} %param.12) | copy-start | bytes 393220
  28.8 13.4 %collective-permute-start.7 = (bf16[2,128,512]{2,1,0:T(8,128)(2,1)S(1)}, bf16[2,128,512]{2,1,0:T(8,128)(2,1)S(1)}, u32[]{:S(2)}, u32[]{:S(2)}) collective-permute-start(bf16[2,128,512]{2,1,0:T(8,128)(2,1)S(1)} %collective-permute-done.5.block), channel_id=1, source_target_pairs={{0,4},{2,6},{4,12},{6,14},{8,0},{10,2},{12,8},{14,10},{1,5},{3,7},... | collective-permute-start | bytes 786440 | tf_op jit(solution)/shard_map/ppermute | solution.py:337
  31.9 7.9 %copy-start.4 = (bf16[2,64,576]{2,1,0:T(8,128)(2,1)S(1)}, bf16[2,64,576]{2,1,0:T(8,128)(2,1)}, u32[]{:S(2)}) copy-start(bf16[2,64,576]{2,1,0:T(8,128)(2,1)} %weight.3) | copy-start | bytes 442372
  36.4 5.7 %collective-permute-start.8 = (f32[2,2,128]{2,1,0:T(2,128)S(1)}, f32[2,2,128]{2,1,0:T(2,128)S(1)}, u32[]{:S(2)}, u32[]{:S(2)}) collective-permute-start(f32[2,2,128]{2,1,0:T(2,128)S(1)} %bitcast.27), channel_id=1, source_target_pairs={{0,1},{1,0},{2,3},{3,2},{4,5},{5,4},{6,7},{7,6},{8,9},{9,8},{10,11... | collective-permute-start | bytes 6152 | tf_op jit(solution)/shard_map/ppermute | solution.py:309
  38.3 7.9 %collective-permute-start.6 = (bf16[2,128,512]{2,1,0:T(8,128)(2,1)S(1)}, bf16[2,128,512]{2,1,0:T(8,128)(2,1)S(1)}, u32[]{:S(2)}, u32[]{:S(2)}) collective-permute-start(bf16[2,128,512]{2,1,0:T(8,128)(2,1)S(1)} %collective-permute-done.4.block), channel_id=1, source_target_pairs={{0,4},{2,6},{4,12},{6,14},{8,0},{10,2},{12,8},{14,10},{1,5},{3,7},... | collective-permute-start | bytes 786440 | tf_op jit(solution)/shard_map/ppermute | solution.py:337
  44.3 17.4 %copy-start.5 = (bf16[2,64]{1,0:T(2,128)(2,1)S(1)}, bf16[2,64]{1,0:T(2,128)(2,1)}, u32[]{:S(2)}) copy-start(bf16[2,64]{1,0:T(2,128)(2,1)} %head.1) | copy-start | bytes 772
  47.5 1.4 %collective-permute-start.9 = (f32[64,512]{1,0:T(8,128)S(1)}, f32[64,512]{1,0:T(8,128)S(1)}, u32[]{:S(2)}, u32[]{:S(2)}) collective-permute-start(f32[64,512]{1,0:T(8,128)S(1)} %get-tuple-element.115), channel_id=1, source_target_pairs={{0,2},{2,0},{4,6},{6,4},{8,10},{10,8},{12,14},{14,12},{1,3},{3,1},... | collective-permute-start | bytes 393224 | tf_op jit(solution)/shard_map/ppermute | solution.py:309
  49.0 4.5 %collective-permute-start.10 = (bf16[64,512]{1,0:T(8,128)(2,1)S(1)}, bf16[64,512]{1,0:T(8,128)(2,1)S(1)}, u32[]{:S(2)}, u32[]{:S(2)}) collective-permute-start(bf16[64,512]{1,0:T(8,128)(2,1)S(1)} %add_convert_fusion.1), channel_id=1, source_target_pairs={{0,1},{1,0},{2,3},{3,2},{4,5},{5,4},{6,7},{7,6},{8,9},{9,8},{10,11... | collective-permute-start | bytes 196616 | tf_op jit(solution)/shard_map/ppermute | solution.py:309
  53.5 1.3 %collective-permute-start.11 = (bf16[80,512]{1,0:T(8,128)(2,1)S(1)}, bf16[80,512]{1,0:T(8,128)(2,1)S(1)}, u32[]{:S(2)}, u32[]{:S(2)}) collective-permute-start(bf16[80,512]{1,0:T(8,128)(2,1)S(1)} %pad_maximum_fusion.1), channel_id=1, source_target_pairs={{0,2},{2,0},{4,6},{6,4},{8,10},{10,8},{12,14},{14,12},{1,3},{3,1},... | collective-permute-start | bytes 245768 | tf_op jit(solution)/shard_map/ppermute | solution.py:309
  54.9 5.4 %collective-permute-start.12 = (bf16[80,1024]{1,0:T(8,128)(2,1)S(1)}, bf16[80,1024]{1,0:T(8,128)(2,1)S(1)}, u32[]{:S(2)}, u32[]{:S(2)}) collective-permute-start(bf16[80,1024]{1,0:T(8,128)(2,1)S(1)} %pad_maximum_fusion.chip_map), channel_id=1, source_target_pairs={{0,4},{1,5},{2,3},{3,2},{4,0},{5,1},{6,10},{7,11},{8,12},{9,13},{1... | collective-permute-start | bytes 491528 | tf_op jit(solution)/shard_map/ppermute | solution.py:327
  60.3 1.4 %collective-permute-start.13 = (bf16[80,1024]{1,0:T(8,128)(2,1)S(1)}, bf16[80,1024]{1,0:T(8,128)(2,1)S(1)}, u32[]{:S(2)}, u32[]{:S(2)}) collective-permute-start(bf16[80,1024]{1,0:T(8,128)(2,1)S(1)} %collective-permute-done.12.near), channel_id=1, source_target_pairs={{0,2},{2,0},{4,6},{6,4},{8,10},{10,8},{12,14},{14,12},{1,3},{3,1},... | collective-permute-start | bytes 491528 | tf_op jit(solution)/shard_map/ppermute | solution.py:309
  65.3 7.3 %collective-permute-start.14 = (bf16[32,896]{1,0:T(8,128)(2,1)S(1)}, bf16[32,896]{1,0:T(8,128)(2,1)S(1)}, u32[]{:S(2)}, u32[]{:S(2)}) collective-permute-start(bf16[32,896]{1,0:T(8,128)(2,1)S(1)} %fusion.14), channel_id=1, source_target_pairs={{0,8},{2,10},{4,12},{6,14},{8,0},{10,2},{12,4},{14,6},{1,9},{3,11}... | collective-permute-start | bytes 172040 | tf_op jit(solution)/shard_map/ppermute | solution.py:315
  67.5 6.1 %collective-permute-start.15 = (bf16[32,896]{1,0:T(8,128)(2,1)S(1)}, bf16[32,896]{1,0:T(8,128)(2,1)S(1)}, u32[]{:S(2)}, u32[]{:S(2)}) collective-permute-start(bf16[32,896]{1,0:T(8,128)(2,1)S(1)} %fusion.14), channel_id=1, source_target_pairs={{0,4},{2,6},{4,8},{6,10},{8,12},{10,14},{12,0},{14,2},{1,5},{3,7},... | collective-permute-start | bytes 172040 | tf_op jit(solution)/shard_map/ppermute | solution.py:315
  69.5 4.7 %collective-permute-start.16 = (bf16[32,896]{1,0:T(8,128)(2,1)S(1)}, bf16[32,896]{1,0:T(8,128)(2,1)S(1)}, u32[]{:S(2)}, u32[]{:S(2)}) collective-permute-start(bf16[32,896]{1,0:T(8,128)(2,1)S(1)} %fusion.14), channel_id=1, source_target_pairs={{0,12},{2,14},{4,0},{6,2},{8,4},{10,6},{12,8},{14,10},{1,13},{3,15... | collective-permute-start | bytes 172040 | tf_op jit(solution)/shard_map/ppermute | solution.py:315
  74.3 4.4 %collective-permute-start.18 = (bf16[32,576]{1,0:T(8,128)(2,1)S(1)}, bf16[32,576]{1,0:T(8,128)(2,1)S(1)}, u32[]{:S(2)}, u32[]{:S(2)}) collective-permute-start(bf16[32,576]{1,0:T(8,128)(2,1)S(1)} %slice.30), channel_id=1, source_target_pairs={{0,1},{1,0},{16,17},{17,16},{2,3},{3,2},{18,19},{19,18},{4,5},{5,4... | collective-permute-start | bytes 110600 | tf_op jit(solution)/shard_map/ppermute | solution.py:358
  75.1 4.9 %collective-permute-start.19 = (bf16[32,576]{1,0:T(8,128)(2,1)S(1)}, bf16[32,576]{1,0:T(8,128)(2,1)S(1)}, u32[]{:S(2)}, u32[]{:S(2)}) collective-permute-start(bf16[32,576]{1,0:T(8,128)(2,1)S(1)} %slice.30), channel_id=1, source_target_pairs={{0,17},{1,16},{16,1},{17,0},{2,19},{3,18},{18,3},{19,2},{4,21},{5,... | collective-permute-start | bytes 110600 | tf_op jit(solution)/shard_map/ppermute | solution.py:358
  78.0 4.2 %collective-permute-start.17 = (bf16[32,896]{1,0:T(8,128)(2,1)S(1)}, bf16[32,896]{1,0:T(8,128)(2,1)S(1)}, u32[]{:S(2)}, u32[]{:S(2)}) collective-permute-start(bf16[32,896]{1,0:T(8,128)(2,1)S(1)} %add_convert_fusion.2), channel_id=1, source_target_pairs={{0,16},{1,17},{16,0},{17,1},{2,18},{3,19},{18,2},{19,3},{4,20},{5,... | collective-permute-start | bytes 172040 | tf_op jit(solution)/shard_map/ppermute | solution.py:358
  82.3 1.3 %collective-permute-start.21 = (f32[64,128]{1,0:T(8,128)S(1)}, f32[64,128]{1,0:T(8,128)S(1)}, u32[]{:S(2)}, u32[]{:S(2)}) collective-permute-start(f32[64,128]{1,0:T(8,128)S(1)} %pad_maximum_fusion.2), channel_id=1, source_target_pairs={{0,2},{2,0},{4,6},{6,4},{8,10},{10,8},{12,14},{14,12},{1,3},{3,1},... | collective-permute-start | bytes 98312 | tf_op jit(solution)/shard_map/ppermute | solution.py:309
  82.4 2.8 %collective-permute-start.20 = (f32[64,576]{1,0:T(8,128)S(1)}, f32[64,576]{1,0:T(8,128)S(1)}, u32[]{:S(2)}, u32[]{:S(2)}) collective-permute-start(f32[64,576]{1,0:T(8,128)S(1)} %maximum_select_fusion.2), channel_id=1, source_target_pairs={{0,2},{2,0},{4,6},{6,4},{8,10},{10,8},{12,14},{14,12},{1,3},{3,1},... | collective-permute-start | bytes 442376 | tf_op jit(solution)/shard_map/ppermute | solution.py:309

commit v7 on v3

--- a/solution.py
+++ b/solution.py
@@ -317,7 +317,9 @@
 
 def everyone(values, axis, stride, count):
     sent = values.astype(BF16)
-    terms = [(passed(sent, axis, stride * step, True) if step else sent).astype(F32) for step in range(count)]
+    terms = [sent.astype(F32)]
+    for step in range(1, count):
+        terms.append(passed(sent, axis, stride * step, True).astype(F32))
     while len(terms) > 1:
         apart = len(terms) // 2
         terms = [terms[at] + terms[at + apart] for at in range(apart)]
@@ -432,21 +434,19 @@
     pieces = gradient.shape[0] // rows
     folded_gradient = [gradient[at * rows : (at + 1) * rows] for at in range(pieces)]
     sent = jnp.concatenate([jnp.pad(sums, ((0, 0), (0, lanes - taps_wide))), *folded_gradient], axis=1)
-    summed, hologram = lax.optimization_barrier((everyone(sent, "tok", 2, chips), hologram))
+    summed = everyone(sent, "tok", 2, chips)
     own_terms = sum_frames(summed, False)
     far_terms = sum_frames(summed[:, :taps_wide], True)
     wide = gradient.shape[1]
     own_small = jnp.concatenate(
         [own_terms[:, lanes + at * wide : lanes + (at + 1) * wide] for at in range(pieces)], axis=0
     )
-    other_small = swapped(own_small, "tok")
-    small = in_order(core, own_small, other_small, 1)
+    small = in_order(core, own_small, swapped(own_small, "tok"), 1)
     out_grad = lax.dot_general(
         small, readout_weight.astype(F32), (((0,), (1,)), ((), ())), precision=lax.Precision.HIGHEST
     )
     layer_grad = in_order(half, own_terms[:, :taps_wide], far_terms, 0)
-    other_grad = swapped(layer_grad, "tok")
-    conv_grad = in_order(core, layer_grad[None], other_grad[None], 0)
+    conv_grad = in_order(core, layer_grad[None], swapped(layer_grad, "tok")[None], 0)
     return (hologram[None], conv_grad, out_grad)
 
 

time: 84.1 us -> 84.8 us (level)
  no operation moved by 1% of the time
where the time goes in v7:
time: 84.8 us; the launch traced here: 84.6 us
  waiting for transfers between devices  29.2 us (34%)
  starting transfers between devices  24.5 us (29%)
  Pallas kernels  23.8 us (28%)
  matrix products  2.25 us (3%)
  local copies, waits for them, and re-layouts  1.96 us (2%)
  other arithmetic  1.88 us (2%)
  between operations  1.03 us (1%)
    pallas_call x7, Pallas kernels, absorb(): pl.pallas_call(functools.partial(absorb_kernel, first), out_shape=shapes,...  14.3 us
    ppermute x6, waiting for transfers between devices, round_ring(): lax.ppermute(values, 'tok', [(i, 2 * following[i // 2] + i % 2) for i in...  10.4 us
    ppermute x6, starting transfers between devices, round_ring(): lax.ppermute(values, 'tok', [(i, 2 * following[i // 2] + i % 2) for i in...  9.34 us
    ppermute x9, waiting for transfers between devices, swapped(): return lax.ppermute(values, axis, [(i, i ^ 1) for i in range(size)])  8.35 us
    ppermute x3, starting transfers between devices, passed(): return lax.ppermute(values, axis, pairs)  6.04 us
    ppermute x9, starting transfers between devices, swapped(): return lax.ppermute(values, axis, [(i, i ^ 1) for i in range(size)])  4.11 us
    ppermute x1, waiting for transfers between devices, beside(): return lax.ppermute(values, ('tok', 'col'), pairs)  3.89 us
    ppermute x3, waiting for transfers between devices, sum_frames(): moved = lax.ppermute(sent, ('dp', 'col'), pairs) if step or across else sent  3.66 us
  transfers between devices with their start and end apart: 22, of which 17 were waited for; matrix products, arithmetic and copies ran while one was open for 4% of the time, Pallas kernels for 20%

profile of v7, /device:TPU:0, one launch (start us, length us, event | category | flops | bytes accessed | tf_op | source)
XLA Modules:
  0.0 84.6 jit_solution(15988947091320687985)
XLA Ops:
  1.5 1.2 %copy-done.2 = bf16[1,512,1024]{2,1,0:T(8,128)(2,1)S(1)} copy-done((bf16[1,512,1024]{2,1,0:T(8,128)(2,1)S(1)}, bf16[1,512,1024]{2,1,0:T(8,128)(2,1)}, u32[]{:S(2)}) %copy-start.2) | copy-done | bytes 1048600
  3.5 1.4 %project.2 = (bf16[2,128,512]{2,1,0:T(8,128)(2,1)S(1)}, bf16[2,128,512]{2,1,0:T(8,128)(2,1)S(1)}) custom-call(s32[4]{0:T(128)S(1)} %pad_add_fusion.place, bf16[512,1024]{1,0:T(8,128)(2,1)S(1)} %normalize.1.normed, bf16[3,1024,256]{2,1,0:T(8,128)(2,1)S(1)} %copy-done.1), custom_call_target="tpu_custom_call" | custom-call | tf_op jit(solution)/shard_map/project/pallas_call | solution.py:69
  5.4 2.6 %collective-permute-start.3 = (bf16[2,128,512]{2,1,0:T(8,128)(2,1)S(1)}, bf16[2,128,512]{2,1,0:T(8,128)(2,1)S(1)}, u32[]{:S(2)}, u32[]{:S(2)}) collective-permute-start(bf16[2,128,512]{2,1,0:T(8,128)(2,1)S(1)} %get-tuple-element.73.block), channel_id=1, source_target_pairs={{0,4},{2,6},{4,12},{6,14},{8,0},{10,2},{12,8},{14,10},{1,5},{3,7},... | collective-permute-start | bytes 786440 | tf_op jit(solution)/shard_map/ppermute | solution.py:315
  8.1 2.6 %collective-permute-start.1 = (bf16[2,128,512]{2,1,0:T(8,128)(2,1)S(1)}, bf16[2,128,512]{2,1,0:T(8,128)(2,1)S(1)}, u32[]{:S(2)}, u32[]{:S(2)}) collective-permute-start(bf16[2,128,512]{2,1,0:T(8,128)(2,1)S(1)} %collective-permute-done.block), channel_id=1, source_target_pairs={{0,4},{2,6},{4,12},{6,14},{8,0},{10,2},{12,8},{14,10},{1,5},{3,7},... | collective-permute-start | bytes 786440 | tf_op jit(solution)/shard_map/ppermute | solution.py:315
  11.8 1.3 %collective-permute-done.2.got.queries = bf16[2,64,512]{2,1,0:T(8,128)(2,1)S(1)} collective-permute-done((bf16[2,64,512]{2,1,0:T(8,128)(2,1)S(1)}, bf16[2,64,512]{2,1,0:T(8,128)(2,1)S(1)}, u32[]{:S(2)}, u32[]{:S(2)}) %collective-permute-start.2) | collective-permute-done | bytes 131104 | tf_op jit(solution)/shard_map/ppermute | solution.py:287
  13.1 2.0 %absorb.7 = (f32[2,80,1024]{2,1,0:T(8,128)S(1)}, f32[2,8,1024]{2,1,0:T(8,128)S(1)}) custom-call(bf16[2,64,512]{2,1,0:T(8,128)(2,1)S(1)} %get-tuple-element.70.own.queries, bf16[2,64,512]{2,1,0:T(8,128)(2,1)S(1)} %collective-permute-done.2.got.queries, bf16[2,128,512]{2,1,0:T(8,128)(2,1)S(1)} %get-tuple-element.73.block), custom_call_target="tpu_custom_call" | custom-call | tf_op jit(solution)/shard_map/absorb/pallas_call | solution.py:115
  17.3 2.1 %absorb.8 = (f32[2,80,1024]{2,1,0:T(8,128)S(1)}, f32[2,8,1024]{2,1,0:T(8,128)S(1)}) custom-call(bf16[2,64,512]{2,1,0:T(8,128)(2,1)S(1)} %get-tuple-element.70.own.queries, bf16[2,64,512]{2,1,0:T(8,128)(2,1)S(1)} %collective-permute-done.2.got.queries, ...), custom_call_target="tpu_custom_call", output_to_operand_aliasing={{0}: (3, {}), {1}: (4, {})} | custom-call | tf_op jit(solution)/shard_map/absorb/pallas_call | solution.py:115
  19.4 2.4 %collective-permute-done.1.block = bf16[2,128,512]{2,1,0:T(8,128)(2,1)S(1)} collective-permute-done((bf16[2,128,512]{2,1,0:T(8,128)(2,1)S(1)}, bf16[2,128,512]{2,1,0:T(8,128)(2,1)S(1)}, u32[]{:S(2)}, u32[]{:S(2)}) %collective-permute-start.1) | collective-permute-done | bytes 262176 | tf_op jit(solution)/shard_map/ppermute | solution.py:315
  23.0 2.0 %absorb.9 = (f32[2,80,1024]{2,1,0:T(8,128)S(1)}, f32[2,8,1024]{2,1,0:T(8,128)S(1)}) custom-call(bf16[2,64,512]{2,1,0:T(8,128)(2,1)S(1)} %get-tuple-element.70.own.queries, bf16[2,64,512]{2,1,0:T(8,128)(2,1)S(1)} %collective-permute-done.2.got.queries, ...), custom_call_target="tpu_custom_call", output_to_operand_aliasing={{0}: (3, {}), {1}: (4, {})} | custom-call | tf_op jit(solution)/shard_map/absorb/pallas_call | solution.py:115
  25.0 2.4 %collective-permute-done.5.block = bf16[2,128,512]{2,1,0:T(8,128)(2,1)S(1)} collective-permute-done((bf16[2,128,512]{2,1,0:T(8,128)(2,1)S(1)}, bf16[2,128,512]{2,1,0:T(8,128)(2,1)S(1)}, u32[]{:S(2)}, u32[]{:S(2)}) %collective-permute-start.5) | collective-permute-done | bytes 262176 | tf_op jit(solution)/shard_map/ppermute | solution.py:315
  28.6 2.1 %absorb.10 = (f32[2,80,1024]{2,1,0:T(8,128)S(1)}, f32[2,8,1024]{2,1,0:T(8,128)S(1)}) custom-call(bf16[2,64,512]{2,1,0:T(8,128)(2,1)S(1)} %get-tuple-element.70.own.queries, bf16[2,64,512]{2,1,0:T(8,128)(2,1)S(1)} %collective-permute-done.2.got.queries, ...), custom_call_target="tpu_custom_call", output_to_operand_aliasing={{0}: (3, {}), {1}: (4, {})} | custom-call | tf_op jit(solution)/shard_map/absorb/pallas_call | solution.py:115
  30.6 2.4 %collective-permute-done.4.block = bf16[2,128,512]{2,1,0:T(8,128)(2,1)S(1)} collective-permute-done((bf16[2,128,512]{2,1,0:T(8,128)(2,1)S(1)}, bf16[2,128,512]{2,1,0:T(8,128)(2,1)S(1)}, u32[]{:S(2)}, u32[]{:S(2)}) %collective-permute-start.4) | collective-permute-done | bytes 262176 | tf_op jit(solution)/shard_map/ppermute | solution.py:315
  33.1 2.1 %absorb.11 = (f32[2,80,1024]{2,1,0:T(8,128)S(1)}, f32[2,8,1024]{2,1,0:T(8,128)S(1)}) custom-call(bf16[2,64,512]{2,1,0:T(8,128)(2,1)S(1)} %get-tuple-element.70.own.queries, bf16[2,64,512]{2,1,0:T(8,128)(2,1)S(1)} %collective-permute-done.2.got.queries, ...), custom_call_target="tpu_custom_call", output_to_operand_aliasing={{0}: (3, {}), {1}: (4, {})} | custom-call | tf_op jit(solution)/shard_map/absorb/pallas_call | solution.py:115
  35.1 1.9 %collective-permute-start.8 = (f32[2,2,128]{2,1,0:T(2,128)S(1)}, f32[2,2,128]{2,1,0:T(2,128)S(1)}, u32[]{:S(2)}, u32[]{:S(2)}) collective-permute-start(f32[2,2,128]{2,1,0:T(2,128)S(1)} %bitcast.27), channel_id=1, source_target_pairs={{0,1},{1,0},{2,3},{3,2},{4,5},{5,4},{6,7},{7,6},{8,9},{9,8},{10,11... | collective-permute-start | bytes 6152 | tf_op jit(solution)/shard_map/ppermute | solution.py:287
  38.7 2.0 %absorb.12 = (f32[2,80,1024]{2,1,0:T(8,128)S(1)}, f32[2,8,1024]{2,1,0:T(8,128)S(1)}) custom-call(bf16[2,64,512]{2,1,0:T(8,128)(2,1)S(1)} %get-tuple-element.70.own.queries, bf16[2,64,512]{2,1,0:T(8,128)(2,1)S(1)} %collective-permute-done.2.got.queries, ...), custom_call_target="tpu_custom_call", output_to_operand_aliasing={{0}: (3, {}), {1}: (4, {})} | custom-call | tf_op jit(solution)/shard_map/absorb/pallas_call | solution.py:115
  40.9 2.0 %absorb.13 = (f32[2,80,1024]{2,1,0:T(8,128)S(1)}, f32[2,8,1024]{2,1,0:T(8,128)S(1)}) custom-call(bf16[2,64,512]{2,1,0:T(8,128)(2,1)S(1)} %get-tuple-element.70.own.queries, bf16[2,64,512]{2,1,0:T(8,128)(2,1)S(1)} %collective-permute-done.2.got.queries, ...), custom_call_target="tpu_custom_call", output_to_operand_aliasing={{0}: (3, {}), {1}: (4, {})} | custom-call | tf_op jit(solution)/shard_map/absorb/pallas_call | solution.py:115
  43.0 2.0 %collective-permute-done.6.block = bf16[2,128,512]{2,1,0:T(8,128)(2,1)S(1)} collective-permute-done((bf16[2,128,512]{2,1,0:T(8,128)(2,1)S(1)}, bf16[2,128,512]{2,1,0:T(8,128)(2,1)S(1)}, u32[]{:S(2)}, u32[]{:S(2)}) %collective-permute-start.6) | collective-permute-done | bytes 262176 | tf_op jit(solution)/shard_map/ppermute | solution.py:315
  44.9 1.3 %closing.3 = (bf16[128,512]{1,0:T(8,128)(2,1)S(1)}, f32[64,512]{1,0:T(8,128)S(1)}) custom-call(bf16[2,64,512]{2,1,0:T(8,128)(2,1)S(1)} %collective-permute-done.2.got.queries, bf16[2,128,512]{2,1,0:T(8,128)(2,1)S(1)} %collective-permute-done.6.block, f32[2,80,1024]{2,1,0:T(8,128)S(1)} %get-tuple-element.113.carried, ...), custom_call_target="tpu_custom_call" | custom-call | tf_op jit(solution)/shard_map/closing/pallas_call | solution.py:138
  46.3 1.3 %closing.2 = (bf16[128,512]{1,0:T(8,128)(2,1)S(1)}, f32[64,512]{1,0:T(8,128)S(1)}) custom-call(bf16[2,64,512]{2,1,0:T(8,128)(2,1)S(1)} %get-tuple-element.70.own.queries, bf16[2,128,512]{2,1,0:T(8,128)(2,1)S(1)} %collective-permute-done.6.block, f32[2,80,1024]{2,1,0:T(8,128)S(1)} %get-tuple-element.113.carried, ...), custom_call_target="tpu_custom_call" | custom-call | tf_op jit(solution)/shard_map/closing/pallas_call | solution.py:138
  48.5 3.7 %collective-permute-done.10 = bf16[64,512]{1,0:T(8,128)(2,1)S(1)} collective-permute-done((bf16[64,512]{1,0:T(8,128)(2,1)S(1)}, bf16[64,512]{1,0:T(8,128)(2,1)S(1)}, u32[]{:S(2)}, u32[]{:S(2)}) %collective-permute-start.10) | collective-permute-done | bytes 65568 | tf_op jit(solution)/shard_map/ppermute | solution.py:287
  52.3 1.3 %collective-permute-done.11 = bf16[80,512]{1,0:T(8,128)(2,1)S(1)} collective-permute-done((bf16[80,512]{1,0:T(8,128)(2,1)S(1)}, bf16[80,512]{1,0:T(8,128)(2,1)S(1)}, u32[]{:S(2)}, u32[]{:S(2)}) %collective-permute-start.11) | collective-permute-done | bytes 81952 | tf_op jit(solution)/shard_map/ppermute | solution.py:287
  53.6 1.5 %collective-permute-start.12 = (bf16[80,1024]{1,0:T(8,128)(2,1)S(1)}, bf16[80,1024]{1,0:T(8,128)(2,1)S(1)}, u32[]{:S(2)}, u32[]{:S(2)}) collective-permute-start(bf16[80,1024]{1,0:T(8,128)(2,1)S(1)} %pad_maximum_fusion.chip_map), channel_id=1, source_target_pairs={{0,4},{1,5},{2,3},{3,2},{4,0},{5,1},{6,10},{7,11},{8,12},{9,13},{1... | collective-permute-start | bytes 491528 | tf_op jit(solution)/shard_map/ppermute | solution.py:305
  55.1 3.9 %collective-permute-done.12.near = bf16[80,1024]{1,0:T(8,128)(2,1)S(1)} collective-permute-done((bf16[80,1024]{1,0:T(8,128)(2,1)S(1)}, bf16[80,1024]{1,0:T(8,128)(2,1)S(1)}, u32[]{:S(2)}, u32[]{:S(2)}) %collective-permute-start.12) | collective-permute-done | bytes 163872 | tf_op jit(solution)/shard_map/ppermute | solution.py:305
  59.0 1.4 %collective-permute-done.13.far = bf16[80,1024]{1,0:T(8,128)(2,1)S(1)} collective-permute-done((bf16[80,1024]{1,0:T(8,128)(2,1)S(1)}, bf16[80,1024]{1,0:T(8,128)(2,1)S(1)}, u32[]{:S(2)}, u32[]{:S(2)}) %collective-permute-start.13) | collective-permute-done | bytes 163872 | tf_op jit(solution)/shard_map/ppermute | solution.py:287
  60.4 3.5 %network.1 = (f32[2,1024]{1,0:T(2,128)S(1)}, f32[32,576]{1,0:T(8,128)S(1)}, f32[64,128]{1,0:T(8,128)S(1)}) custom-call(s32[4]{0:T(128)S(1)} %pad_add_fusion.place, bf16[80,1024]{1,0:T(8,128)(2,1)S(1)} %pad_maximum_fusion.chip_map, bf16[80,1024]{1,0:T(8,128)(2,1)S(1)} %collective-permute-done.12.near, bf16[80,1024]{1,0:T(8,128)(2,1)S(1)} %collective-permute-done.13.far, ...), custom_call_target="tpu_custom_call" | custom-call | tf_op jit(solution)/shard_map/network/pallas_call | solution.py:270
  64.0 2.2 %collective-permute-start.14 = (bf16[32,896]{1,0:T(8,128)(2,1)S(1)}, bf16[32,896]{1,0:T(8,128)(2,1)S(1)}, u32[]{:S(2)}, u32[]{:S(2)}) collective-permute-start(bf16[32,896]{1,0:T(8,128)(2,1)S(1)} %fusion.14), channel_id=1, source_target_pairs={{0,8},{2,10},{4,12},{6,14},{8,0},{10,2},{12,4},{14,6},{1,9},{3,11}... | collective-permute-start | bytes 172040 | tf_op jit(solution)/shard_map/ppermute | solution.py:293
  66.2 2.0 %collective-permute-start.15 = (bf16[32,896]{1,0:T(8,128)(2,1)S(1)}, bf16[32,896]{1,0:T(8,128)(2,1)S(1)}, u32[]{:S(2)}, u32[]{:S(2)}) collective-permute-start(bf16[32,896]{1,0:T(8,128)(2,1)S(1)} %fusion.14), channel_id=1, source_target_pairs={{0,4},{2,6},{4,8},{6,10},{8,12},{10,14},{12,0},{14,2},{1,5},{3,7},... | collective-permute-start | bytes 172040 | tf_op jit(solution)/shard_map/ppermute | solution.py:293
  68.2 1.8 %collective-permute-start.16 = (bf16[32,896]{1,0:T(8,128)(2,1)S(1)}, bf16[32,896]{1,0:T(8,128)(2,1)S(1)}, u32[]{:S(2)}, u32[]{:S(2)}) collective-permute-start(bf16[32,896]{1,0:T(8,128)(2,1)S(1)} %fusion.14), channel_id=1, source_target_pairs={{0,12},{2,14},{4,0},{6,2},{8,4},{10,6},{12,8},{14,10},{1,13},{3,15... | collective-permute-start | bytes 172040 | tf_op jit(solution)/shard_map/ppermute | solution.py:293
  73.8 2.2 %collective-permute-start.19 = (bf16[32,576]{1,0:T(8,128)(2,1)S(1)}, bf16[32,576]{1,0:T(8,128)(2,1)S(1)}, u32[]{:S(2)}, u32[]{:S(2)}) collective-permute-start(bf16[32,576]{1,0:T(8,128)(2,1)S(1)} %slice.30), channel_id=1, source_target_pairs={{0,17},{1,16},{16,1},{17,0},{2,19},{3,18},{18,3},{19,2},{4,21},{5,... | collective-permute-start | bytes 110600 | tf_op jit(solution)/shard_map/ppermute | solution.py:338
  77.5 1.3 %collective-permute-done.19 = bf16[32,576]{1,0:T(8,128)(2,1)S(1)} collective-permute-done((bf16[32,576]{1,0:T(8,128)(2,1)S(1)}, bf16[32,576]{1,0:T(8,128)(2,1)S(1)}, u32[]{:S(2)}, u32[]{:S(2)}) %collective-permute-start.19) | collective-permute-done | bytes 36896 | tf_op jit(solution)/shard_map/ppermute | solution.py:338
  78.8 2.1 %collective-permute-done.17 = bf16[32,896]{1,0:T(8,128)(2,1)S(1)} collective-permute-done((bf16[32,896]{1,0:T(8,128)(2,1)S(1)}, bf16[32,896]{1,0:T(8,128)(2,1)S(1)}, u32[]{:S(2)}, u32[]{:S(2)}) %collective-permute-start.17) | collective-permute-done | bytes 57376 | tf_op jit(solution)/shard_map/ppermute | solution.py:338
  82.2 1.6 %fusion.3 = f32[256,1024]{1,0:T(8,128)} fusion(bf16[1024,64]{0,1:T(8,128)(2,1)S(1)} %copy-done.6, f32[64,128]{1,0:T(8,128)S(1)} %collective-permute-done.21, f32[32,128]{1,0:T(8,128)S(1)} %get-tuple-element.128, f32[32,128]{1,0:T(8,128)S(1)} %get-tuple-element.127, pred[]{:T(512)S(6)} %eq.10), kind=kOutput, calls=%fused_computation.15 | convolution fusion | flops 201408512 | bytes 1245185 | tf_op jit(solution)/shard_map/dot_general | solution.py:445
  (72 shorter events, 17.8 us)
Async XLA Ops:
  0.6 37.6 %copy-start = (bf16[256,1024]{1,0:T(8,128)(2,1)S(1)}, bf16[256,1024]{1,0:T(8,128)(2,1)}, u32[]{:S(2)}) copy-start(bf16[256,1024]{1,0:T(8,128)(2,1)} %param.11) | copy-start | bytes 1572868
  0.6 2.8 %copy-start.1 = (bf16[3,1024,256]{2,1,0:T(8,128)(2,1)S(1)}, bf16[3,1024,256]{2,1,0:T(8,128)(2,1)}, u32[]{:S(2)}) copy-start(bf16[3,1024,256]{2,1,0:T(8,128)(2,1)} %weight.1) | copy-start | bytes 4718596
  1.5 1.2 %copy-start.2 = (bf16[1,512,1024]{2,1,0:T(8,128)(2,1)S(1)}, bf16[1,512,1024]{2,1,0:T(8,128)(2,1)}, u32[]{:S(2)}) copy-start(bf16[1,512,1024]{2,1,0:T(8,128)(2,1)} %param.8) | copy-start | bytes 3145732
  4.9 3.2 %collective-permute-start = (bf16[2,128,512]{2,1,0:T(8,128)(2,1)S(1)}, bf16[2,128,512]{2,1,0:T(8,128)(2,1)S(1)}, u32[]{:S(2)}, u32[]{:S(2)}) collective-permute-start(bf16[2,128,512]{2,1,0:T(8,128)(2,1)S(1)} %get-tuple-element.71), channel_id=1, source_target_pairs={{0,2},{2,0},{4,6},{6,4},{8,10},{10,8},{12,14},{14,12},{1,3},{3,1},... | collective-permute-start | bytes 786440 | tf_op jit(solution)/shard_map/ppermute | solution.py:287
  5.4 10.8 %collective-permute-start.3 = (bf16[2,128,512]{2,1,0:T(8,128)(2,1)S(1)}, bf16[2,128,512]{2,1,0:T(8,128)(2,1)S(1)}, u32[]{:S(2)}, u32[]{:S(2)}) collective-permute-start(bf16[2,128,512]{2,1,0:T(8,128)(2,1)S(1)} %get-tuple-element.73.block), channel_id=1, source_target_pairs={{0,4},{2,6},{4,12},{6,14},{8,0},{10,2},{12,8},{14,10},{1,5},{3,7},... | collective-permute-start | bytes 786440 | tf_op jit(solution)/shard_map/ppermute | solution.py:315
  8.1 13.8 %collective-permute-start.1 = (bf16[2,128,512]{2,1,0:T(8,128)(2,1)S(1)}, bf16[2,128,512]{2,1,0:T(8,128)(2,1)S(1)}, u32[]{:S(2)}, u32[]{:S(2)}) collective-permute-start(bf16[2,128,512]{2,1,0:T(8,128)(2,1)S(1)} %collective-permute-done.block), channel_id=1, source_target_pairs={{0,4},{2,6},{4,12},{6,14},{8,0},{10,2},{12,8},{14,10},{1,5},{3,7},... | collective-permute-start | bytes 786440 | tf_op jit(solution)/shard_map/ppermute | solution.py:315
  11.7 1.4 %collective-permute-start.2 = (bf16[2,64,512]{2,1,0:T(8,128)(2,1)S(1)}, bf16[2,64,512]{2,1,0:T(8,128)(2,1)S(1)}, u32[]{:S(2)}, u32[]{:S(2)}) collective-permute-start(bf16[2,64,512]{2,1,0:T(8,128)(2,1)S(1)} %get-tuple-element.72), channel_id=1, source_target_pairs={{0,2},{2,0},{4,6},{6,4},{8,10},{10,8},{12,14},{14,12},{1,3},{3,1},... | collective-permute-start | bytes 393224 | tf_op jit(solution)/shard_map/ppermute | solution.py:287
  16.2 11.2 %collective-permute-start.5 = (bf16[2,128,512]{2,1,0:T(8,128)(2,1)S(1)}, bf16[2,128,512]{2,1,0:T(8,128)(2,1)S(1)}, u32[]{:S(2)}, u32[]{:S(2)}) collective-permute-start(bf16[2,128,512]{2,1,0:T(8,128)(2,1)S(1)} %collective-permute-done.3.block), channel_id=1, source_target_pairs={{0,4},{2,6},{4,12},{6,14},{8,0},{10,2},{12,8},{14,10},{1,5},{3,7},... | collective-permute-start | bytes 786440 | tf_op jit(solution)/shard_map/ppermute | solution.py:315
  21.8 11.2 %collective-permute-start.4 = (bf16[2,128,512]{2,1,0:T(8,128)(2,1)S(1)}, bf16[2,128,512]{2,1,0:T(8,128)(2,1)S(1)}, u32[]{:S(2)}, u32[]{:S(2)}) collective-permute-start(bf16[2,128,512]{2,1,0:T(8,128)(2,1)S(1)} %collective-permute-done.1.block), channel_id=1, source_target_pairs={{0,4},{2,6},{4,12},{6,14},{8,0},{10,2},{12,8},{14,10},{1,5},{3,7},... | collective-permute-start | bytes 786440 | tf_op jit(solution)/shard_map/ppermute | solution.py:315
  23.0 12.2 %copy-start.7 = (f32[1,2,2,128]{3,2,1,0:T(2,128)S(1)}, f32[1,2,2,128]{3,2,1,0:T(2,128)}, u32[]{:S(2)}) copy-start(f32[1,2,2,128]{3,2,1,0:T(2,128)} %param.15) | copy-start | bytes 6148
  23.0 14.9 %copy-start.3 = (bf16[1,512,1024]{2,1,0:T(8,128)(2,1)S(1)}, bf16[1,512,1024]{2,1,0:T(8,128)(2,1)}, u32[]{:S(2)}) copy-start(bf16[1,512,1024]{2,1,0:T(8,128)(2,1)} %param.8) | copy-start | bytes 3145732
  23.0 14.9 %copy-start.6 = (bf16[1024,64]{0,1:T(8,128)(2,1)S(1)}, bf16[1024,64]{0,1:T(8,128)(2,1)}, u32[]{:S(2)}) copy-start(bf16[1024,64]{0,1:T(8,128)(2,1)} %param.12) | copy-start | bytes 393220
  27.5 13.4 %collective-permute-start.7 = (bf16[2,128,512]{2,1,0:T(8,128)(2,1)S(1)}, bf16[2,128,512]{2,1,0:T(8,128)(2,1)S(1)}, u32[]{:S(2)}, u32[]{:S(2)}) collective-permute-start(bf16[2,128,512]{2,1,0:T(8,128)(2,1)S(1)} %collective-permute-done.5.block), channel_id=1, source_target_pairs={{0,4},{2,6},{4,12},{6,14},{8,0},{10,2},{12,8},{14,10},{1,5},{3,7},... | collective-permute-start | bytes 786440 | tf_op jit(solution)/shard_map/ppermute | solution.py:315
  30.6 7.9 %copy-start.4 = (bf16[2,64,576]{2,1,0:T(8,128)(2,1)S(1)}, bf16[2,64,576]{2,1,0:T(8,128)(2,1)}, u32[]{:S(2)}) copy-start(bf16[2,64,576]{2,1,0:T(8,128)(2,1)} %weight.2) | copy-start | bytes 442372
  35.1 5.7 %collective-permute-start.8 = (f32[2,2,128]{2,1,0:T(2,128)S(1)}, f32[2,2,128]{2,1,0:T(2,128)S(1)}, u32[]{:S(2)}, u32[]{:S(2)}) collective-permute-start(f32[2,2,128]{2,1,0:T(2,128)S(1)} %bitcast.27), channel_id=1, source_target_pairs={{0,1},{1,0},{2,3},{3,2},{4,5},{5,4},{6,7},{7,6},{8,9},{9,8},{10,11... | collective-permute-start | bytes 6152 | tf_op jit(solution)/shard_map/ppermute | solution.py:287
  37.0 7.9 %collective-permute-start.6 = (bf16[2,128,512]{2,1,0:T(8,128)(2,1)S(1)}, bf16[2,128,512]{2,1,0:T(8,128)(2,1)S(1)}, u32[]{:S(2)}, u32[]{:S(2)}) collective-permute-start(bf16[2,128,512]{2,1,0:T(8,128)(2,1)S(1)} %collective-permute-done.4.block), channel_id=1, source_target_pairs={{0,4},{2,6},{4,12},{6,14},{8,0},{10,2},{12,8},{14,10},{1,5},{3,7},... | collective-permute-start | bytes 786440 | tf_op jit(solution)/shard_map/ppermute | solution.py:315
  43.0 17.4 %copy-start.5 = (bf16[2,64]{1,0:T(2,128)(2,1)S(1)}, bf16[2,64]{1,0:T(2,128)(2,1)}, u32[]{:S(2)}) copy-start(bf16[2,64]{1,0:T(2,128)(2,1)} %head.1) | copy-start | bytes 772
  46.2 1.4 %collective-permute-start.9 = (f32[64,512]{1,0:T(8,128)S(1)}, f32[64,512]{1,0:T(8,128)S(1)}, u32[]{:S(2)}, u32[]{:S(2)}) collective-permute-start(f32[64,512]{1,0:T(8,128)S(1)} %get-tuple-element.117), channel_id=1, source_target_pairs={{0,2},{2,0},{4,6},{6,4},{8,10},{10,8},{12,14},{14,12},{1,3},{3,1},... | collective-permute-start | bytes 393224 | tf_op jit(solution)/shard_map/ppermute | solution.py:287
  47.7 4.5 %collective-permute-start.10 = (bf16[64,512]{1,0:T(8,128)(2,1)S(1)}, bf16[64,512]{1,0:T(8,128)(2,1)S(1)}, u32[]{:S(2)}, u32[]{:S(2)}) collective-permute-start(bf16[64,512]{1,0:T(8,128)(2,1)S(1)} %add_convert_fusion.1), channel_id=1, source_target_pairs={{0,1},{1,0},{2,3},{3,2},{4,5},{5,4},{6,7},{7,6},{8,9},{9,8},{10,11... | collective-permute-start | bytes 196616 | tf_op jit(solution)/shard_map/ppermute | solution.py:287
  52.2 1.3 %collective-permute-start.11 = (bf16[80,512]{1,0:T(8,128)(2,1)S(1)}, bf16[80,512]{1,0:T(8,128)(2,1)S(1)}, u32[]{:S(2)}, u32[]{:S(2)}) collective-permute-start(bf16[80,512]{1,0:T(8,128)(2,1)S(1)} %pad_maximum_fusion.1), channel_id=1, source_target_pairs={{0,2},{2,0},{4,6},{6,4},{8,10},{10,8},{12,14},{14,12},{1,3},{3,1},... | collective-permute-start | bytes 245768 | tf_op jit(solution)/shard_map/ppermute | solution.py:287
  53.6 5.4 %collective-permute-start.12 = (bf16[80,1024]{1,0:T(8,128)(2,1)S(1)}, bf16[80,1024]{1,0:T(8,128)(2,1)S(1)}, u32[]{:S(2)}, u32[]{:S(2)}) collective-permute-start(bf16[80,1024]{1,0:T(8,128)(2,1)S(1)} %pad_maximum_fusion.chip_map), channel_id=1, source_target_pairs={{0,4},{1,5},{2,3},{3,2},{4,0},{5,1},{6,10},{7,11},{8,12},{9,13},{1... | collective-permute-start | bytes 491528 | tf_op jit(solution)/shard_map/ppermute | solution.py:305
  59.0 1.4 %collective-permute-start.13 = (bf16[80,1024]{1,0:T(8,128)(2,1)S(1)}, bf16[80,1024]{1,0:T(8,128)(2,1)S(1)}, u32[]{:S(2)}, u32[]{:S(2)}) collective-permute-start(bf16[80,1024]{1,0:T(8,128)(2,1)S(1)} %collective-permute-done.12.near), channel_id=1, source_target_pairs={{0,2},{2,0},{4,6},{6,4},{8,10},{10,8},{12,14},{14,12},{1,3},{3,1},... | collective-permute-start | bytes 491528 | tf_op jit(solution)/shard_map/ppermute | solution.py:287
  64.0 7.3 %collective-permute-start.14 = (bf16[32,896]{1,0:T(8,128)(2,1)S(1)}, bf16[32,896]{1,0:T(8,128)(2,1)S(1)}, u32[]{:S(2)}, u32[]{:S(2)}) collective-permute-start(bf16[32,896]{1,0:T(8,128)(2,1)S(1)} %fusion.14), channel_id=1, source_target_pairs={{0,8},{2,10},{4,12},{6,14},{8,0},{10,2},{12,4},{14,6},{1,9},{3,11}... | collective-permute-start | bytes 172040 | tf_op jit(solution)/shard_map/ppermute | solution.py:293
  66.2 6.1 %collective-permute-start.15 = (bf16[32,896]{1,0:T(8,128)(2,1)S(1)}, bf16[32,896]{1,0:T(8,128)(2,1)S(1)}, u32[]{:S(2)}, u32[]{:S(2)}) collective-permute-start(bf16[32,896]{1,0:T(8,128)(2,1)S(1)} %fusion.14), channel_id=1, source_target_pairs={{0,4},{2,6},{4,8},{6,10},{8,12},{10,14},{12,0},{14,2},{1,5},{3,7},... | collective-permute-start | bytes 172040 | tf_op jit(solution)/shard_map/ppermute | solution.py:293
  68.2 4.7 %collective-permute-start.16 = (bf16[32,896]{1,0:T(8,128)(2,1)S(1)}, bf16[32,896]{1,0:T(8,128)(2,1)S(1)}, u32[]{:S(2)}, u32[]{:S(2)}) collective-permute-start(bf16[32,896]{1,0:T(8,128)(2,1)S(1)} %fusion.14), channel_id=1, source_target_pairs={{0,12},{2,14},{4,0},{6,2},{8,4},{10,6},{12,8},{14,10},{1,13},{3,15... | collective-permute-start | bytes 172040 | tf_op jit(solution)/shard_map/ppermute | solution.py:293
  73.0 4.5 %collective-permute-start.18 = (bf16[32,576]{1,0:T(8,128)(2,1)S(1)}, bf16[32,576]{1,0:T(8,128)(2,1)S(1)}, u32[]{:S(2)}, u32[]{:S(2)}) collective-permute-start(bf16[32,576]{1,0:T(8,128)(2,1)S(1)} %slice.30), channel_id=1, source_target_pairs={{0,1},{1,0},{16,17},{17,16},{2,3},{3,2},{18,19},{19,18},{4,5},{5,4... | collective-permute-start | bytes 110600 | tf_op jit(solution)/shard_map/ppermute | solution.py:338
  73.8 4.9 %collective-permute-start.19 = (bf16[32,576]{1,0:T(8,128)(2,1)S(1)}, bf16[32,576]{1,0:T(8,128)(2,1)S(1)}, u32[]{:S(2)}, u32[]{:S(2)}) collective-permute-start(bf16[32,576]{1,0:T(8,128)(2,1)S(1)} %slice.30), channel_id=1, source_target_pairs={{0,17},{1,16},{16,1},{17,0},{2,19},{3,18},{18,3},{19,2},{4,21},{5,... | collective-permute-start | bytes 110600 | tf_op jit(solution)/shard_map/ppermute | solution.py:338
  76.7 4.2 %collective-permute-start.17 = (bf16[32,896]{1,0:T(8,128)(2,1)S(1)}, bf16[32,896]{1,0:T(8,128)(2,1)S(1)}, u32[]{:S(2)}, u32[]{:S(2)}) collective-permute-start(bf16[32,896]{1,0:T(8,128)(2,1)S(1)} %add_convert_fusion.2), channel_id=1, source_target_pairs={{0,16},{1,17},{16,0},{17,1},{2,18},{3,19},{18,2},{19,3},{4,20},{5,... | collective-permute-start | bytes 172040 | tf_op jit(solution)/shard_map/ppermute | solution.py:338
  81.0 1.3 %collective-permute-start.21 = (f32[64,128]{1,0:T(8,128)S(1)}, f32[64,128]{1,0:T(8,128)S(1)}, u32[]{:S(2)}, u32[]{:S(2)}) collective-permute-start(f32[64,128]{1,0:T(8,128)S(1)} %pad_maximum_fusion.2), channel_id=1, source_target_pairs={{0,2},{2,0},{4,6},{6,4},{8,10},{10,8},{12,14},{14,12},{1,3},{3,1},... | collective-permute-start | bytes 98312 | tf_op jit(solution)/shard_map/ppermute | solution.py:287
  81.1 2.8 %collective-permute-start.20 = (f32[64,576]{1,0:T(8,128)S(1)}, f32[64,576]{1,0:T(8,128)S(1)}, u32[]{:S(2)}, u32[]{:S(2)}) collective-permute-start(f32[64,576]{1,0:T(8,128)S(1)} %maximum_select_fusion.2), channel_id=1, source_target_pairs={{0,2},{2,0},{4,6},{6,4},{8,10},{10,8},{12,14},{14,12},{1,3},{3,1},... | collective-permute-start | bytes 442376 | tf_op jit(solution)/shard_map/ppermute | solution.py:287
